TPU v7x, 32 devices: a whole 2x2x4 slice. The times are simulated.
32 devices in a mesh: grp: 2 (over y), dom: 8 (over z, x), segment: 2 (over core).
Axes of the slice: x: 2, y: 2, z: 4, core: 2. Of those that a mesh axis runs over, the one named last changes fastest.
Arguments:
- section_inputs: bfloat16 [2, 2, 4096, 512], P('segment', None, ('grp', 'dom')), parts along dimension 2, may hold values from -6 to 6
- out_cot: bfloat16 [2, 4096, 512], P(None, ('grp', 'dom')), parts along dimension 1, may hold values from -2 to 2
- w_node: bfloat16 [2, 512, 512], P('segment'), may hold values from -0.25 to 0.25
- w_agg: bfloat16 [2, 512, 512], P('segment'), may hold values from -0.25 to 0.25
- w_out: bfloat16 [2, 512, 512], P('segment'), may hold values from -0.25 to 0.25
- bias: bfloat16 [2, 512], P('segment'), may hold values from -3 to 3
- gain: bfloat16 [2, 512], P('segment'), may hold values from 0.25 to 1.75
- send_rows: int32 [8, 4, 32], P('dom'), may hold values from 0 to 255
- blk_pairs: int32 [8, 2, 7], P('dom'), may hold values from 0 to 2, as said below
- blk_count: int32 [8], P('dom'), may hold values from 3 to 7, as said below
- blk_values: bfloat16 [8, 7, 128, 128], P('dom'), may hold values from -0.375 to 0.375
Outputs:
- cotangents: bfloat16 [2, 2, 4096, 512], P('segment', None, ('grp', 'dom')), parts along dimension 2
- grad_node: float32 [2, 1024, 512], P('segment', ('grp', 'dom')), parts along dimension 1
- grad_agg: float32 [2, 1024, 512], P('segment', ('grp', 'dom')), parts along dimension 1
- grad_out: float32 [2, 1024, 512], P('segment', ('grp', 'dom')), parts along dimension 1
- grad_bias: float32 [2, 1024], P('segment', 'grp'), parts along dimension 1
- grad_gain: float32 [2, 1024], P('segment', 'grp'), parts along dimension 1
There are 2 independent parts, one for each index of `grp`. A program takes and returns all parts, laid end to end along the dimension named above; an argument that names none is the same for every part. Nothing has to cross between parts.
Inputs may be any that keep to these rules, and one draw needn't show every extreme that they name: `blk_pairs`: slots 0 to 1 pair destination block k with source block k; slot 2 reads source block 2, the first block of halo rows; destination blocks lie below 2. `blk_count`: some partition has all 7 slots live.
All inputs are finite; a program needn't handle non-finite values.
Results may differ from a plain program's by a relative error of at most 0.0075.
Values may be sent and summed in bfloat16 or wider, within the bound.
No kernel may reach another device: no remote copies, remote signals or barrier semaphores. Data moves between devices by JAX's collectives and lax.ppermute only.
A program may use at most 64 MiB of HBM per device.

v0:
```python
import jax
import jax.numpy as jnp
from jax import lax
from jax.sharding import PartitionSpec as P

EPSILON = 1e-05
PRECISE = lax.Precision.HIGHEST
OFFSETS = (1, -1, 2, -2)


def shifted(x, axis, by):
    devices = lax.axis_size(axis)
    return lax.ppermute(x, axis, [(i, (i + by) % devices) for i in range(devices)])


def shifted_2(x, axis, by):
    devices = lax.axis_size(axis)
    pairs = [(i, i + by) for i in range(devices) if 0 <= i + by < devices]
    return lax.ppermute(x, axis, pairs)


def aggregate(source, values, pairs, live_count, out_blocks):
    feat_width = source.shape[1]
    blocks = source.reshape(-1, 128, feat_width)
    picked = blocks[pairs[1]]
    products = jnp.einsum("kij,kjd->kid", values, picked, preferred_element_type=jnp.float32)
    is_live = jnp.arange(pairs.shape[1], dtype=jnp.int32) < live_count
    onehot = (
        (pairs[0][None, :] == jnp.arange(out_blocks, dtype=jnp.int32)[:, None]) & is_live[None, :]
    ).astype(jnp.float32)
    summed = jnp.einsum("bk,kid->bid", onehot, products, precision=PRECISE)
    return summed.reshape(out_blocks * 128, feat_width)


def spread(grad_rows, values, pairs, live_count, out_blocks):
    feat_width = grad_rows.shape[1]
    blocks = grad_rows.reshape(-1, 128, feat_width)
    picked = blocks[pairs[0]]
    products = jnp.einsum("kij,kid->kjd", values, picked, preferred_element_type=jnp.float32)
    is_live = jnp.arange(pairs.shape[1], dtype=jnp.int32) < live_count
    onehot = (
        (pairs[1][None, :] == jnp.arange(out_blocks, dtype=jnp.int32)[:, None]) & is_live[None, :]
    ).astype(jnp.float32)
    summed = jnp.einsum("sk,kjd->sjd", onehot, products, precision=PRECISE)
    return summed.reshape(out_blocks * 128, feat_width)


def fetch_halo(x_rows, targets):
    pieces = []
    for slot_num, offset in enumerate(OFFSETS):
        outgoing = x_rows[targets[slot_num]]
        pieces.append(shifted(outgoing, "dom", offset))
    return jnp.concatenate(pieces, 0)


def return_grads(grad_halo, num_slots, per_peer, feat_width):
    shaped = grad_halo.reshape(num_slots, per_peer, feat_width)
    pieces = []
    for slot_num, offset in enumerate(OFFSETS):
        pieces.append(shifted(shaped[slot_num], "dom", -offset))
    return jnp.concatenate(pieces, 0)


def body(
    section_inputs,
    out_cot,
    w_node,
    w_agg,
    w_out,
    bias,
    gain,
    send_rows,
    blk_pairs,
    blk_count,
    blk_values,
):
    num_segments = lax.axis_size("segment")
    segment_index = lax.axis_index("segment")
    num_peers = lax.axis_size("dom")
    inputs = section_inputs[0]
    num_micro, num_rows, feat_width = inputs.shape
    node_mat = w_node[0]
    agg_mat = w_agg[0]
    out_mat = w_out[0]
    bias_row = bias[0].astype(jnp.float32)
    gain_row = gain[0].astype(jnp.float32)
    targets = send_rows[0]
    num_slots, per_peer = targets.shape
    flat_targets = targets.reshape(-1)
    pairs = blk_pairs[0]
    live_count = blk_count[0]
    values = blk_values[0]
    row_blocks = num_rows // 128
    is_last = segment_index == num_segments - 1
    total_steps = num_micro + num_segments - 1
    carried = jnp.zeros((num_rows, feat_width), jnp.bfloat16)
    cot_result = jnp.zeros((num_micro, num_rows, feat_width), jnp.bfloat16)
    x_list, agg_list, hidden_list, pre_norm_list, preact_list = ([], [], [], [], [])
    bias_total = jnp.zeros((feat_width,), jnp.float32)
    gain_total = jnp.zeros((feat_width,), jnp.float32)
    for step_num in range(total_steps):
        micro_index = step_num - (num_segments - 1 - segment_index)
        is_live = (micro_index >= 0) & (micro_index < num_micro)
        slot_index = jnp.clip(micro_index, 0, num_micro - 1)
        x_rows = lax.dynamic_index_in_dim(inputs, slot_index, 0, keepdims=False)
        given = lax.dynamic_index_in_dim(out_cot, slot_index, 0, keepdims=False)
        grad_in = jnp.where(is_last, given, carried)
        halo_rows = fetch_halo(x_rows, targets)
        source = jnp.concatenate([x_rows, halo_rows], 0)
        agg = aggregate(source, values, pairs, live_count, row_blocks).astype(jnp.bfloat16)
        preact = (
            jnp.dot(x_rows, node_mat, preferred_element_type=jnp.float32)
            + jnp.dot(agg, agg_mat, preferred_element_type=jnp.float32)
            + bias_row
        )
        sigmoid_z = jax.nn.sigmoid(preact)
        hidden = (preact * sigmoid_z).astype(jnp.bfloat16)
        output = jnp.dot(hidden, out_mat, preferred_element_type=jnp.float32)
        centred = output - jnp.mean(output, axis=1, keepdims=True)
        inv_std = lax.rsqrt(jnp.mean(centred * centred, axis=1, keepdims=True) + EPSILON)
        normed = centred * inv_std
        grad_f32 = grad_in.astype(jnp.float32)
        grad_normed = grad_f32 * gain_row
        grad_pre_norm = (
            inv_std
            * (
                grad_normed
                - jnp.mean(grad_normed, axis=1, keepdims=True)
                - normed * jnp.mean(grad_normed * normed, axis=1, keepdims=True)
            )
        ).astype(jnp.bfloat16)
        grad_hidden = jnp.einsum(
            "rj,ij->ri", grad_pre_norm, out_mat, preferred_element_type=jnp.float32
        )
        grad_preact = (grad_hidden * sigmoid_z * (1.0 + preact * (1.0 - sigmoid_z))).astype(
            jnp.bfloat16
        )
        grad_x = grad_f32 + jnp.einsum(
            "rj,ij->ri", grad_preact, node_mat, preferred_element_type=jnp.float32
        )
        grad_messages = jnp.einsum(
            "rj,ij->ri", grad_preact, agg_mat, preferred_element_type=jnp.float32
        ).astype(jnp.bfloat16)
        grad_source = spread(grad_messages, values, pairs, live_count, source.shape[0] // 128)
        grad_x = grad_x + grad_source[:num_rows]
        grad_halo = grad_source[num_rows:].astype(jnp.bfloat16)
        returned = return_grads(grad_halo, num_slots, per_peer, feat_width)
        grad_x = grad_x.at[flat_targets].add(returned.astype(jnp.float32))
        grad_x_bf = grad_x.astype(jnp.bfloat16)
        cot_result = jnp.where(
            is_live,
            lax.dynamic_update_index_in_dim(cot_result, grad_x_bf, slot_index, 0),
            cot_result,
        )
        if step_num + 1 < total_steps:
            carried = shifted_2(grad_x_bf, "segment", -1)
        zero_rows = jnp.zeros_like(grad_preact)
        masked_preact = jnp.where(is_live, grad_preact, zero_rows)
        masked_pre_norm = jnp.where(is_live, grad_pre_norm, zero_rows)
        x_list.append(x_rows)
        agg_list.append(agg)
        hidden_list.append(hidden)
        pre_norm_list.append(masked_pre_norm)
        preact_list.append(masked_preact)
        bias_total = bias_total + jnp.sum(masked_preact.astype(jnp.float32), axis=0)
        gain_total = gain_total + jnp.where(is_live, jnp.sum(grad_f32 * normed, axis=0), 0.0)
    x_stack = jnp.stack(x_list)
    agg_stack = jnp.stack(agg_list)
    hidden_stack = jnp.stack(hidden_list)
    pre_norm_stack = jnp.stack(pre_norm_list)
    preact_stack = jnp.stack(preact_list)
    share = feat_width // num_peers
    full_node = jnp.einsum("mri,mrj->ij", x_stack, preact_stack, preferred_element_type=jnp.float32)
    full_agg = jnp.einsum(
        "mri,mrj->ij", agg_stack, preact_stack, preferred_element_type=jnp.float32
    )
    full_out = jnp.einsum(
        "mri,mrj->ij", hidden_stack, pre_norm_stack, preferred_element_type=jnp.float32
    )
    sum_node, sum_agg, sum_out, bias_sum, gain_sum = lax.psum(
        (full_node, full_agg, full_out, bias_total, gain_total), "dom"
    )
    row_start = lax.axis_index("dom") * share
    grad_node = lax.dynamic_slice_in_dim(sum_node, row_start, share, 0)
    grad_agg = lax.dynamic_slice_in_dim(sum_agg, row_start, share, 0)
    grad_out = lax.dynamic_slice_in_dim(sum_out, row_start, share, 0)
    return (
        cot_result[None],
        grad_node[None],
        grad_agg[None],
        grad_out[None],
        bias_sum[None],
        gain_sum[None],
    )


def solution(mesh):
    placed = (
        P("segment", None, ("grp", "dom"), None),
        P(None, ("grp", "dom"), None),
        P("segment", None, None),
        P("segment", None, None),
        P("segment", None, None),
        P("segment", None),
        P("segment", None),
        P("dom", None, None),
        P("dom", None, None),
        P("dom"),
        P("dom", None, None, None),
    )
    return jax.shard_map(
        body,
        mesh=mesh,
        in_specs=placed,
        out_specs=(
            P("segment", None, ("grp", "dom"), None),
            P("segment", ("grp", "dom"), None),
            P("segment", ("grp", "dom"), None),
            P("segment", ("grp", "dom"), None),
            P("segment", "grp"),
            P("segment", "grp"),
        ),
        check_vma=False,
    )
```

profile of v0, /device:TPU:0, one launch (start us, length us, event | category | flops | bytes accessed | tf_op | source)
XLA Modules:
  0.0 334.4 jit_solution(9825132496447534594)
XLA Ops:
  8.1 2.0 constant_dynamic-update-slice_fusion.14
  11.3 2.9 collective-permute-start.9
  15.5 3.0 collective-permute-start.10
  20.4 3.9 %collective-permute-start.12 = (bf16[32,512]{1,0:T(8,128)(2,1)S(1)}, bf16[32,512]{1,0:T(8,128)(2,1)}, u32[]{:S(2)}, u32[]{:S(2)}) collective-permute-start(bf16[32,512]{1,0:T(8,128)(2,1)S(1)} %gather_fusion.9), channel_id=1, source_target_pairs={{0,12},{2,14},{4,0},{6,2},{8,4},{10,6},{12,8},{14,10},{1,13},{3,15... | collective-permute-start | bytes 98312 | tf_op jit(solution)/shard_map/ppermute | solution.py:13
  38.5 4.7 %collective-permute-start.1 = (bf16[32,512]{1,0:T(8,128)(2,1)S(1)}, bf16[32,512]{1,0:T(8,128)(2,1)S(1)}, u32[]{:S(2)}, u32[]{:S(2)}) collective-permute-start(bf16[32,512]{1,0:T(8,128)(2,1)S(1)} %gather_fusion.1), channel_id=1, source_target_pairs={{0,14},{2,0},{4,2},{6,4},{8,6},{10,8},{12,10},{14,12},{1,15},{3,1}... | collective-permute-start | bytes 98312 | tf_op jit(solution)/shard_map/ppermute | solution.py:13
  44.8 5.7 %collective-permute-done.2 = bf16[32,512]{1,0:T(8,128)(2,1)S(1)} collective-permute-done((bf16[32,512]{1,0:T(8,128)(2,1)S(1)}, bf16[32,512]{1,0:T(8,128)(2,1)S(1)}, u32[]{:S(2)}, u32[]{:S(2)}) %collective-permute-start.2) | collective-permute-done | bytes 32800 | tf_op jit(solution)/shard_map/ppermute | solution.py:13
  50.5 3.9 %collective-permute-done.3 = bf16[32,512]{1,0:T(8,128)(2,1)S(1)} collective-permute-done((bf16[32,512]{1,0:T(8,128)(2,1)S(1)}, bf16[32,512]{1,0:T(8,128)(2,1)S(1)}, u32[]{:S(2)}, u32[]{:S(2)}) %collective-permute-start.3) | collective-permute-done | bytes 32800 | tf_op jit(solution)/shard_map/ppermute | solution.py:13
  54.4 1.8 collective-permute-start.18
  57.1 1.7 gather_fusion.4
  58.8 1.7 fusion.121
  60.5 3.1 copy.46
  63.6 2.7 fusion.24
  66.3 3.2 collective-permute-start.19
  71.2 5.7 %collective-permute-done.20 = bf16[32,512]{1,0:T(8,128)(2,1)S(1)} collective-permute-done((bf16[32,512]{1,0:T(8,128)(2,1)S(1)}, bf16[32,512]{1,0:T(8,128)(2,1)S(1)}, u32[]{:S(2)}, u32[]{:S(2)}) %collective-permute-start.20) | collective-permute-done | bytes 32800 | tf_op jit(solution)/shard_map/ppermute | solution.py:13
  78.0 2.8 collective-permute-done.21
  81.5 1.7 fusion.113
  83.2 3.1 copy.50
  86.3 2.7 fusion.30
  97.8 1.7 fusion.119
  99.5 3.1 copy.47
  102.5 2.7 fusion.8
  110.1 1.7 gather_fusion.10
  111.7 2.9 fusion.117
  114.6 3.1 copy.48
  117.7 2.7 fusion.27
  125.4 5.1 %collective-permute-start.4 = (bf16[32,512]{1,0:T(8,128)(2,1)S(1)}, bf16[32,512]{1,0:T(8,128)(2,1)S(1)}, u32[]{:S(2)}, u32[]{:S(2)}) collective-permute-start(bf16[32,512]{1,0:T(8,128)(2,1)S(1)} %get-tuple-element.50), channel_id=1, source_target_pairs={{0,14},{2,0},{4,2},{6,4},{8,6},{10,8},{12,10},{14,12},{1,15},{3,1}... | collective-permute-start | bytes 98312 | tf_op jit(solution)/shard_map/ppermute | solution.py:13
  132.8 4.4 %collective-permute-done.5 = bf16[32,512]{1,0:T(8,128)(2,1)S(1)} collective-permute-done((bf16[32,512]{1,0:T(8,128)(2,1)S(1)}, bf16[32,512]{1,0:T(8,128)(2,1)S(1)}, u32[]{:S(2)}, u32[]{:S(2)}) %collective-permute-start.5) | collective-permute-done | bytes 32800 | tf_op jit(solution)/shard_map/ppermute | solution.py:13
  137.2 3.3 scatter_custom_fusion
  141.3 1.8 bitcast_dynamic-update-slice_fusion.1
  144.7 2.3 fusion.165
  151.1 1.7 fusion.115
  152.9 3.1 copy.49
  155.9 2.6 fusion.4
  159.1 3.9 %collective-permute-start.13 = (bf16[32,512]{1,0:T(8,128)(2,1)S(1)}, bf16[32,512]{1,0:T(8,128)(2,1)S(1)}, u32[]{:S(2)}, u32[]{:S(2)}) collective-permute-start(bf16[32,512]{1,0:T(8,128)(2,1)S(1)} %get-tuple-element.46), channel_id=1, source_target_pairs={{0,14},{2,0},{4,2},{6,4},{8,6},{10,8},{12,10},{14,12},{1,15},{3,1}... | collective-permute-start | bytes 98312 | tf_op jit(solution)/shard_map/ppermute | solution.py:13
  163.6 2.0 collective-permute-start.16
  166.8 3.2 collective-permute-done.14
  170.0 3.3 scatter_custom_fusion.1
  173.2 2.0 fusion.101
  176.5 1.8 copy.43
  188.7 1.9 copy.76
  191.6 1.7 fusion.111
  193.3 3.1 copy.51
  196.4 2.7 fusion
  199.6 4.1 %collective-permute-start.22 = (bf16[32,512]{1,0:T(8,128)(2,1)S(1)}, bf16[32,512]{1,0:T(8,128)(2,1)S(1)}, u32[]{:S(2)}, u32[]{:S(2)}) collective-permute-start(bf16[32,512]{1,0:T(8,128)(2,1)S(1)} %get-tuple-element.42), channel_id=1, source_target_pairs={{0,14},{2,0},{4,2},{6,4},{8,6},{10,8},{12,10},{14,12},{1,15},{3,1}... | collective-permute-start | bytes 98312 | tf_op jit(solution)/shard_map/ppermute | solution.py:13
  206.4 25.3 %all-reduce = (f32[1,512]{1,0:T(1,128)}, f32[1,512]{1,0:T(1,128)}) all-reduce(f32[1,512]{1,0:T(1,128)S(1)} %bitcast.305, f32[1,512]{1,0:T(1,128)S(1)} %bitcast.304), channel_id=1, replica_groups=mesh['grp'=2,'dom'=8,'segment'=2] {'dom'}, use_global_device_ids=true, to_apply=%region_21.22 | all-reduce | flops 1024 | bytes 8192 | tf_op jit(solution)/shard_map/psum | solution.py:180
  231.8 1.7 scatter_custom_fusion.2
  233.5 1.7 bitcast_dynamic-update-slice_fusion
  235.2 87.6 %all-reduce.4.cloned.1.call-done = (f32[512,512]{1,0:T(8,128)}, f32[512,512]{1,0:T(8,128)}, f32[512,512]{1,0:T(8,128)}) async-done(((f32[512,512]{1,0:T(8,128)}, f32[512,512]{1,0:T(8,128)}, f32[512,512]{1,0:T(8,128)}), (f32[512,512]{1,0:T(8,128)}, f32[512,512]{1,0:T(8,128)}, f32[512,512]{1,0:T(8,128)})) %all-reduce.4.cloned.1.call-update) | async-done | bytes 3145744 | tf_op jit(solution)/shard_map/psum | solution.py:180
  (260 shorter events, 74.4 us)
Async XLA Ops:
  7.2 83.2 %copy-start = (bf16[1,512,512]{2,1,0:T(8,128)(2,1)S(1)}, bf16[1,512,512]{2,1,0:T(8,128)(2,1)}, u32[]{:S(2)}) copy-start(bf16[1,512,512]{2,1,0:T(8,128)(2,1)} %param.15) | copy-start | bytes 1572868
  7.2 17.8 %copy-start.49 = (s32[1,2,7]{2,1,0:T(2,128)S(1)}, s32[1,2,7]{2,1,0:T(2,128)}, u32[]{:S(2)}) copy-start(s32[1,2,7]{2,1,0:T(2,128)} %param.19) | copy-start | bytes 172
  7.2 18.4 %copy-start.2 = (bf16[1,512,512]{2,1,0:T(8,128)(2,1)S(1)}, bf16[1,512,512]{2,1,0:T(8,128)(2,1)}, u32[]{:S(2)}) copy-start(bf16[1,512,512]{2,1,0:T(8,128)(2,1)} %param.13) | copy-start | bytes 1572868
  7.2 315.7 %all-reduce.4.cloned.1.call-start = ((), (), s32[]{:S(2)}) async-start(), calls=%async_computation | async-start | bytes 6291456 | tf_op jit(solution)/shard_map/psum | solution.py:180
  10.1 17.7 %copy-start.45 = (s32[1,4,32]{2,1,0:T(4,128)S(1)}, s32[1,4,32]{2,1,0:T(4,128)}, u32[]{:S(2)}) copy-start(s32[1,4,32]{2,1,0:T(4,128)} %param.18) | copy-start | bytes 1540
  11.3 94.7 %collective-permute-start.9 = (bf16[32,512]{1,0:T(8,128)(2,1)}, bf16[32,512]{1,0:T(8,128)(2,1)}, u32[]{:S(2)}, u32[]{:S(2)}) collective-permute-start(bf16[32,512]{1,0:T(8,128)(2,1)} %gather_fusion.6), channel_id=1, source_target_pairs={{0,2},{2,4},{4,6},{6,8},{8,10},{10,12},{12,14},{14,0},{1,3},{3,5},... | collective-permute-start | bytes 98312 | tf_op jit(solution)/shard_map/ppermute | solution.py:13
  15.5 91.3 %collective-permute-start.10 = (bf16[32,512]{1,0:T(8,128)(2,1)}, bf16[32,512]{1,0:T(8,128)(2,1)}, u32[]{:S(2)}, u32[]{:S(2)}) collective-permute-start(bf16[32,512]{1,0:T(8,128)(2,1)} %gather_fusion.7), channel_id=1, source_target_pairs={{0,14},{2,0},{4,2},{6,4},{8,6},{10,8},{12,10},{14,12},{1,15},{3,1}... | collective-permute-start | bytes 98312 | tf_op jit(solution)/shard_map/ppermute | solution.py:13
  19.8 87.8 %collective-permute-start.11 = (bf16[32,512]{1,0:T(8,128)(2,1)}, bf16[32,512]{1,0:T(8,128)(2,1)}, u32[]{:S(2)}, u32[]{:S(2)}) collective-permute-start(bf16[32,512]{1,0:T(8,128)(2,1)} %gather_fusion.8), channel_id=1, source_target_pairs={{0,4},{2,6},{4,8},{6,10},{8,12},{10,14},{12,0},{14,2},{1,5},{3,7},... | collective-permute-start | bytes 98312 | tf_op jit(solution)/shard_map/ppermute | solution.py:13
  20.4 88.9 %collective-permute-start.12 = (bf16[32,512]{1,0:T(8,128)(2,1)S(1)}, bf16[32,512]{1,0:T(8,128)(2,1)}, u32[]{:S(2)}, u32[]{:S(2)}) collective-permute-start(bf16[32,512]{1,0:T(8,128)(2,1)S(1)} %gather_fusion.9), channel_id=1, source_target_pairs={{0,12},{2,14},{4,0},{6,2},{8,4},{10,6},{12,8},{14,10},{1,13},{3,15... | collective-permute-start | bytes 98312 | tf_op jit(solution)/shard_map/ppermute | solution.py:13
  24.9 13.5 %collective-permute-start = (bf16[32,512]{1,0:T(8,128)(2,1)S(1)}, bf16[32,512]{1,0:T(8,128)(2,1)S(1)}, u32[]{:S(2)}, u32[]{:S(2)}) collective-permute-start(bf16[32,512]{1,0:T(8,128)(2,1)S(1)} %gather_fusion), channel_id=1, source_target_pairs={{0,2},{2,4},{4,6},{6,8},{8,10},{10,12},{12,14},{14,0},{1,3},{3,5},... | collective-permute-start | bytes 98312 | tf_op jit(solution)/shard_map/ppermute | solution.py:13
  31.4 7.0 %copy-start.50 = (bf16[1,512]{1,0:T(2,128)(2,1)S(1)}, bf16[1,512]{1,0:T(2,128)(2,1)}, u32[]{:S(2)}) copy-start(bf16[1,512]{1,0:T(2,128)(2,1)} %param.16) | copy-start | bytes 3076
  31.4 7.0 %copy-start.51 = (bf16[1,512]{1,0:T(2,128)(2,1)S(1)}, bf16[1,512]{1,0:T(2,128)(2,1)}, u32[]{:S(2)}) copy-start(bf16[1,512]{1,0:T(2,128)(2,1)} %param.17) | copy-start | bytes 3076
  34.6 24.3 %copy-start.3 = (bf16[1,7,128,128]{3,2,1,0:T(8,128)(2,1)S(1)}, bf16[1,7,128,128]{3,2,1,0:T(8,128)(2,1)}, u32[]{:S(2)}) copy-start(bf16[1,7,128,128]{3,2,1,0:T(8,128)(2,1)} %param.21) | copy-start | bytes 688132
  38.5 6.3 %collective-permute-start.1 = (bf16[32,512]{1,0:T(8,128)(2,1)S(1)}, bf16[32,512]{1,0:T(8,128)(2,1)S(1)}, u32[]{:S(2)}, u32[]{:S(2)}) collective-permute-start(bf16[32,512]{1,0:T(8,128)(2,1)S(1)} %gather_fusion.1), channel_id=1, source_target_pairs={{0,14},{2,0},{4,2},{6,4},{8,6},{10,8},{12,10},{14,12},{1,15},{3,1}... | collective-permute-start | bytes 98312 | tf_op jit(solution)/shard_map/ppermute | solution.py:13
  44.8 5.7 %collective-permute-start.2 = (bf16[32,512]{1,0:T(8,128)(2,1)S(1)}, bf16[32,512]{1,0:T(8,128)(2,1)S(1)}, u32[]{:S(2)}, u32[]{:S(2)}) collective-permute-start(bf16[32,512]{1,0:T(8,128)(2,1)S(1)} %gather_fusion.2), channel_id=1, source_target_pairs={{0,4},{2,6},{4,8},{6,10},{8,12},{10,14},{12,0},{14,2},{1,5},{3,7},... | collective-permute-start | bytes 98312 | tf_op jit(solution)/shard_map/ppermute | solution.py:13
  50.5 3.9 %collective-permute-start.3 = (bf16[32,512]{1,0:T(8,128)(2,1)S(1)}, bf16[32,512]{1,0:T(8,128)(2,1)S(1)}, u32[]{:S(2)}, u32[]{:S(2)}) collective-permute-start(bf16[32,512]{1,0:T(8,128)(2,1)S(1)} %gather_fusion.3), channel_id=1, source_target_pairs={{0,12},{2,14},{4,0},{6,2},{8,4},{10,6},{12,8},{14,10},{1,13},{3,15... | collective-permute-start | bytes 98312 | tf_op jit(solution)/shard_map/ppermute | solution.py:13
  54.4 11.9 %collective-permute-start.18 = (bf16[32,512]{1,0:T(8,128)(2,1)S(1)}, bf16[32,512]{1,0:T(8,128)(2,1)S(1)}, u32[]{:S(2)}, u32[]{:S(2)}) collective-permute-start(bf16[32,512]{1,0:T(8,128)(2,1)S(1)} %gather_fusion.12), channel_id=1, source_target_pairs={{0,2},{2,4},{4,6},{6,8},{8,10},{10,12},{12,14},{14,0},{1,3},{3,5},... | collective-permute-start | bytes 98312 | tf_op jit(solution)/shard_map/ppermute | solution.py:13
  66.3 4.8 %collective-permute-start.19 = (bf16[32,512]{1,0:T(8,128)(2,1)S(1)}, bf16[32,512]{1,0:T(8,128)(2,1)S(1)}, u32[]{:S(2)}, u32[]{:S(2)}) collective-permute-start(bf16[32,512]{1,0:T(8,128)(2,1)S(1)} %gather_fusion.13), channel_id=1, source_target_pairs={{0,14},{2,0},{4,2},{6,4},{8,6},{10,8},{12,10},{14,12},{1,15},{3,1}... | collective-permute-start | bytes 98312 | tf_op jit(solution)/shard_map/ppermute | solution.py:13
  71.2 5.7 %collective-permute-start.20 = (bf16[32,512]{1,0:T(8,128)(2,1)S(1)}, bf16[32,512]{1,0:T(8,128)(2,1)S(1)}, u32[]{:S(2)}, u32[]{:S(2)}) collective-permute-start(bf16[32,512]{1,0:T(8,128)(2,1)S(1)} %gather_fusion.14), channel_id=1, source_target_pairs={{0,4},{2,6},{4,8},{6,10},{8,12},{10,14},{12,0},{14,2},{1,5},{3,7},... | collective-permute-start | bytes 98312 | tf_op jit(solution)/shard_map/ppermute | solution.py:13
  76.9 3.9 %collective-permute-start.21 = (bf16[32,512]{1,0:T(8,128)(2,1)S(1)}, bf16[32,512]{1,0:T(8,128)(2,1)S(1)}, u32[]{:S(2)}, u32[]{:S(2)}) collective-permute-start(bf16[32,512]{1,0:T(8,128)(2,1)S(1)} %gather_fusion.15), channel_id=1, source_target_pairs={{0,12},{2,14},{4,0},{6,2},{8,4},{10,6},{12,8},{14,10},{1,13},{3,15... | collective-permute-start | bytes 98312 | tf_op jit(solution)/shard_map/ppermute | solution.py:13
  78.0 14.0 %copy-start.11 = (bf16[2,128,512]{2,1,0:T(8,128)(2,1)}, bf16[2,128,512]{2,1,0:T(8,128)(2,1)S(1)}, u32[]{:S(2)}) copy-start(bf16[2,128,512]{2,1,0:T(8,128)(2,1)S(1)} %copy.27) | copy-start | bytes 786436
  105.2 6.5 %copy-start.4 = (f32[3,128,512]{2,0,1:T(4,128)}, f32[3,128,512]{2,0,1:T(4,128)S(1)}, u32[]{:S(2)}) copy-start(f32[3,128,512]{2,0,1:T(4,128)S(1)} %fusion.8) | copy-start | bytes 2359300
  122.7 9.9 %copy-start.53 = (f32[256]{0:T(256)S(1)}, f32[256]{0:T(256)}, u32[]{:S(2)}) copy-start(f32[256]{0:T(256)} %get-tuple-element.66) | copy-start | bytes 3076
  122.7 9.9 %copy-start.5 = (f32[256,512]{1,0:T(8,128)S(1)}, f32[256,512]{1,0:T(8,128)}, u32[]{:S(2)}) copy-start(f32[256,512]{1,0:T(8,128)} %get-tuple-element.67) | copy-start | bytes 1572868
  125.4 7.4 %collective-permute-start.4 = (bf16[32,512]{1,0:T(8,128)(2,1)S(1)}, bf16[32,512]{1,0:T(8,128)(2,1)S(1)}, u32[]{:S(2)}, u32[]{:S(2)}) collective-permute-start(bf16[32,512]{1,0:T(8,128)(2,1)S(1)} %get-tuple-element.50), channel_id=1, source_target_pairs={{0,14},{2,0},{4,2},{6,4},{8,6},{10,8},{12,10},{14,12},{1,15},{3,1}... | collective-permute-start | bytes 98312 | tf_op jit(solution)/shard_map/ppermute | solution.py:13
  130.5 6.6 %collective-permute-start.5 = (bf16[32,512]{1,0:T(8,128)(2,1)S(1)}, bf16[32,512]{1,0:T(8,128)(2,1)S(1)}, u32[]{:S(2)}, u32[]{:S(2)}) collective-permute-start(bf16[32,512]{1,0:T(8,128)(2,1)S(1)} %get-tuple-element.53), channel_id=1, source_target_pairs={{0,2},{2,4},{4,6},{6,8},{8,10},{10,12},{12,14},{14,0},{1,3},{3,5},... | collective-permute-start | bytes 98312 | tf_op jit(solution)/shard_map/ppermute | solution.py:13
  130.5 6.6 %collective-permute-start.6 = (bf16[32,512]{1,0:T(8,128)(2,1)S(1)}, bf16[32,512]{1,0:T(8,128)(2,1)S(1)}, u32[]{:S(2)}, u32[]{:S(2)}) collective-permute-start(bf16[32,512]{1,0:T(8,128)(2,1)S(1)} %get-tuple-element.52), channel_id=1, source_target_pairs={{0,12},{2,14},{4,0},{6,2},{8,4},{10,6},{12,8},{14,10},{1,13},{3,15... | collective-permute-start | bytes 98312 | tf_op jit(solution)/shard_map/ppermute | solution.py:13
  131.2 6.0 %collective-permute-start.7 = (bf16[32,512]{1,0:T(8,128)(2,1)S(1)}, bf16[32,512]{1,0:T(8,128)(2,1)S(1)}, u32[]{:S(2)}, u32[]{:S(2)}) collective-permute-start(bf16[32,512]{1,0:T(8,128)(2,1)S(1)} %get-tuple-element.51), channel_id=1, source_target_pairs={{0,4},{2,6},{4,8},{6,10},{8,12},{10,14},{12,0},{14,2},{1,5},{3,7},... | collective-permute-start | bytes 98312 | tf_op jit(solution)/shard_map/ppermute | solution.py:13
  143.1 6.2 %copy-start.26 = (f32[256,512]{1,0:T(8,128)S(1)}, f32[256,512]{1,0:T(8,128)}, u32[]{:S(2)}) copy-start(f32[256,512]{1,0:T(8,128)} %copy-done.25) | copy-start | bytes 1572868
  143.1 3.9 %collective-permute-start.8 = (bf16[256,512]{1,0:T(8,128)(2,1)S(1)}, bf16[256,512]{1,0:T(8,128)(2,1)S(1)}, u32[]{:S(2)}, u32[]{:S(2)}) collective-permute-start(bf16[256,512]{1,0:T(8,128)(2,1)S(1)} %get-tuple-element.35), channel_id=1, source_target_pairs={{1,0},{3,2},{5,4},{7,6},{9,8},{11,10},{13,12},{15,14},{17,16},{19,... | collective-permute-start | bytes 786440 | tf_op jit(solution)/shard_map/ppermute | solution.py:19
  158.6 7.1 %copy-start.19 = (bf16[256,512]{1,0:T(8,128)(2,1)S(1)}, bf16[256,512]{1,0:T(8,128)(2,1)}, u32[]{:S(2)}) copy-start(bf16[256,512]{1,0:T(8,128)(2,1)} %copy-done.18) | copy-start | bytes 786436
  158.6 7.1 %copy-start.23 = (bf16[256,512]{1,0:T(8,128)(2,1)S(1)}, bf16[256,512]{1,0:T(8,128)(2,1)}, u32[]{:S(2)}) copy-start(bf16[256,512]{1,0:T(8,128)(2,1)} %copy-done.22) | copy-start | bytes 786436
  159.1 7.7 %collective-permute-start.13 = (bf16[32,512]{1,0:T(8,128)(2,1)S(1)}, bf16[32,512]{1,0:T(8,128)(2,1)S(1)}, u32[]{:S(2)}, u32[]{:S(2)}) collective-permute-start(bf16[32,512]{1,0:T(8,128)(2,1)S(1)} %get-tuple-element.46), channel_id=1, source_target_pairs={{0,14},{2,0},{4,2},{6,4},{8,6},{10,8},{12,10},{14,12},{1,15},{3,1}... | collective-permute-start | bytes 98312 | tf_op jit(solution)/shard_map/ppermute | solution.py:13
  163.0 7.0 %collective-permute-start.14 = (bf16[32,512]{1,0:T(8,128)(2,1)S(1)}, bf16[32,512]{1,0:T(8,128)(2,1)S(1)}, u32[]{:S(2)}, u32[]{:S(2)}) collective-permute-start(bf16[32,512]{1,0:T(8,128)(2,1)S(1)} %get-tuple-element.49), channel_id=1, source_target_pairs={{0,2},{2,4},{4,6},{6,8},{8,10},{10,12},{12,14},{14,0},{1,3},{3,5},... | collective-permute-start | bytes 98312 | tf_op jit(solution)/shard_map/ppermute | solution.py:13
  163.6 6.3 %collective-permute-start.15 = (bf16[32,512]{1,0:T(8,128)(2,1)S(1)}, bf16[32,512]{1,0:T(8,128)(2,1)S(1)}, u32[]{:S(2)}, u32[]{:S(2)}) collective-permute-start(bf16[32,512]{1,0:T(8,128)(2,1)S(1)} %get-tuple-element.48), channel_id=1, source_target_pairs={{0,12},{2,14},{4,0},{6,2},{8,4},{10,6},{12,8},{14,10},{1,13},{3,15... | collective-permute-start | bytes 98312 | tf_op jit(solution)/shard_map/ppermute | solution.py:13
  163.6 6.3 %collective-permute-start.16 = (bf16[32,512]{1,0:T(8,128)(2,1)S(1)}, bf16[32,512]{1,0:T(8,128)(2,1)S(1)}, u32[]{:S(2)}, u32[]{:S(2)}) collective-permute-start(bf16[32,512]{1,0:T(8,128)(2,1)S(1)} %get-tuple-element.47), channel_id=1, source_target_pairs={{0,4},{2,6},{4,8},{6,10},{8,12},{10,14},{12,0},{14,2},{1,5},{3,7},... | collective-permute-start | bytes 98312 | tf_op jit(solution)/shard_map/ppermute | solution.py:13
  165.7 12.7 %copy-start.14 = (bf16[2,128,512]{2,1,0:T(8,128)(2,1)S(1)}, bf16[2,128,512]{2,1,0:T(8,128)(2,1)}, u32[]{:S(2)}) copy-start(bf16[2,128,512]{2,1,0:T(8,128)(2,1)} %copy-done.13) | copy-start | bytes 786436
  165.7 13.5 %copy-start.12 = (bf16[2,128,512]{2,1,0:T(8,128)(2,1)S(1)}, bf16[2,128,512]{2,1,0:T(8,128)(2,1)}, u32[]{:S(2)}) copy-start(bf16[2,128,512]{2,1,0:T(8,128)(2,1)} %copy-done.11) | copy-start | bytes 786436
  166.8 14.2 %copy-start.10 = (bf16[2,256,512]{2,1,0:T(8,128)(2,1)S(1)}, bf16[2,256,512]{2,1,0:T(8,128)(2,1)}, u32[]{:S(2)}) copy-start(bf16[2,256,512]{2,1,0:T(8,128)(2,1)} %param.12) | copy-start | bytes 1572868
  175.2 5.8 %collective-permute-start.17 = (bf16[256,512]{1,0:T(8,128)(2,1)}, bf16[256,512]{1,0:T(8,128)(2,1)}, u32[]{:S(2)}, u32[]{:S(2)}) collective-permute-start(bf16[256,512]{1,0:T(8,128)(2,1)} %get-tuple-element.30), channel_id=1, source_target_pairs={{1,0},{3,2},{5,4},{7,6},{9,8},{11,10},{13,12},{15,14},{17,16},{19,... | collective-permute-start | bytes 786440 | tf_op jit(solution)/shard_map/ppermute | solution.py:19
  183.1 7.4 %copy-start.16 = (bf16[256,512]{1,0:T(8,128)(2,1)}, bf16[256,512]{1,0:T(8,128)(2,1)S(1)}, u32[]{:S(2)}) copy-start(bf16[256,512]{1,0:T(8,128)(2,1)S(1)} %get-tuple-element.69) | copy-start | bytes 786436
  199.1 7.0 %copy-start.44 = (f32[512]{0:T(512)S(1)}, f32[512]{0:T(512)}, u32[]{:S(2)}) copy-start(f32[512]{0:T(512)} %get-tuple-element.6) | copy-start | bytes 6148
  199.1 7.0 %copy-start.17 = (bf16[256,512]{1,0:T(8,128)(2,1)S(1)}, bf16[256,512]{1,0:T(8,128)(2,1)}, u32[]{:S(2)}) copy-start(bf16[256,512]{1,0:T(8,128)(2,1)} %copy-done.16) | copy-start | bytes 786436
  199.3 7.1 %copy-start.52 = (f32[512]{0:T(512)S(1)}, f32[512]{0:T(512)}, u32[]{:S(2)}) copy-start(f32[512]{0:T(512)} %get-tuple-element.70) | copy-start | bytes 6148
  199.6 32.1 %collective-permute-start.22 = (bf16[32,512]{1,0:T(8,128)(2,1)S(1)}, bf16[32,512]{1,0:T(8,128)(2,1)S(1)}, u32[]{:S(2)}, u32[]{:S(2)}) collective-permute-start(bf16[32,512]{1,0:T(8,128)(2,1)S(1)} %get-tuple-element.42), channel_id=1, source_target_pairs={{0,14},{2,0},{4,2},{6,4},{8,6},{10,8},{12,10},{14,12},{1,15},{3,1}... | collective-permute-start | bytes 98312 | tf_op jit(solution)/shard_map/ppermute | solution.py:13
  203.8 28.0 %collective-permute-start.23 = (bf16[32,512]{1,0:T(8,128)(2,1)S(1)}, bf16[32,512]{1,0:T(8,128)(2,1)S(1)}, u32[]{:S(2)}, u32[]{:S(2)}) collective-permute-start(bf16[32,512]{1,0:T(8,128)(2,1)S(1)} %get-tuple-element.45), channel_id=1, source_target_pairs={{0,2},{2,4},{4,6},{6,8},{8,10},{10,12},{12,14},{14,0},{1,3},{3,5},... | collective-permute-start | bytes 98312 | tf_op jit(solution)/shard_map/ppermute | solution.py:13
  204.0 27.7 %collective-permute-start.24 = (bf16[32,512]{1,0:T(8,128)(2,1)S(1)}, bf16[32,512]{1,0:T(8,128)(2,1)S(1)}, u32[]{:S(2)}, u32[]{:S(2)}) collective-permute-start(bf16[32,512]{1,0:T(8,128)(2,1)S(1)} %get-tuple-element.44), channel_id=1, source_target_pairs={{0,12},{2,14},{4,0},{6,2},{8,4},{10,6},{12,8},{14,10},{1,13},{3,15... | collective-permute-start | bytes 98312 | tf_op jit(solution)/shard_map/ppermute | solution.py:13
  204.4 27.4 %collective-permute-start.25 = (bf16[32,512]{1,0:T(8,128)(2,1)S(1)}, bf16[32,512]{1,0:T(8,128)(2,1)S(1)}, u32[]{:S(2)}, u32[]{:S(2)}) collective-permute-start(bf16[32,512]{1,0:T(8,128)(2,1)S(1)} %get-tuple-element.43), channel_id=1, source_target_pairs={{0,4},{2,6},{4,8},{6,10},{8,12},{10,14},{12,0},{14,2},{1,5},{3,7},... | collective-permute-start | bytes 98312 | tf_op jit(solution)/shard_map/ppermute | solution.py:13
  (34 other events, 65.7 us)
Sparse Core Ops, SparseCore 0:
  188.8 134.0 all-reduce.3
where the time goes:
time: 336 us; the launch traced here: 334 us
  waiting for transfers between devices  117 us (35%)
  local copies, waits for them, and re-layouts  61.1 us (18%)
  matrix products  44.5 us (13%)
  starting transfers between devices  43.9 us (13%)
  other arithmetic  27.6 us (8%)
  blocking collectives  25.3 us (8%)
  between operations  15.6 us (5%)
    psum x1, waiting for transfers between devices, body(): lax.psum((full_node, full_agg, full_out, bias_total, gain_total), 'dom')  87.6 us
    ppermute x24, starting transfers between devices, shifted(): lax.ppermute(x, axis, [(i, (i + by) % devices) for i in range(devices)])  40.9 us
    ppermute x24, waiting for transfers between devices, shifted(): lax.ppermute(x, axis, [(i, (i + by) % devices) for i in range(devices)])  28.9 us
    psum x1, blocking collectives, body(): lax.psum((full_node, full_agg, full_out, bias_total, gain_total), 'dom')  25.3 us
    unnamed x119, local copies, waits for them, and re-layouts  10.6 us
    gather x12, local copies, waits for them, and re-layouts, fetch_halo(): outgoing = x_rows[targets[slot_num]]  9.37 us
    dot_general x3, local copies, waits for them, and re-layouts, spread(): jnp.einsum('kij,kid->kjd', values, picked, preferred_element_type=jnp.flo...  9.2 us
    dot_general x3, local copies, waits for them, and re-layouts, aggregate(): jnp.einsum('kij,kjd->kid', values, picked, preferred_element_type=jnp.flo...  9.2 us
  transfers between devices with their start and end apart: 27, of which 9 were waited for; matrix products, arithmetic and copies ran while one was open for 23% of the time, Pallas kernels for 0%

commit v1 on v0

v1 whole, which is shorter than its diff:
```python
import functools

import jax
import jax.numpy as jnp
from jax import lax
from jax.experimental import pallas as pl
from jax.experimental.pallas import tpu as pltpu
from jax.sharding import PartitionSpec as P

EPSILON = 1e-05
OFFSETS = (1, -1, 2, -2)
F32 = jnp.float32
BF16 = jnp.bfloat16
VMEM = pl.BlockSpec(memory_space=pltpu.VMEM)
SMEM = pl.BlockSpec(memory_space=pltpu.SMEM)
EXTRA = 8


def nt_dot(a, b):
    return lax.dot_general(a, b, (((1,), (1,)), ((), ())), preferred_element_type=F32)


def tn_dot(a, b):
    return lax.dot_general(a, b, (((0,), (0,)), ((), ())), preferred_element_type=F32)


def call(kernel, outs, scratch, flops, byts, *args):
    specs = [SMEM if a.dtype == jnp.int32 and a.ndim < 3 and a.size < 64 else VMEM for a in args]
    return pl.pallas_call(
        kernel,
        out_shape=outs,
        in_specs=specs,
        out_specs=jax.tree.map(lambda _: VMEM, outs),
        scratch_shapes=scratch,
        compiler_params=pltpu.CompilerParams(vmem_limit_bytes=48 * 1024 * 1024),
        cost_estimate=pl.CostEstimate(flops=flops, bytes_accessed=byts, transcendentals=0),
    )(*args)


def gather_kernel(targets_ref, x_ref, *outs):
    micro, rows, _ = x_ref.shape
    for k in range(len(OFFSETS)):
        per_peer = outs[k].shape[0] // micro
        ids = targets_ref[k]
        onehot = (lax.broadcasted_iota(jnp.int32, (per_peer, rows), 1) == ids).astype(BF16)
        for m in range(micro):
            outs[k][m * per_peer : (m + 1) * per_peer, :] = jnp.dot(
                onehot, x_ref[m], preferred_element_type=F32
            ).astype(BF16)


def node_kernel(x_ref, w_ref, bias_ref, z_ref):
    micro, rows, _ = x_ref.shape
    for m in range(micro):
        z_ref[m * rows : (m + 1) * rows, :] = (
            jnp.dot(x_ref[m], w_ref[...], preferred_element_type=F32) + bias_ref[...].astype(F32)
        )


def layer_back(g, dact, normed, inv_std, gain, w_out_ref):
    e = g * gain
    gpn = (
        inv_std
        * (
            e
            - jnp.mean(e, axis=1, keepdims=True)
            - normed * jnp.mean(e * normed, axis=1, keepdims=True)
        )
    ).astype(BF16)
    gpre = (nt_dot(gpn, w_out_ref[...]) * dact).astype(BF16)
    return gpn, gpre


def spread_out(pairs_ref, count_ref, values_ref, gm_ref, t_ref, cpart_ref, halo_outs):
    slots = values_ref.shape[0]
    micro_rows = cpart_ref.shape[0] // 2
    feat = cpart_ref.shape[1]
    t_ref[...] = jnp.zeros_like(t_ref)
    for k in range(slots):

        @pl.when(k < count_ref[0])
        def _():
            src = pairs_ref[1, k]
            t_ref[src] += tn_dot(values_ref[k], gm_ref[pairs_ref[0, k]])

    row_blocks = micro_rows // 128
    for m in range(2):
        cols = slice(m * feat, (m + 1) * feat)
        for b in range(row_blocks):
            rows = slice(m * micro_rows + b * 128, m * micro_rows + (b + 1) * 128)
            cpart_ref[rows, :] += t_ref[b, :, cols]
        for k in range(len(halo_outs)):
            per_peer = halo_outs[k].shape[0] // 2
            first = k * per_peer
            blk, off = row_blocks + first // 128, first % 128
            halo_outs[k][m * per_peer : (m + 1) * per_peer, :] = t_ref[
                blk, off : off + per_peer, cols
            ].astype(BF16)


def tail(m, rows, g, gpre, w_node_ref, w_agg_ref, cpart_ref, gm_ref):
    feat = w_node_ref.shape[0]
    cpart_ref[m * rows : (m + 1) * rows, :] = g + nt_dot(gpre, w_node_ref[...])
    gm = nt_dot(gpre, w_agg_ref[...]).astype(BF16)
    for b in range(rows // 128):
        gm_ref[b, :, m * feat : (m + 1) * feat] = gm[b * 128 : (b + 1) * 128]


def first_kernel(
    pairs_ref, count_ref, x_ref, h0, h1, h2, h3, values_ref, z_ref, g_ref, w_node_ref, w_agg_ref,
    w_out_ref, gain_ref,
    o0, o1, o2, o3, cpart_ref, dact_ref, normed_ref, inv_ref, agg_ref, hidden_ref, gpn_ref,
    gpre_ref, sums_ref,
    src_ref, acc_ref, gm_ref, t_ref,
):
    micro, rows, feat = x_ref.shape
    row_blocks = rows // 128
    halos = (h0, h1, h2, h3)
    for m in range(micro):
        cols = slice(m * feat, (m + 1) * feat)
        for b in range(row_blocks):
            src_ref[b, :, cols] = x_ref[m, b * 128 : (b + 1) * 128, :]
        for k, h in enumerate(halos):
            per_peer = h.shape[0] // micro
            first = k * per_peer
            blk, off = row_blocks + first // 128, first % 128
            src_ref[blk, off : off + per_peer, cols] = h[m * per_peer : (m + 1) * per_peer, :]
    acc_ref[...] = jnp.zeros_like(acc_ref)
    for k in range(values_ref.shape[0]):

        @pl.when(k < count_ref[0])
        def _():
            dst = pairs_ref[0, k]
            acc_ref[dst] += jnp.dot(
                values_ref[k], src_ref[pairs_ref[1, k]], preferred_element_type=F32
            )

    gain = gain_ref[...].astype(F32)
    gain_sum = jnp.zeros((1, feat), F32)
    bias_sum = jnp.zeros((1, feat), F32)
    for m in range(micro):
        part = slice(m * rows, (m + 1) * rows)
        agg = jnp.concatenate(
            [acc_ref[b, :, m * feat : (m + 1) * feat] for b in range(row_blocks)], 0
        ).astype(BF16)
        agg_ref[part, :] = agg
        preact = z_ref[part, :] + jnp.dot(agg, w_agg_ref[...], preferred_element_type=F32)
        sig = 1.0 / (1.0 + jnp.exp(-preact))
        hidden = (preact * sig).astype(BF16)
        dact = sig * (1.0 + preact * (1.0 - sig))
        dact_ref[part, :] = dact
        hidden_ref[part, :] = hidden
        output = jnp.dot(hidden, w_out_ref[...], preferred_element_type=F32)
        centred = output - jnp.mean(output, axis=1, keepdims=True)
        inv_std = lax.rsqrt(jnp.mean(centred * centred, axis=1, keepdims=True) + EPSILON)
        normed = centred * inv_std
        normed_ref[part, :] = normed
        inv_ref[part, :] = jnp.broadcast_to(inv_std, (rows, 128))
        g = g_ref[m].astype(F32)
        gpn, gpre = layer_back(g, dact, normed, inv_std, gain, w_out_ref)
        gpn_ref[part, :] = gpn
        gpre_ref[part, :] = gpre
        gain_sum += jnp.sum(g * normed, axis=0, keepdims=True)
        bias_sum += jnp.sum(gpre.astype(F32), axis=0, keepdims=True)
        tail(m, rows, g, gpre, w_node_ref, w_agg_ref, cpart_ref, gm_ref)
    sums_ref[0:1, :] = bias_sum
    sums_ref[1:2, :] = gain_sum
    spread_out(pairs_ref, count_ref, values_ref, gm_ref, t_ref, cpart_ref, (o0, o1, o2, o3))


def scatter_onehot(targets_ref, rows):
    ids = targets_ref[...]
    return (lax.broadcasted_iota(jnp.int32, (ids.shape[0], rows), 1) == ids).astype(BF16)


def scatter_add(onehot, rets, m):
    per_peer = rets[0].shape[0] // 2
    ret = jnp.concatenate([r[m * per_peer : (m + 1) * per_peer, :] for r in rets], 0)
    return tn_dot(onehot, ret)


def second_kernel(
    me_ref, pairs_ref, count_ref, targets_ref, r0, r1, r2, r3, cin_ref, values_ref, dact_ref,
    normed_ref, inv_ref, gpn1_ref, gpre1_ref, sums1_ref, w_node_ref, w_agg_ref, w_out_ref, gain_ref,
    o0, o1, o2, o3, cpart_ref, g_out_ref, gpn_ref, gpre_ref, sums_ref,
    gm_ref, t_ref,
):
    rows = dact_ref.shape[0] // 2
    feat = dact_ref.shape[1]
    onehot = scatter_onehot(targets_ref, rows)
    gain = gain_ref[...].astype(F32)
    is_last = me_ref[0] == 1
    gain_sum = jnp.zeros((1, feat), F32)
    bias_sum = jnp.zeros((1, feat), F32)
    for m in range(2):
        part = slice(m * rows, (m + 1) * rows)
        g16 = (cin_ref[part, :] + scatter_add(onehot, (r0, r1, r2, r3), m)).astype(BF16)
        g_out_ref[part, :] = g16
        g = g16.astype(F32)
        normed = normed_ref[part, :]
        gpn, gpre = layer_back(
            g, dact_ref[part, :], normed, inv_ref[part, 0:1], gain, w_out_ref
        )
        gpn_ref[part, :] = jnp.where(is_last, gpn1_ref[part, :], gpn)
        gpre_ref[part, :] = jnp.where(is_last, gpre1_ref[part, :], gpre)
        gain_sum += jnp.sum(g * normed, axis=0, keepdims=True)
        bias_sum += jnp.sum(gpre.astype(F32), axis=0, keepdims=True)
        tail(m, rows, g, gpre, w_node_ref, w_agg_ref, cpart_ref, gm_ref)
    sums_ref[0:1, :] = jnp.where(is_last, sums1_ref[0:1, :], bias_sum)
    sums_ref[1:2, :] = jnp.where(is_last, sums1_ref[1:2, :], gain_sum)
    spread_out(pairs_ref, count_ref, values_ref, gm_ref, t_ref, cpart_ref, (o0, o1, o2, o3))


def split_chunks(refs_at, keep_ref, send_ref, bit, mine):
    count = 2 * keep_ref.shape[0]
    step = 1 << bit
    low = [d for d in range(count) if not d & step]
    for i, d in enumerate(low):
        refs_at(d + mine * step, i, keep_ref, False)
        refs_at(d + (1 - mine) * step, i, send_ref, True)


def weight_kernel(
    me_ref, x_ref, agg_ref, hidden_ref, gpn_ref, gpre_ref, sums_ref,
    keep_a, keep_b, send_a, send_b, node_s, agg_s, out_s,
):
    micro, rows, feat = x_ref.shape
    chunks = node_s.shape[0]
    share = feat // chunks
    half = share // 2
    gpre = gpre_ref[...]
    node = tn_dot(x_ref[0], gpre[:rows]) + tn_dot(x_ref[1], gpre[rows:])
    node_s[...] = node.reshape(chunks, share, feat)
    agg_s[...] = tn_dot(agg_ref[...], gpre).reshape(chunks, share, feat)

    def put_a(d, i, ref, narrow):
        ref[i, 0:share, :] = node_s[d].astype(ref.dtype)
        ref[i, share : share + half, :] = agg_s[d, 0:half, :].astype(ref.dtype)

    split_chunks(put_a, keep_a, send_a, 0, me_ref[1])
    out_s[...] = tn_dot(hidden_ref[...], gpn_ref[...]).reshape(chunks, share, feat)
    sums = jnp.concatenate([sums_ref[0:2, :], jnp.zeros((EXTRA - 2, feat), F32)], 0)

    def put_b(d, i, ref, narrow):
        ref[i, 0:half, :] = agg_s[d, half:share, :].astype(ref.dtype)
        ref[i, half : half + share, :] = out_s[d].astype(ref.dtype)
        ref[i, half + share : half + share + EXTRA, :] = sums.astype(ref.dtype)

    split_chunks(put_b, keep_b, send_b, 1, me_ref[2])


def halve_kernel(bits, me_ref, keep_a, keep_b, recv_a, recv_b, keep_a2, keep_b2, send_a2, send_b2):
    for (pos, which), keep, recv, keep2, send2 in (
        (bits[0], keep_a, recv_a, keep_a2, send_a2),
        (bits[1], keep_b, recv_b, keep_b2, send_b2),
    ):

        def put(d, i, ref, narrow):
            ref[i] = (keep[d] + recv[d].astype(F32)).astype(ref.dtype)

        split_chunks(put, keep2, send2, pos, me_ref[which])


def last_kernel(keep_a, keep_b, recv_a, recv_b, node_ref, agg_ref, out_ref, sums_ref):
    share = node_ref.shape[0]
    half = share // 2
    a = keep_a[0] + recv_a[0].astype(F32)
    b = keep_b[0] + recv_b[0].astype(F32)
    node_ref[...] = a[0:share]
    agg_ref[0:half, :] = a[share : share + half]
    agg_ref[half:share, :] = b[0:half]
    out_ref[...] = b[half : half + share]
    sums_ref[...] = b[half + share : half + share + EXTRA]


def cot_kernel(me_ref, targets_ref, r0, r1, r2, r3, cpart_ref, other_ref, cot_ref):
    micro, rows, feat = cot_ref.shape

    @pl.when(me_ref[0] == 1)
    def _():
        for m in range(micro):
            cot_ref[m] = other_ref[m * rows : (m + 1) * rows, :]

    @pl.when(me_ref[0] != 1)
    def _():
        onehot = scatter_onehot(targets_ref, rows)
        for m in range(micro):
            cot_ref[m] = (
                cpart_ref[m * rows : (m + 1) * rows, :] + scatter_add(onehot, (r0, r1, r2, r3), m)
            ).astype(BF16)


def whole_kernel(x_ref, agg_ref, hidden_ref, gpn_ref, gpre_ref, node_ref, agg_out, out_ref):
    rows = x_ref.shape[1]
    gpre = gpre_ref[...]
    node_ref[...] = tn_dot(x_ref[0], gpre[:rows]) + tn_dot(x_ref[1], gpre[rows:])
    agg_out[...] = tn_dot(agg_ref[...], gpre)
    out_ref[...] = tn_dot(hidden_ref[...], gpn_ref[...])


def shape(dims, dtype):
    return jax.ShapeDtypeStruct(dims, dtype)


def body(
    section_inputs,
    out_cot,
    w_node,
    w_agg,
    w_out,
    bias,
    gain,
    send_rows,
    blk_pairs,
    blk_count,
    blk_values,
):
    assert lax.axis_size("segment") == 2
    segment = lax.axis_index("segment")
    peers = lax.axis_size("dom")
    dom = lax.axis_index("dom")
    x = section_inputs[0]
    micro, rows, feat = x.shape
    targets = send_rows[0]
    slots, per_peer = targets.shape
    total = micro * rows
    pairs = blk_pairs[0]
    values = blk_values[0]
    halo_blocks = slots * per_peer // 128
    row_blocks = rows // 128
    blocks = row_blocks + halo_blocks
    wide = micro * feat
    flat_targets = targets.reshape(slots * per_peer, 1)
    w_n, w_a, w_o = w_node[0], w_agg[0], w_out[0]
    me = jnp.stack([segment, dom & 1, (dom >> 1) & 1, (dom >> 2) & 1]).astype(jnp.int32)
    matmul = 2 * total * feat * feat
    size = total * feat
    chunk = shape((micro * per_peer, feat), BF16)

    def moved(v, offset, src, dst):
        return lax.ppermute(
            v,
            ("dom", "segment"),
            [(2 * p + src, 2 * ((p + offset) % peers) + dst) for p in range(peers)],
        )

    def shifted(v, offset):
        return lax.ppermute(v, "dom", [(p, (p + offset) % peers) for p in range(peers)])

    def flipped(v, bit):
        return lax.ppermute(v, "dom", [(p, p ^ (1 << bit)) for p in range(peers)])

    outgoing = call(
        gather_kernel, [chunk] * slots, [], matmul // 8, 2 * size,
        targets.reshape(slots, per_peer, 1), x,
    )
    halos = [shifted(v, o) for v, o in zip(outgoing, OFFSETS)]
    z = call(node_kernel, shape((total, feat), F32), [], matmul, 8 * size, x, w_n, bias)
    f_full, b_full = shape((total, feat), F32), shape((total, feat), BF16)
    s_sums = shape((EXTRA, feat), F32)
    scr_gm = pltpu.VMEM((row_blocks, 128, wide), BF16)
    scr_t = pltpu.VMEM((blocks, 128, wide), F32)
    first = call(
        first_kernel,
        [chunk] * slots
        + [f_full, f_full, f_full, shape((total, 128), F32), b_full, b_full, b_full, b_full, s_sums],
        [
            pltpu.VMEM((blocks, 128, wide), BF16),
            pltpu.VMEM((row_blocks, 128, wide), F32),
            scr_gm,
            scr_t,
        ],
        6 * matmul, 24 * size,
        pairs, blk_count, x, *halos, values, z, out_cot, w_n, w_a, w_o, gain,
    )
    to_return, (cpart1, dact, normed, inv_std, agg, hidden, gpn1, gpre1, sums1) = (
        first[:slots], first[slots:],
    )
    returned = [moved(v, -o, 1, 0) for v, o in zip(to_return, OFFSETS)]
    c_in = moved(cpart1, 0, 1, 0)
    second = call(
        second_kernel,
        [chunk] * slots + [f_full, b_full, b_full, b_full, s_sums],
        [scr_gm, scr_t],
        4 * matmul, 24 * size,
        me, pairs, blk_count, flat_targets, *returned, c_in, values, dact, normed, inv_std, gpn1, gpre1,
        sums1, w_n, w_a, w_o, gain,
    )
    to_return, (cpart0, g_low, gpn, gpre, sums) = second[:slots], second[slots:]
    returned = [moved(v, -o, 0, 0) for v, o in zip(to_return, OFFSETS)]
    other = moved(g_low, 0, 0, 1)
    share = feat // peers
    if peers == 8:
        half = share // 2
        na, nb = share + half, share + half + EXTRA

        def parts(n):
            return [
                shape((n, na, feat), F32), shape((n, nb, feat), F32),
                shape((n, na, feat), BF16), shape((n, nb, feat), BF16),
            ]

        keep_a, keep_b, send_a, send_b = call(
            weight_kernel, parts(4), [pltpu.VMEM((8, share, feat), F32)] * 3,
            3 * matmul, 12 * size, me, x, agg, hidden, gpn, gpre, sums,
        )
        recv_a, recv_b = flipped(send_a, 0), flipped(send_b, 1)
        keep_a, keep_b, send_a, send_b = call(
            functools.partial(halve_kernel, ((0, 2), (0, 1))), parts(2), [], size, 8 * size,
            me, keep_a, keep_b, recv_a, recv_b,
        )
        recv_a, recv_b = flipped(send_a, 1), flipped(send_b, 0)
        keep_a, keep_b, send_a, send_b = call(
            functools.partial(halve_kernel, ((0, 3), (0, 3))), parts(1), [], size, 4 * size,
            me, keep_a, keep_b, recv_a, recv_b,
        )
        recv_a, recv_b = flipped(send_a, 2), flipped(send_b, 2)
        part = shape((share, feat), F32)
        grad_node, grad_agg, grad_out, sums = call(
            last_kernel, [part, part, part, s_sums], [], size, 2 * size,
            keep_a, keep_b, recv_a, recv_b,
        )
    else:
        square = shape((feat, feat), F32)
        full = call(
            whole_kernel, [square] * 3, [], 3 * matmul, 12 * size, x, agg, hidden, gpn, gpre
        )
        grad_node, grad_agg, grad_out = [
            lax.psum_scatter(v, "dom", scatter_dimension=0, tiled=True) for v in full
        ]
        sums = lax.psum(sums, "dom")
    cot = call(
        cot_kernel, shape((micro, rows, feat), BF16), [], matmul // 4, 4 * size,
        me, flat_targets, *returned, cpart0, other,
    )
    return (
        cot[None],
        grad_node[None],
        grad_agg[None],
        grad_out[None],
        sums[0:1],
        sums[1:2],
    )


def solution(mesh):
    placed = (
        P("segment", None, ("grp", "dom"), None),
        P(None, ("grp", "dom"), None),
        P("segment", None, None),
        P("segment", None, None),
        P("segment", None, None),
        P("segment", None),
        P("segment", None),
        P("dom", None, None),
        P("dom", None, None),
        P("dom"),
        P("dom", None, None, None),
    )
    return jax.shard_map(
        body,
        mesh=mesh,
        in_specs=placed,
        out_specs=(
            P("segment", None, ("grp", "dom"), None),
            P("segment", ("grp", "dom"), None),
            P("segment", ("grp", "dom"), None),
            P("segment", ("grp", "dom"), None),
            P("segment", "grp"),
            P("segment", "grp"),
        ),
        check_vma=False,
    )
```

time: 336 us -> 87.5 us (0.26)
  waiting for transfers between devices: 117 us -> 22.2 us
  local copies, waits for them, and re-layouts: 61.1 us -> 6.53 us
  matrix products: 44.5 us -> 0 us
  other arithmetic: 27.6 us -> 0.08 us
  blocking collectives: 25.3 us -> 0 us
  Pallas kernels: 0 us -> 21.7 us
  between operations: 15.6 us -> 1.58 us
  starting transfers between devices: 43.9 us -> 34.7 us
    psum x1 -> x0, waiting for transfers between devices: 87.6 us -> none  [body(): lax.psum((full_node, full_agg, full_out, bias_total, gain_total), 'dom')]
    dot_general x33 -> x0, matrix products: 44.5 us -> none  [the longest x3 8.17 us: aggregate(): summed = jnp.einsum('bk,kid->bid', onehot, products, precision=PRECISE)]
    psum x1 -> x0, blocking collectives: 25.3 us -> none  [body(): lax.psum((full_node, full_agg, full_out, bias_total, gain_total), 'dom')]
    pallas_call x0 -> x9, Pallas kernels: none -> 21.7 us  [call(): pl.pallas_call(kernel, out_shape=outs, in_specs=specs, out_specs=jax.tree...]
    dot_general x9 -> x0, local copies, waits for them, and re-layouts: 19.8 us -> none  [the longest x3 9.2 us: spread(): jnp.einsum('kij,kid->kjd', values, picked, preferred_element_type=jnp.flo...]
    gather x18 -> x0, local copies, waits for them, and re-layouts: 15.7 us -> none  [the longest x12 9.37 us: fetch_halo(): outgoing = x_rows[targets[slot_num]]]
    ppermute x26 -> x20, starting transfers between devices: 43.8 us -> 34.7 us  [the longest x10 20.2 us: moved(): lax.ppermute(v, ('dom', 'segment'), [(2 * p + src, 2 * ((p + offset) % pe...]
    scatter-add x3 -> x0, other arithmetic: 8.25 us -> none  [body(): grad_x = grad_x.at[flat_targets].add(returned.astype(jnp.float32))]
  transfers between devices with their start and end apart: 27 -> 20, of which waited for: 9 -> 8; matrix products, arithmetic and copies ran while one was open for 23% -> 0% of each run, Pallas kernels for 0% -> 4%
where the time goes in v1:
time: 87.5 us; the launch traced here: 86.8 us
  starting transfers between devices  34.7 us (40%)
  waiting for transfers between devices  22.2 us (25%)
  Pallas kernels  21.7 us (25%)
  local copies, waits for them, and re-layouts  6.53 us (7%)
  between operations  1.58 us (2%)
    pallas_call x9, Pallas kernels, call(): pl.pallas_call(kernel, out_shape=outs, in_specs=specs, out_specs=jax.tree...  21.7 us
    ppermute x10, starting transfers between devices, moved(): lax.ppermute(v, ('dom', 'segment'), [(2 * p + src, 2 * ((p + offset) % pe...  20.2 us
    ppermute x10, waiting for transfers between devices, moved(): lax.ppermute(v, ('dom', 'segment'), [(2 * p + src, 2 * ((p + offset) % pe...  13.3 us
    ppermute x4, starting transfers between devices, shifted(): lax.ppermute(v, 'dom', [(p, (p + offset) % peers) for p in range(peers)])  9.9 us
    ppermute x6, waiting for transfers between devices, flipped(): return lax.ppermute(v, 'dom', [(p, p ^ 1 << bit) for p in range(peers)])  8.63 us
    unnamed x34, local copies, waits for them, and re-layouts  5.01 us
    ppermute x6, starting transfers between devices, flipped(): return lax.ppermute(v, 'dom', [(p, p ^ 1 << bit) for p in range(peers)])  4.63 us
  transfers between devices with their start and end apart: 20, of which 8 were waited for; matrix products, arithmetic and copies ran while one was open for 0% of the time, Pallas kernels for 4%

profile of v1, /device:TPU:0, one launch (start us, length us, event | category | flops | bytes accessed | tf_op | source)
XLA Modules:
  0.0 86.8 jit_solution(13240545715334908661)
XLA Ops:
  0.6 0.8 copy.17.targets_ref
  1.5 1.0 %copy-done.1 = bf16[1,2,256,512]{3,2,1,0:T(8,128)(2,1)S(1)} copy-done((bf16[1,2,256,512]{3,2,1,0:T(8,128)(2,1)S(1)}, bf16[1,2,256,512]{3,2,1,0:T(8,128)(2,1)}, u32[]{:S(2)}) %copy-start.1) | copy-done | bytes 524312
  2.5 0.5 shard_map.154
  3.0 3.0 %collective-permute-start = (bf16[64,512]{1,0:T(8,128)(2,1)S(1)}, bf16[64,512]{1,0:T(8,128)(2,1)S(1)}, u32[]{:S(2)}, u32[]{:S(2)}) collective-permute-start(bf16[64,512]{1,0:T(8,128)(2,1)S(1)} %get-tuple-element.48), channel_id=1, source_target_pairs={{0,2},{2,4},{4,6},{6,8},{8,10},{10,12},{12,14},{14,0},{1,3},{3,5},... | collective-permute-start | bytes 196616 | tf_op jit(solution)/shard_map/ppermute | solution.py:348
  6.0 3.1 %collective-permute-start.1 = (bf16[64,512]{1,0:T(8,128)(2,1)S(1)}, bf16[64,512]{1,0:T(8,128)(2,1)S(1)}, u32[]{:S(2)}, u32[]{:S(2)}) collective-permute-start(bf16[64,512]{1,0:T(8,128)(2,1)S(1)} %get-tuple-element.49), channel_id=1, source_target_pairs={{0,14},{2,0},{4,2},{6,4},{8,6},{10,8},{12,10},{14,12},{1,15},{3,1}... | collective-permute-start | bytes 196616 | tf_op jit(solution)/shard_map/ppermute | solution.py:348
  9.1 3.8 %collective-permute-start.3 = (bf16[64,512]{1,0:T(8,128)(2,1)S(1)}, bf16[64,512]{1,0:T(8,128)(2,1)S(1)}, u32[]{:S(2)}, u32[]{:S(2)}) collective-permute-start(bf16[64,512]{1,0:T(8,128)(2,1)S(1)} %get-tuple-element.51), channel_id=1, source_target_pairs={{0,12},{2,14},{4,0},{6,2},{8,4},{10,6},{12,8},{14,10},{1,13},{3,15... | collective-permute-start | bytes 196616 | tf_op jit(solution)/shard_map/ppermute | solution.py:348
  13.6 0.0 copy-start.6
  13.6 0.4 shard_map.155.z_ref
  14.1 1.0 %copy-done.3 = f32[512,512]{1,0:T(8,128)} copy-done((f32[512,512]{1,0:T(8,128)}, f32[512,512]{1,0:T(8,128)S(1)}, u32[]{:S(2)}) %copy-start.3) | copy-done | bytes 1048600
  15.1 0.3 collective-permute-done.2.h2
  15.4 0.6 copy-done.9
  16.1 0.0 copy-done.10
  16.1 8.7 %shard_map.156 = (bf16[64,512]{1,0:T(8,128)(2,1)S(1)}, bf16[64,512]{1,0:T(8,128)(2,1)S(1)}, bf16[64,512]{1,0:T(8,128)(2,1)S(1)}, bf16[64,512]{1,0:T(8,128)(2,1)S...) custom-call(s32[2,7]{1,0:T(2,128)S(1)} %bitcast.28, ...), custom_call_target="tpu_custom_call" | custom-call | flops 1610612736 | bytes 6291456 | tf_op jit(solution)/shard_map/pallas_call | solution.py:29
  24.8 0.8 copy-done.12
  25.6 0.8 copy-done.14
  26.4 1.3 %collective-permute-start.8 = (f32[512,512]{1,0:T(8,128)}, f32[512,512]{1,0:T(8,128)}, u32[]{:S(2)}, u32[]{:S(2)}) collective-permute-start(f32[512,512]{1,0:T(8,128)} %get-tuple-element.56), channel_id=1, source_target_pairs={{1,0},{3,2},{5,4},{7,6},{9,8},{11,10},{13,12},{15,14},{17,16},{19,... | collective-permute-start | bytes 3145736 | tf_op jit(solution)/shard_map/ppermute | solution.py:341
  27.7 0.7 copy-done.16
  28.4 0.1 reshape_squeeze.8.targets_ref
  28.5 1.3 %collective-permute-start.4 = (bf16[64,512]{1,0:T(8,128)(2,1)S(1)}, bf16[64,512]{1,0:T(8,128)(2,1)S(1)}, u32[]{:S(2)}, u32[]{:S(2)}) collective-permute-start(bf16[64,512]{1,0:T(8,128)(2,1)S(1)} %get-tuple-element.52), channel_id=1, source_target_pairs={{1,14},{3,0},{5,2},{7,4},{9,6},{11,8},{13,10},{15,12},{17,30},{19,... | collective-permute-start | bytes 196616 | tf_op jit(solution)/shard_map/ppermute | solution.py:341
  29.8 1.3 %collective-permute-start.5 = (bf16[64,512]{1,0:T(8,128)(2,1)S(1)}, bf16[64,512]{1,0:T(8,128)(2,1)S(1)}, u32[]{:S(2)}, u32[]{:S(2)}) collective-permute-start(bf16[64,512]{1,0:T(8,128)(2,1)S(1)} %get-tuple-element.53), channel_id=1, source_target_pairs={{1,2},{3,4},{5,6},{7,8},{9,10},{11,12},{13,14},{15,0},{17,18},{19,... | collective-permute-start | bytes 196616 | tf_op jit(solution)/shard_map/ppermute | solution.py:341
  31.1 1.3 %collective-permute-start.6 = (bf16[64,512]{1,0:T(8,128)(2,1)S(1)}, bf16[64,512]{1,0:T(8,128)(2,1)S(1)}, u32[]{:S(2)}, u32[]{:S(2)}) collective-permute-start(bf16[64,512]{1,0:T(8,128)(2,1)S(1)} %get-tuple-element.54), channel_id=1, source_target_pairs={{1,12},{3,14},{5,0},{7,2},{9,4},{11,6},{13,8},{15,10},{17,28},{19,... | collective-permute-start | bytes 196616 | tf_op jit(solution)/shard_map/ppermute | solution.py:341
  32.4 1.3 %collective-permute-start.7 = (bf16[64,512]{1,0:T(8,128)(2,1)S(1)}, bf16[64,512]{1,0:T(8,128)(2,1)S(1)}, u32[]{:S(2)}, u32[]{:S(2)}) collective-permute-start(bf16[64,512]{1,0:T(8,128)(2,1)S(1)} %get-tuple-element.55), channel_id=1, source_target_pairs={{1,4},{3,6},{5,8},{7,10},{9,12},{11,14},{13,0},{15,2},{17,20},{19,... | collective-permute-start | bytes 196616 | tf_op jit(solution)/shard_map/ppermute | solution.py:341
  33.7 0.1 pad_add_fusion.me_ref
  33.8 0.3 collective-permute-done.4.r0
  34.1 4.8 %collective-permute-done.5.r1 = bf16[64,512]{1,0:T(8,128)(2,1)S(1)} collective-permute-done((bf16[64,512]{1,0:T(8,128)(2,1)S(1)}, bf16[64,512]{1,0:T(8,128)(2,1)S(1)}, u32[]{:S(2)}, u32[]{:S(2)}) %collective-permute-start.5) | collective-permute-done | bytes 65568 | tf_op jit(solution)/shard_map/ppermute | solution.py:341
  38.9 2.5 %collective-permute-done.7.r3 = bf16[64,512]{1,0:T(8,128)(2,1)S(1)} collective-permute-done((bf16[64,512]{1,0:T(8,128)(2,1)S(1)}, bf16[64,512]{1,0:T(8,128)(2,1)S(1)}, u32[]{:S(2)}, u32[]{:S(2)}) %collective-permute-start.7) | collective-permute-done | bytes 65568 | tf_op jit(solution)/shard_map/ppermute | solution.py:341
  41.4 6.6 %shard_map.157 = (bf16[64,512]{1,0:T(8,128)(2,1)S(1)}, bf16[64,512]{1,0:T(8,128)(2,1)S(1)}, bf16[64,512]{1,0:T(8,128)(2,1)S(1)}, bf16[64,512]{1,0:T(8,128)(2,1)S...) custom-call(s32[4]{0:T(128)S(1)} %pad_add_fusion.me_ref, ...), custom_call_target="tpu_custom_call" | custom-call | flops 1073741824 | bytes 6291456 | tf_op jit(solution)/shard_map/pallas_call | solution.py:29
  48.0 1.6 %shard_map.159 = (f32[4,96,512]{2,1,0:T(8,128)S(1)}, f32[4,104,512]{2,1,0:T(8,128)S(1)}, bf16[4,96,512]{2,1,0:T(8,128)(2,1)S(1)}, bf16[4,104,512]{2,1,0:T(8,128)(2,1)S(1)}) custom-call(s32[4]{0:T(128)S(1)} %pad_add_fusion.me_ref, bf16[2,256,512]{2,1,0:T(8,128)(2,1)S(1)} %bitcast.21, bf16[512,512]{1,0:T(8,128)(2,1)S(1)} %copy-done.13, ...), custom_call_target="tpu_custom_call" | custom-call | flops 805306368 | bytes 3145728 | tf_op jit(solution)/shard_map/pallas_call | solution.py:29
  49.7 0.2 collective-permute-start.15
  49.9 0.0 collective-permute-start.14
  49.9 1.3 %collective-permute-start.13 = (bf16[512,512]{1,0:T(8,128)(2,1)S(1)}, bf16[512,512]{1,0:T(8,128)(2,1)S(1)}, u32[]{:S(2)}, u32[]{:S(2)}) collective-permute-start(bf16[512,512]{1,0:T(8,128)(2,1)S(1)} %get-tuple-element.68), channel_id=1, source_target_pairs={{0,1},{2,3},{4,5},{6,7},{8,9},{10,11},{12,13},{14,15},{16,17},{18,... | collective-permute-start | bytes 1572872 | tf_op jit(solution)/shard_map/ppermute | solution.py:341
  51.2 8.0 %collective-permute-done.14.recv_a = bf16[4,96,512]{2,1,0:T(8,128)(2,1)S(1)} collective-permute-done((bf16[4,96,512]{2,1,0:T(8,128)(2,1)S(1)}, bf16[4,96,512]{2,1,0:T(8,128)(2,1)S(1)}, u32[]{:S(2)}, u32[]{:S(2)}) %collective-permute-start.14) | collective-permute-done | bytes 393248 | tf_op jit(solution)/shard_map/ppermute | solution.py:351
  59.2 0.6 collective-permute-done.15.recv_b
  59.9 0.7 shard_map.160
  60.6 0.1 collective-permute-start.17
  60.6 1.3 %collective-permute-start.16 = (bf16[2,96,512]{2,1,0:T(8,128)(2,1)S(1)}, bf16[2,96,512]{2,1,0:T(8,128)(2,1)S(1)}, u32[]{:S(2)}, u32[]{:S(2)}) collective-permute-start(bf16[2,96,512]{2,1,0:T(8,128)(2,1)S(1)} %get-tuple-element.80), channel_id=1, source_target_pairs={{0,4},{2,6},{4,0},{6,2},{8,12},{10,14},{12,8},{14,10},{1,5},{3,7},... | collective-permute-start | bytes 589832 | tf_op jit(solution)/shard_map/ppermute | solution.py:351
  62.0 4.7 %collective-permute-start.9 = (bf16[64,512]{1,0:T(8,128)(2,1)S(1)}, bf16[64,512]{1,0:T(8,128)(2,1)S(1)}, u32[]{:S(2)}, u32[]{:S(2)}) collective-permute-start(bf16[64,512]{1,0:T(8,128)(2,1)S(1)} %get-tuple-element.63), channel_id=1, source_target_pairs={{0,14},{2,0},{4,2},{6,4},{8,6},{10,8},{12,10},{14,12},{16,30},{18,... | collective-permute-start | bytes 196616 | tf_op jit(solution)/shard_map/ppermute | solution.py:341
  66.7 1.9 %collective-permute-start.10 = (bf16[64,512]{1,0:T(8,128)(2,1)S(1)}, bf16[64,512]{1,0:T(8,128)(2,1)S(1)}, u32[]{:S(2)}, u32[]{:S(2)}) collective-permute-start(bf16[64,512]{1,0:T(8,128)(2,1)S(1)} %get-tuple-element.64), channel_id=1, source_target_pairs={{0,2},{2,4},{4,6},{6,8},{8,10},{10,12},{12,14},{14,0},{16,18},{18,... | collective-permute-start | bytes 196616 | tf_op jit(solution)/shard_map/ppermute | solution.py:341
  68.6 0.6 shard_map.161
  69.2 1.3 %collective-permute-start.19 = (bf16[1,104,512]{2,1,0:T(8,128)(2,1)S(1)}, bf16[1,104,512]{2,1,0:T(8,128)(2,1)S(1)}, u32[]{:S(2)}, u32[]{:S(2)}) collective-permute-start(bf16[1,104,512]{2,1,0:T(8,128)(2,1)S(1)} %get-tuple-element.85), channel_id=1, source_target_pairs={{0,8},{2,10},{4,12},{6,14},{8,0},{10,2},{12,4},{14,6},{1,9},{3,11}... | collective-permute-start | bytes 319496 | tf_op jit(solution)/shard_map/ppermute | solution.py:351
  70.5 1.7 %collective-permute-start.18 = (bf16[1,96,512]{2,1,0:T(8,128)(2,1)S(1)}, bf16[1,96,512]{2,1,0:T(8,128)(2,1)S(1)}, u32[]{:S(2)}, u32[]{:S(2)}) collective-permute-start(bf16[1,96,512]{2,1,0:T(8,128)(2,1)S(1)} %get-tuple-element.84), channel_id=1, source_target_pairs={{0,8},{2,10},{4,12},{6,14},{8,0},{10,2},{12,4},{14,6},{1,9},{3,11}... | collective-permute-start | bytes 294920 | tf_op jit(solution)/shard_map/ppermute | solution.py:351
  72.2 3.5 %collective-permute-start.11 = (bf16[64,512]{1,0:T(8,128)(2,1)S(1)}, bf16[64,512]{1,0:T(8,128)(2,1)S(1)}, u32[]{:S(2)}, u32[]{:S(2)}) collective-permute-start(bf16[64,512]{1,0:T(8,128)(2,1)S(1)} %get-tuple-element.65), channel_id=1, source_target_pairs={{0,12},{2,14},{4,0},{6,2},{8,4},{10,6},{12,8},{14,10},{16,28},{18,... | collective-permute-start | bytes 196616 | tf_op jit(solution)/shard_map/ppermute | solution.py:341
  75.8 2.3 %collective-permute-start.12 = (bf16[64,512]{1,0:T(8,128)(2,1)S(1)}, bf16[64,512]{1,0:T(8,128)(2,1)S(1)}, u32[]{:S(2)}, u32[]{:S(2)}) collective-permute-start(bf16[64,512]{1,0:T(8,128)(2,1)S(1)} %get-tuple-element.66), channel_id=1, source_target_pairs={{0,4},{2,6},{4,8},{6,10},{8,12},{10,14},{12,0},{14,2},{16,20},{18,... | collective-permute-start | bytes 196616 | tf_op jit(solution)/shard_map/ppermute | solution.py:341
  78.1 1.1 %collective-permute-done.11.r2 = bf16[64,512]{1,0:T(8,128)(2,1)S(1)} collective-permute-done((bf16[64,512]{1,0:T(8,128)(2,1)S(1)}, bf16[64,512]{1,0:T(8,128)(2,1)S(1)}, u32[]{:S(2)}, u32[]{:S(2)}) %collective-permute-start.11) | collective-permute-done | bytes 65568 | tf_op jit(solution)/shard_map/ppermute | solution.py:341
  79.2 4.6 %collective-permute-done.12.r3 = bf16[64,512]{1,0:T(8,128)(2,1)S(1)} collective-permute-done((bf16[64,512]{1,0:T(8,128)(2,1)S(1)}, bf16[64,512]{1,0:T(8,128)(2,1)S(1)}, u32[]{:S(2)}, u32[]{:S(2)}) %collective-permute-start.12) | collective-permute-done | bytes 65568 | tf_op jit(solution)/shard_map/ppermute | solution.py:341
  83.7 1.7 %shard_map.158 = bf16[2,256,512]{2,1,0:T(8,128)(2,1)} custom-call(s32[4]{0:T(128)S(1)} %pad_add_fusion.me_ref, s32[128,1]{1,0:T(8,128)S(1)} %reshape_squeeze.8.targets_ref, bf16[64,512]{1,0:T(8,128)(2,1)S(1)} %collective-permute-done.9.r0, bf16[64,512]{1,0:T(8,128)(2,1)S(1)} %collective-permute-done.10.r1, bf16[64,512]{1,0:T(8,128)(2,1)S(1)} %collective-permute-done.11.r2, ...), custom_call_target="tpu_custom_call" | custom-call | flops 67108864 | bytes 1048576 | tf_op jit(solution)/shard_map/pallas_call | solution.py:29
  85.5 0.8 shard_map.162
  86.3 0.6 fusion
  (39 shorter events, 0.1 us)
Async XLA Ops:
  0.6 12.9 %copy-start = (bf16[1,512,512]{2,1,0:T(8,128)(2,1)S(1)}, bf16[1,512,512]{2,1,0:T(8,128)(2,1)}, u32[]{:S(2)}) copy-start(bf16[1,512,512]{2,1,0:T(8,128)(2,1)} %param.13) | copy-start | bytes 1572868
  1.5 1.0 %copy-start.1 = (bf16[1,2,256,512]{3,2,1,0:T(8,128)(2,1)S(1)}, bf16[1,2,256,512]{3,2,1,0:T(8,128)(2,1)}, u32[]{:S(2)}) copy-start(bf16[1,2,256,512]{3,2,1,0:T(8,128)(2,1)} %param.11) | copy-start | bytes 1572868
  3.0 12.1 %collective-permute-start = (bf16[64,512]{1,0:T(8,128)(2,1)S(1)}, bf16[64,512]{1,0:T(8,128)(2,1)S(1)}, u32[]{:S(2)}, u32[]{:S(2)}) collective-permute-start(bf16[64,512]{1,0:T(8,128)(2,1)S(1)} %get-tuple-element.48), channel_id=1, source_target_pairs={{0,2},{2,4},{4,6},{6,8},{8,10},{10,12},{12,14},{14,0},{1,3},{3,5},... | collective-permute-start | bytes 196616 | tf_op jit(solution)/shard_map/ppermute | solution.py:348
  6.0 9.1 %collective-permute-start.1 = (bf16[64,512]{1,0:T(8,128)(2,1)S(1)}, bf16[64,512]{1,0:T(8,128)(2,1)S(1)}, u32[]{:S(2)}, u32[]{:S(2)}) collective-permute-start(bf16[64,512]{1,0:T(8,128)(2,1)S(1)} %get-tuple-element.49), channel_id=1, source_target_pairs={{0,14},{2,0},{4,2},{6,4},{8,6},{10,8},{12,10},{14,12},{1,15},{3,1}... | collective-permute-start | bytes 196616 | tf_op jit(solution)/shard_map/ppermute | solution.py:348
  9.1 6.3 %collective-permute-start.2 = (bf16[64,512]{1,0:T(8,128)(2,1)S(1)}, bf16[64,512]{1,0:T(8,128)(2,1)S(1)}, u32[]{:S(2)}, u32[]{:S(2)}) collective-permute-start(bf16[64,512]{1,0:T(8,128)(2,1)S(1)} %get-tuple-element.50), channel_id=1, source_target_pairs={{0,4},{2,6},{4,8},{6,10},{8,12},{10,14},{12,0},{14,2},{1,5},{3,7},... | collective-permute-start | bytes 196616 | tf_op jit(solution)/shard_map/ppermute | solution.py:348
  9.1 4.5 %copy-start.8 = (bf16[1,512]{1,0:T(2,128)(2,1)S(1)}, bf16[1,512]{1,0:T(2,128)(2,1)}, u32[]{:S(2)}) copy-start(bf16[1,512]{1,0:T(2,128)(2,1)} %bias_ref.1) | copy-start | bytes 3076
  9.1 6.3 %collective-permute-start.3 = (bf16[64,512]{1,0:T(8,128)(2,1)S(1)}, bf16[64,512]{1,0:T(8,128)(2,1)S(1)}, u32[]{:S(2)}, u32[]{:S(2)}) collective-permute-start(bf16[64,512]{1,0:T(8,128)(2,1)S(1)} %get-tuple-element.51), channel_id=1, source_target_pairs={{0,12},{2,14},{4,0},{6,2},{8,4},{10,6},{12,8},{14,10},{1,13},{3,15... | collective-permute-start | bytes 196616 | tf_op jit(solution)/shard_map/ppermute | solution.py:348
  13.6 1.8 %copy-start.5 = (bf16[1,512,512]{2,1,0:T(8,128)(2,1)S(1)}, bf16[1,512,512]{2,1,0:T(8,128)(2,1)}, u32[]{:S(2)}) copy-start(bf16[1,512,512]{2,1,0:T(8,128)(2,1)} %param.14) | copy-start | bytes 1572868
  13.6 1.8 %copy-start.6 = (bf16[1,512,512]{2,1,0:T(8,128)(2,1)S(1)}, bf16[1,512,512]{2,1,0:T(8,128)(2,1)}, u32[]{:S(2)}) copy-start(bf16[1,512,512]{2,1,0:T(8,128)(2,1)} %param.15) | copy-start | bytes 1572868
  13.6 1.8 %copy-start.7 = (bf16[1,7,128,128]{3,2,1,0:T(8,128)(2,1)S(1)}, bf16[1,7,128,128]{3,2,1,0:T(8,128)(2,1)}, u32[]{:S(2)}) copy-start(bf16[1,7,128,128]{3,2,1,0:T(8,128)(2,1)} %param.21) | copy-start | bytes 688132
  13.6 1.8 %copy-start.11 = (bf16[2,256,512]{2,1,0:T(8,128)(2,1)S(1)}, bf16[2,256,512]{2,1,0:T(8,128)(2,1)}, u32[]{:S(2)}) copy-start(bf16[2,256,512]{2,1,0:T(8,128)(2,1)} %g_ref.1) | copy-start | bytes 1572868
  14.1 1.0 %copy-start.3 = (f32[512,512]{1,0:T(8,128)}, f32[512,512]{1,0:T(8,128)S(1)}, u32[]{:S(2)}) copy-start(f32[512,512]{1,0:T(8,128)S(1)} %shard_map.155.z_ref) | copy-start | bytes 3145732
  15.4 0.7 copy-start.9
  15.4 0.7 copy-start.10
  24.8 0.8 copy-start.12
  25.6 0.8 copy-start.14
  26.4 15.0 %collective-permute-start.8 = (f32[512,512]{1,0:T(8,128)}, f32[512,512]{1,0:T(8,128)}, u32[]{:S(2)}, u32[]{:S(2)}) collective-permute-start(f32[512,512]{1,0:T(8,128)} %get-tuple-element.56), channel_id=1, source_target_pairs={{1,0},{3,2},{5,4},{7,6},{9,8},{11,10},{13,12},{15,14},{17,16},{19,... | collective-permute-start | bytes 3145736 | tf_op jit(solution)/shard_map/ppermute | solution.py:341
  27.7 0.7 copy-start.16
  28.5 5.6 %collective-permute-start.4 = (bf16[64,512]{1,0:T(8,128)(2,1)S(1)}, bf16[64,512]{1,0:T(8,128)(2,1)S(1)}, u32[]{:S(2)}, u32[]{:S(2)}) collective-permute-start(bf16[64,512]{1,0:T(8,128)(2,1)S(1)} %get-tuple-element.52), channel_id=1, source_target_pairs={{1,14},{3,0},{5,2},{7,4},{9,6},{11,8},{13,10},{15,12},{17,30},{19,... | collective-permute-start | bytes 196616 | tf_op jit(solution)/shard_map/ppermute | solution.py:341
  29.8 9.1 %collective-permute-start.5 = (bf16[64,512]{1,0:T(8,128)(2,1)S(1)}, bf16[64,512]{1,0:T(8,128)(2,1)S(1)}, u32[]{:S(2)}, u32[]{:S(2)}) collective-permute-start(bf16[64,512]{1,0:T(8,128)(2,1)S(1)} %get-tuple-element.53), channel_id=1, source_target_pairs={{1,2},{3,4},{5,6},{7,8},{9,10},{11,12},{13,14},{15,0},{17,18},{19,... | collective-permute-start | bytes 196616 | tf_op jit(solution)/shard_map/ppermute | solution.py:341
  31.1 7.8 %collective-permute-start.6 = (bf16[64,512]{1,0:T(8,128)(2,1)S(1)}, bf16[64,512]{1,0:T(8,128)(2,1)S(1)}, u32[]{:S(2)}, u32[]{:S(2)}) collective-permute-start(bf16[64,512]{1,0:T(8,128)(2,1)S(1)} %get-tuple-element.54), channel_id=1, source_target_pairs={{1,12},{3,14},{5,0},{7,2},{9,4},{11,6},{13,8},{15,10},{17,28},{19,... | collective-permute-start | bytes 196616 | tf_op jit(solution)/shard_map/ppermute | solution.py:341
  32.4 9.0 %collective-permute-start.7 = (bf16[64,512]{1,0:T(8,128)(2,1)S(1)}, bf16[64,512]{1,0:T(8,128)(2,1)S(1)}, u32[]{:S(2)}, u32[]{:S(2)}) collective-permute-start(bf16[64,512]{1,0:T(8,128)(2,1)S(1)} %get-tuple-element.55), channel_id=1, source_target_pairs={{1,4},{3,6},{5,8},{7,10},{9,12},{11,14},{13,0},{15,2},{17,20},{19,... | collective-permute-start | bytes 196616 | tf_op jit(solution)/shard_map/ppermute | solution.py:341
  41.4 6.6 %copy-start.2 = (bf16[1,2,256,512]{3,2,1,0:T(8,128)(2,1)S(1)}, bf16[1,2,256,512]{3,2,1,0:T(8,128)(2,1)}, u32[]{:S(2)}) copy-start(bf16[1,2,256,512]{3,2,1,0:T(8,128)(2,1)} %param.11) | copy-start | bytes 1572868
  41.4 6.6 %copy-start.13 = (bf16[512,512]{1,0:T(8,128)(2,1)S(1)}, bf16[512,512]{1,0:T(8,128)(2,1)}, u32[]{:S(2)}) copy-start(bf16[512,512]{1,0:T(8,128)(2,1)} %copy-done.12) | copy-start | bytes 1572868
  41.4 6.6 %copy-start.15 = (bf16[512,512]{1,0:T(8,128)(2,1)S(1)}, bf16[512,512]{1,0:T(8,128)(2,1)}, u32[]{:S(2)}) copy-start(bf16[512,512]{1,0:T(8,128)(2,1)} %copy-done.14) | copy-start | bytes 1572868
  49.7 10.2 %collective-permute-start.15 = (bf16[4,104,512]{2,1,0:T(8,128)(2,1)S(1)}, bf16[4,104,512]{2,1,0:T(8,128)(2,1)S(1)}, u32[]{:S(2)}, u32[]{:S(2)}) collective-permute-start(bf16[4,104,512]{2,1,0:T(8,128)(2,1)S(1)} %get-tuple-element.77), channel_id=1, source_target_pairs={{0,4},{2,6},{4,0},{6,2},{8,12},{10,14},{12,8},{14,10},{1,5},{3,7},... | collective-permute-start | bytes 1277960 | tf_op jit(solution)/shard_map/ppermute | solution.py:351
  49.9 9.3 %collective-permute-start.14 = (bf16[4,96,512]{2,1,0:T(8,128)(2,1)S(1)}, bf16[4,96,512]{2,1,0:T(8,128)(2,1)S(1)}, u32[]{:S(2)}, u32[]{:S(2)}) collective-permute-start(bf16[4,96,512]{2,1,0:T(8,128)(2,1)S(1)} %get-tuple-element.76), channel_id=1, source_target_pairs={{0,2},{2,0},{4,6},{6,4},{8,10},{10,8},{12,14},{14,12},{1,3},{3,1},... | collective-permute-start | bytes 1179656 | tf_op jit(solution)/shard_map/ppermute | solution.py:351
  49.9 33.8 %collective-permute-start.13 = (bf16[512,512]{1,0:T(8,128)(2,1)S(1)}, bf16[512,512]{1,0:T(8,128)(2,1)S(1)}, u32[]{:S(2)}, u32[]{:S(2)}) collective-permute-start(bf16[512,512]{1,0:T(8,128)(2,1)S(1)} %get-tuple-element.68), channel_id=1, source_target_pairs={{0,1},{2,3},{4,5},{6,7},{8,9},{10,11},{12,13},{14,15},{16,17},{18,... | collective-permute-start | bytes 1572872 | tf_op jit(solution)/shard_map/ppermute | solution.py:341
  60.6 23.2 %copy-start.4 = (f32[512,512]{1,0:T(8,128)S(1)}, f32[512,512]{1,0:T(8,128)}, u32[]{:S(2)}) copy-start(f32[512,512]{1,0:T(8,128)} %get-tuple-element.67.cpart_ref) | copy-start | bytes 3145732
  60.6 8.0 %collective-permute-start.17 = (bf16[2,104,512]{2,1,0:T(8,128)(2,1)S(1)}, bf16[2,104,512]{2,1,0:T(8,128)(2,1)S(1)}, u32[]{:S(2)}, u32[]{:S(2)}) collective-permute-start(bf16[2,104,512]{2,1,0:T(8,128)(2,1)S(1)} %get-tuple-element.81), channel_id=1, source_target_pairs={{0,2},{2,0},{4,6},{6,4},{8,10},{10,8},{12,14},{14,12},{1,3},{3,1},... | collective-permute-start | bytes 638984 | tf_op jit(solution)/shard_map/ppermute | solution.py:351
  60.6 8.0 %collective-permute-start.16 = (bf16[2,96,512]{2,1,0:T(8,128)(2,1)S(1)}, bf16[2,96,512]{2,1,0:T(8,128)(2,1)S(1)}, u32[]{:S(2)}, u32[]{:S(2)}) collective-permute-start(bf16[2,96,512]{2,1,0:T(8,128)(2,1)S(1)} %get-tuple-element.80), channel_id=1, source_target_pairs={{0,4},{2,6},{4,0},{6,2},{8,12},{10,14},{12,8},{14,10},{1,5},{3,7},... | collective-permute-start | bytes 589832 | tf_op jit(solution)/shard_map/ppermute | solution.py:351
  62.0 10.3 %collective-permute-start.9 = (bf16[64,512]{1,0:T(8,128)(2,1)S(1)}, bf16[64,512]{1,0:T(8,128)(2,1)S(1)}, u32[]{:S(2)}, u32[]{:S(2)}) collective-permute-start(bf16[64,512]{1,0:T(8,128)(2,1)S(1)} %get-tuple-element.63), channel_id=1, source_target_pairs={{0,14},{2,0},{4,2},{6,4},{8,6},{10,8},{12,10},{14,12},{16,30},{18,... | collective-permute-start | bytes 196616 | tf_op jit(solution)/shard_map/ppermute | solution.py:341
  66.7 9.1 %collective-permute-start.10 = (bf16[64,512]{1,0:T(8,128)(2,1)S(1)}, bf16[64,512]{1,0:T(8,128)(2,1)S(1)}, u32[]{:S(2)}, u32[]{:S(2)}) collective-permute-start(bf16[64,512]{1,0:T(8,128)(2,1)S(1)} %get-tuple-element.64), channel_id=1, source_target_pairs={{0,2},{2,4},{4,6},{6,8},{8,10},{10,12},{12,14},{14,0},{16,18},{18,... | collective-permute-start | bytes 196616 | tf_op jit(solution)/shard_map/ppermute | solution.py:341
  69.2 16.2 %collective-permute-start.19 = (bf16[1,104,512]{2,1,0:T(8,128)(2,1)S(1)}, bf16[1,104,512]{2,1,0:T(8,128)(2,1)S(1)}, u32[]{:S(2)}, u32[]{:S(2)}) collective-permute-start(bf16[1,104,512]{2,1,0:T(8,128)(2,1)S(1)} %get-tuple-element.85), channel_id=1, source_target_pairs={{0,8},{2,10},{4,12},{6,14},{8,0},{10,2},{12,4},{14,6},{1,9},{3,11}... | collective-permute-start | bytes 319496 | tf_op jit(solution)/shard_map/ppermute | solution.py:351
  70.5 15.0 %collective-permute-start.18 = (bf16[1,96,512]{2,1,0:T(8,128)(2,1)S(1)}, bf16[1,96,512]{2,1,0:T(8,128)(2,1)S(1)}, u32[]{:S(2)}, u32[]{:S(2)}) collective-permute-start(bf16[1,96,512]{2,1,0:T(8,128)(2,1)S(1)} %get-tuple-element.84), channel_id=1, source_target_pairs={{0,8},{2,10},{4,12},{6,14},{8,0},{10,2},{12,4},{14,6},{1,9},{3,11}... | collective-permute-start | bytes 294920 | tf_op jit(solution)/shard_map/ppermute | solution.py:351
  72.2 6.9 %collective-permute-start.11 = (bf16[64,512]{1,0:T(8,128)(2,1)S(1)}, bf16[64,512]{1,0:T(8,128)(2,1)S(1)}, u32[]{:S(2)}, u32[]{:S(2)}) collective-permute-start(bf16[64,512]{1,0:T(8,128)(2,1)S(1)} %get-tuple-element.65), channel_id=1, source_target_pairs={{0,12},{2,14},{4,0},{6,2},{8,4},{10,6},{12,8},{14,10},{16,28},{18,... | collective-permute-start | bytes 196616 | tf_op jit(solution)/shard_map/ppermute | solution.py:341
  75.8 8.0 %collective-permute-start.12 = (bf16[64,512]{1,0:T(8,128)(2,1)S(1)}, bf16[64,512]{1,0:T(8,128)(2,1)S(1)}, u32[]{:S(2)}, u32[]{:S(2)}) collective-permute-start(bf16[64,512]{1,0:T(8,128)(2,1)S(1)} %get-tuple-element.66), channel_id=1, source_target_pairs={{0,4},{2,6},{4,8},{6,10},{8,12},{10,14},{12,0},{14,2},{16,20},{18,... | collective-permute-start | bytes 196616 | tf_op jit(solution)/shard_map/ppermute | solution.py:341

commit v2 on v0

v2 whole, which is shorter than its diff:
```python
import functools

import jax
import jax.numpy as jnp
from jax import lax
from jax.experimental import pallas as pl
from jax.experimental.pallas import tpu as pltpu
from jax.sharding import PartitionSpec as P

EPSILON = 1e-05
F32 = jnp.float32
BF16 = jnp.bfloat16
VMEM = pl.BlockSpec(memory_space=pltpu.VMEM)
SMEM = pl.BlockSpec(memory_space=pltpu.SMEM)
PEERS = 4
EXTRA = 8
PIECE = 64


def nn_dot(a, b):
    return jnp.dot(a, b, preferred_element_type=F32)


def nt_dot(a, b):
    return lax.dot_general(a, b, (((1,), (1,)), ((), ())), preferred_element_type=F32)


def tn_dot(a, b):
    return lax.dot_general(a, b, (((0,), (0,)), ((), ())), preferred_element_type=F32)


def shape(dims, dtype):
    return jax.ShapeDtypeStruct(dims, dtype)


def call(kernel, outs, scratch, flops, byts, *args, scalars=0):
    return pl.pallas_call(
        kernel,
        out_shape=outs,
        in_specs=[SMEM] * scalars + [VMEM] * (len(args) - scalars),
        out_specs=jax.tree.map(lambda _: VMEM, outs),
        scratch_shapes=scratch,
        compiler_params=pltpu.CompilerParams(vmem_limit_bytes=24 * 1024 * 1024),
        cost_estimate=pl.CostEstimate(flops=flops, bytes_accessed=byts, transcendentals=0),
    )(*args)


def dom_bit(i):
    return (lax.axis_index("dom") >> i) & 1


def sent_slots():
    x, z = dom_bit(0), dom_bit(1)
    return x, 1 - x, 2 + z, 3 - z


def read_slots():
    x, z = dom_bit(0), dom_bit(1)
    return 1 - x, x, 3 - z, 2 + z


def target_onehot(targets_ref, rows):
    ids = jnp.concatenate([targets_ref[0, pl.ds(s, 1), :] for s in sent_slots()], 1)
    return (lax.broadcasted_iota(jnp.int32, (rows, ids.shape[1]), 0) == ids).astype(BF16)


def gather_kernel(targets_ref, x_ref, *outs):
    micro, rows, _ = x_ref.shape
    per_peer = outs[0].shape[0] // micro
    onehot = target_onehot(targets_ref, rows)
    for m in range(micro):
        picked = tn_dot(onehot, x_ref[m]).astype(BF16)
        for k, out in enumerate(outs):
            out[m * per_peer : (m + 1) * per_peer, :] = picked[k * per_peer : (k + 1) * per_peer]


def node_kernel(pairs_ref, count_ref, x_ref, values_ref, w_ref, bias_ref, z_ref, acc_ref, src_ref):
    micro, rows, feat = x_ref.shape
    row_blocks = rows // 128
    for m in range(micro):
        z_ref[m * rows : (m + 1) * rows, :] = nn_dot(x_ref[m], w_ref[...]) + bias_ref[
            ...
        ].astype(F32)
        for b in range(row_blocks):
            src_ref[b, :, m * feat : (m + 1) * feat] = x_ref[m, b * 128 : (b + 1) * 128, :]
    acc_ref[...] = jnp.zeros_like(acc_ref)
    for k in range(values_ref.shape[0]):
        src = pairs_ref[1, k]

        @pl.when((k < count_ref[0]) & (src < row_blocks))
        def _():
            acc_ref[pairs_ref[0, k]] += nn_dot(values_ref[k], src_ref[src])


def pieces(part):
    return [slice(r, r + PIECE) for r in range(part.start, part.stop, PIECE)]


def row_mean(v):
    return jnp.mean(v, axis=1, keepdims=True)


def norm_back(g, normed, inv_std, gain):
    e = g * gain
    return (inv_std * (e - row_mean(e) - normed * row_mean(e * normed))).astype(BF16)


def parts_of(total, micro):
    rows = total // micro
    return [slice(m * rows, (m + 1) * rows) for m in range(micro)]


def wide_blocks(part, m, feat):
    cols = slice(m * feat, (m + 1) * feat)
    return [
        (b, slice(part.start + b * 128, part.start + (b + 1) * 128), cols)
        for b in range((part.stop - part.start) // 128)
    ]


def halo_spread(pairs_ref, count_ref, values_ref, gm_ref, t_ref, row_blocks):
    t_ref[...] = jnp.zeros_like(t_ref)
    for k in range(values_ref.shape[0]):
        src = pairs_ref[1, k]

        @pl.when((k < count_ref[0]) & (src >= row_blocks))
        def _():
            t_ref[src - row_blocks] += tn_dot(values_ref[k], gm_ref[pairs_ref[0, k]])


def local_spread(pairs_ref, count_ref, values_ref, gm_ref, t_ref, row_blocks):
    t_ref[...] = jnp.zeros_like(t_ref)
    for k in range(values_ref.shape[0]):
        src = pairs_ref[1, k]

        @pl.when((k < count_ref[0]) & (src < row_blocks))
        def _():
            t_ref[src] += tn_dot(values_ref[k], gm_ref[pairs_ref[0, k]])


def put_halo_grads(t_ref, outs):
    feat = outs[0].shape[1]
    per_peer = outs[0].shape[0] // 2
    for slot, out in zip(read_slots(), outs):
        for m in range(2):
            at = pl.ds(pl.multiple_of(slot * per_peer, per_peer), per_peer)
            out[m * per_peer : (m + 1) * per_peer, :] = t_ref[
                0, at, m * feat : (m + 1) * feat
            ].astype(BF16)


def first_kernel(
    pairs_ref, count_ref, h0, h1, h2, h3, values_ref, z_ref, accin_ref, g_ref, w_agg_ref,
    w_out_ref, gain_ref,
    o0, o1, o2, o3, gm_ref, dact_ref, normed_ref, inv_ref, agg_ref, hidden_ref, gpn_ref,
    gpre_ref, sums_ref,
    src_ref, acc_ref, s0_ref, t_ref,
):
    micro, rows, feat = g_ref.shape
    row_blocks = rows // 128
    per_peer = h0.shape[0] // micro
    for slot, h in zip(read_slots(), (h0, h1, h2, h3)):
        for m in range(micro):
            at = pl.ds(pl.multiple_of(slot * per_peer, per_peer), per_peer)
            src_ref[0, at, m * feat : (m + 1) * feat] = h[m * per_peer : (m + 1) * per_peer, :]
    acc_ref[...] = jnp.zeros_like(acc_ref)
    for k in range(values_ref.shape[0]):
        src = pairs_ref[1, k]

        @pl.when((k < count_ref[0]) & (src >= row_blocks))
        def _():
            acc_ref[pairs_ref[0, k]] += nn_dot(values_ref[k], src_ref[src - row_blocks])

    gain = gain_ref[...].astype(F32)
    parts = parts_of(micro * rows, micro)
    for m, part in enumerate(parts):
        for b, at, cols in wide_blocks(part, m, feat):
            agg_ref[at, :] = (accin_ref[b, :, cols] + acc_ref[b, :, cols]).astype(BF16)
    for part in parts:
        s0_ref[part, :] = nn_dot(agg_ref[part, :], w_agg_ref[...])
    for part in parts:
        for at in pieces(part):
            preact = z_ref[at, :] + s0_ref[at, :]
            sig = 1.0 / (1.0 + jnp.exp(-preact))
            hidden_ref[at, :] = (preact * sig).astype(BF16)
            dact_ref[at, :] = sig * (1.0 + preact * (1.0 - sig))
    for part in parts:
        s0_ref[part, :] = nn_dot(hidden_ref[part, :], w_out_ref[...])
    gain_sum = jnp.zeros((1, feat), F32)
    for m, part in enumerate(parts):
        for at in pieces(part):
            output = s0_ref[at, :]
            centred = output - row_mean(output)
            inv_std = lax.rsqrt(row_mean(centred * centred) + EPSILON)
            normed = centred * inv_std
            normed_ref[at, :] = normed
            inv_ref[at, :] = jnp.broadcast_to(inv_std, (PIECE, 128))
            g = g_ref[m, at.start - part.start : at.stop - part.start, :].astype(F32)
            gpn_ref[at, :] = norm_back(g, normed, inv_std, gain)
            gain_sum += jnp.sum(g * normed, axis=0, keepdims=True)
    for part in parts:
        s0_ref[part, :] = nt_dot(gpn_ref[part, :], w_out_ref[...])
    bias_sum = jnp.zeros((1, feat), F32)
    for part in parts:
        for at in pieces(part):
            gpre = (s0_ref[at, :] * dact_ref[at, :]).astype(BF16)
            gpre_ref[at, :] = gpre
            bias_sum += jnp.sum(gpre.astype(F32), axis=0, keepdims=True)
    for m, part in enumerate(parts):
        gm = nt_dot(gpre_ref[part, :], w_agg_ref[...]).astype(BF16)
        for b, at, cols in wide_blocks(part, m, feat):
            gm_ref[b, :, cols] = gm[b * 128 : (b + 1) * 128]
    halo_spread(pairs_ref, count_ref, values_ref, gm_ref, t_ref, row_blocks)
    put_halo_grads(t_ref, (o0, o1, o2, o3))
    sums_ref[0:1, :] = bias_sum
    sums_ref[1:2, :] = gain_sum


def cpart_kernel(pairs_ref, count_ref, g_ref, gpre_ref, gm_ref, values_ref, w_node_ref, cpart_ref, t_ref):
    micro, rows, feat = g_ref.shape
    local_spread(pairs_ref, count_ref, values_ref, gm_ref, t_ref, rows // 128)
    for m, part in enumerate(parts_of(micro * rows, micro)):
        back = nt_dot(gpre_ref[part, :], w_node_ref[...])
        for b, at, cols in wide_blocks(part, m, feat):
            here = slice(b * 128, (b + 1) * 128)
            cpart_ref[at, :] = g_ref[m, here, :].astype(F32) + back[here] + t_ref[b, :, cols]


def order_of(bit, chunks):
    step = 1 << bit
    low = [d for d in range(chunks) if not d & step]
    mine = dom_bit(bit)
    return [d + mine * step for d in low] + [d + (1 - mine) * step for d in low]


def turn_kernel(chunks, x_ref, agg_ref, hidden_ref, la_ref, lb_ref, lc_ref, turned_ref):
    micro, rows, feat = x_ref.shape
    share = feat // chunks
    half = share // 2
    na = share + half

    def at(d, n, off=0):
        return pl.ds(pl.multiple_of(d * share + off, half), n)

    for m in range(micro):
        turned_ref[:, m * rows : (m + 1) * rows] = x_ref[m].T
    for i, d in enumerate(order_of(0, chunks)):
        la_ref[i * na : i * na + share, :] = turned_ref[at(d, share), :]
    turned_ref[...] = agg_ref[...].T
    for i, d in enumerate(order_of(0, chunks)):
        la_ref[i * na + share : (i + 1) * na, :] = turned_ref[at(d, half), :]
    for i, d in enumerate(order_of(1, chunks)):
        lb_ref[i * half : (i + 1) * half, :] = turned_ref[at(d, half, half), :]
    turned_ref[...] = hidden_ref[...].T
    for i, d in enumerate(order_of(1, chunks)):
        lc_ref[i * share : (i + 1) * share, :] = turned_ref[at(d, share), :]


def second_kernel(
    targets_ref, r0, r1, r2, r3, cin_ref, dact_ref, normed_ref, inv_ref, gpn1_ref, gpre1_ref,
    sums1_ref, w_out_ref, gain_ref, *rest,
):
    weights = len(rest) > 6
    if weights:
        la_ref, lb_ref, lc_ref = rest[:3]
        keep_a, keep_b, send_a, send_b = rest[3:7]
        rest = rest[7:]
    g_ref, gpn_ref, gpre_ref, sums_ref, onehot_ref, s0_ref = rest[-6:]
    total, feat = dact_ref.shape
    parts = parts_of(total, 2)
    rows = total // 2
    per_peer = r0.shape[0] // 2
    onehot_ref[...] = target_onehot(targets_ref, rows)
    gain = gain_ref[...].astype(F32)
    is_last = lax.axis_index("segment") == 1
    for m, part in enumerate(parts):
        ret = jnp.concatenate([r[m * per_peer : (m + 1) * per_peer, :] for r in (r0, r1, r2, r3)], 0)
        s0_ref[part, :] = nn_dot(onehot_ref[...], ret)
    gain_sum = jnp.zeros((1, feat), F32)
    for part in parts:
        for at in pieces(part):
            g16 = (cin_ref[at, :] + s0_ref[at, :]).astype(BF16)
            g_ref[at, :] = g16
            g = g16.astype(F32)
            normed = normed_ref[at, :]
            gpn = norm_back(g, normed, inv_ref[at, 0:1], gain)
            gpn_ref[at, :] = jnp.where(is_last, gpn1_ref[at, :], gpn)
            gain_sum += jnp.sum(g * normed, axis=0, keepdims=True)
    for part in parts:
        s0_ref[part, :] = nt_dot(gpn_ref[part, :], w_out_ref[...])
    bias_sum = jnp.zeros((1, feat), F32)
    for part in parts:
        for at in pieces(part):
            gpre = (s0_ref[at, :] * dact_ref[at, :]).astype(BF16)
            gpre = jnp.where(is_last, gpre1_ref[at, :], gpre)
            gpre_ref[at, :] = gpre
            bias_sum += jnp.sum(gpre.astype(F32), axis=0, keepdims=True)
    gain_sum = jnp.where(is_last, sums1_ref[1:2, :], gain_sum)
    sums = jnp.concatenate([bias_sum, gain_sum, jnp.zeros((EXTRA - 2, feat), F32)], 0)
    sums_ref[...] = sums
    if not weights:
        return
    n = keep_a.shape[0]
    na, nb = keep_a.shape[1], keep_b.shape[1]
    half = lb_ref.shape[0] // (2 * n)
    share = 2 * half
    mid = n * na
    keep_a[...] = nn_dot(la_ref[:mid, :], gpre_ref[...]).reshape(n, na, feat)
    send_a[...] = nn_dot(la_ref[mid:, :], gpre_ref[...]).astype(BF16)
    for base, fill in (
        (0, lambda i, lo, v: put(keep_b, i, lo, v)),
        (n, lambda i, lo, v: put_flat(send_b, nb, i, lo, v)),
    ):
        b = nn_dot(lb_ref[base * half : (base + n) * half, :], gpre_ref[...])
        c = nn_dot(lc_ref[base * share : (base + n) * share, :], gpn_ref[...])
        for i in range(n):
            fill(i, 0, b[i * half : (i + 1) * half])
            fill(i, half, c[i * share : (i + 1) * share])
            fill(i, half + share, sums)


def put(ref, i, lo, v):
    ref[i, lo : lo + v.shape[0], :] = v.astype(ref.dtype)


def put_flat(ref, n, i, lo, v):
    ref[i * n + lo : i * n + lo + v.shape[0], :] = v.astype(ref.dtype)


def tail_kernel(
    pairs_ref, count_ref, g_ref, gpre_ref, values_ref, w_node_ref, w_agg_ref, o0, o1, o2, o3, cpart_ref,
    gm_ref, t_ref, th_ref,
):
    total, feat = g_ref.shape
    row_blocks = total // 256
    parts = parts_of(total, 2)
    for m, part in enumerate(parts):
        gm = nt_dot(gpre_ref[part, :], w_agg_ref[...]).astype(BF16)
        for b, at, cols in wide_blocks(part, m, feat):
            gm_ref[b, :, cols] = gm[b * 128 : (b + 1) * 128]
    halo_spread(pairs_ref, count_ref, values_ref, gm_ref, th_ref, row_blocks)
    put_halo_grads(th_ref, (o0, o1, o2, o3))
    local_spread(pairs_ref, count_ref, values_ref, gm_ref, t_ref, row_blocks)
    for m, part in enumerate(parts):
        back = nt_dot(gpre_ref[part, :], w_node_ref[...])
        for b, at, cols in wide_blocks(part, m, feat):
            cpart_ref[at, :] = (
                g_ref[at, :].astype(F32) + back[b * 128 : (b + 1) * 128] + t_ref[b, :, cols]
            )


def halve_kernel(bits, riders, keep_a, keep_b, recv_a, recv_b, *rest):
    extra, (keep_a2, keep_b2, send_a2, send_b2) = rest[:riders], rest[riders:]
    jobs = (
        (bits[0], keep_a, recv_a, keep_a2, send_a2, extra[:1]),
        (bits[1], keep_b, recv_b, keep_b2, send_b2, extra[1:]),
    )
    for bit, keep, recv, keep2, send2, ride in jobs:
        n, rows, _ = keep2.shape
        mine = dom_bit(bit)
        for i in range(n):
            d, o = 2 * i + mine, 2 * i + 1 - mine
            at = pl.ds(pl.multiple_of(d * rows, 8), rows)
            keep2[i] = keep[d] + recv[at, :].astype(F32)
            at = pl.ds(pl.multiple_of(o * rows, 8), rows)
            send2[i * rows : (i + 1) * rows, :] = (keep[o] + recv[at, :].astype(F32)).astype(BF16)
        for r in ride:
            send2[n * rows :, :] = r[...]


def last_kernel(keep_a, keep_b, recv_a, recv_b, node_ref, agg_ref, out_ref, bias_ref, gain_ref):
    share = node_ref.shape[0]
    half = share // 2
    a = keep_a[0] + recv_a[...].astype(F32)
    b = keep_b[0] + recv_b[...].astype(F32)
    node_ref[...] = a[0:share]
    agg_ref[0:half, :] = a[share : share + half]
    agg_ref[half:share, :] = b[0:half]
    out_ref[...] = b[half : half + share]
    bias_ref[...] = b[half + share : half + share + 1]
    gain_ref[...] = b[half + share + 1 : half + share + 2]


def cot_kernel(skips, targets_ref, r0, r1, r2, r3, cpart_ref, other_ref, cot_ref):
    micro, rows, feat = cot_ref.shape
    is_last = lax.axis_index("segment") == 1

    @pl.when(is_last)
    def _():
        for m in range(micro):
            cot_ref[m] = other_ref[m * rows : (m + 1) * rows, :]

    @pl.when(jnp.logical_not(is_last))
    def _():
        onehot = target_onehot(targets_ref, rows)
        n = onehot.shape[1] // PEERS
        for m in range(micro):
            ret = jnp.concatenate(
                [r[s + m * n : s + (m + 1) * n, :] for r, s in zip((r0, r1, r2, r3), skips)], 0
            )
            cot_ref[m] = (cpart_ref[m * rows : (m + 1) * rows, :] + nn_dot(onehot, ret)).astype(BF16)


def whole_kernel(x_ref, agg_ref, hidden_ref, gpn_ref, gpre_ref, node_ref, agg_out, out_ref):
    rows = x_ref.shape[1]
    gpre = gpre_ref[...]
    node_ref[...] = tn_dot(x_ref[0], gpre[:rows]) + tn_dot(x_ref[1], gpre[rows:])
    agg_out[...] = tn_dot(agg_ref[...], gpre)
    out_ref[...] = tn_dot(hidden_ref[...], gpn_ref[...])


def body(
    section_inputs,
    out_cot,
    w_node,
    w_agg,
    w_out,
    bias,
    gain,
    send_rows,
    blk_pairs,
    blk_count,
    blk_values,
):
    peers = lax.axis_size("dom")
    assert lax.axis_size("segment") == 2 and peers % 4 == 0
    x = section_inputs[0]
    micro, rows, feat = x.shape
    _, slots, per_peer = send_rows.shape
    assert slots * per_peer == 128 and slots == PEERS and micro == 2
    total = micro * rows
    pairs = blk_pairs[0]
    values = blk_values[0]
    row_blocks = rows // 128
    wide = micro * feat
    w_n, w_a, w_o = w_node[0], w_agg[0], w_out[0]
    matmul = 2 * total * feat * feat
    size = total * feat
    chunk = shape((micro * per_peer, feat), BF16)

    def swap_partner(p, k):
        if k == 0:
            return p ^ 1
        if k == 1:
            return (p + 1 if p & 1 else p - 1) % peers
        up = (p >> 1) & 1
        return (p + 2 if up == (k == 3) else p - 2) % peers

    def swapped(v, k, cores):
        return lax.ppermute(
            v,
            ("dom", "segment"),
            [(2 * p + s, 2 * swap_partner(p, k) + d) for p in range(peers) for s, d in cores],
        )

    def across(v, src, dst):
        return lax.ppermute(
            v, ("dom", "segment"), [(2 * p + src, 2 * p + dst) for p in range(peers)]
        )

    def flipped(v, bit):
        return lax.ppermute(v, "dom", [(p, p ^ (1 << bit)) for p in range(peers)])

    f_full, b_full = shape((total, feat), F32), shape((total, feat), BF16)
    s_sums = shape((EXTRA, feat), F32)
    outgoing = call(gather_kernel, [chunk] * slots, [], matmul // 8, 2 * size, send_rows, x)
    halos = [swapped(v, k, ((0, 0), (1, 1))) for k, v in enumerate(outgoing)]
    z, acc = call(
        node_kernel,
        [f_full, shape((row_blocks, 128, wide), F32)],
        [pltpu.VMEM((row_blocks, 128, wide), BF16)],
        2 * matmul, 8 * size,
        pairs, blk_count, x, values, w_n, bias,
        scalars=2,
    )
    gm_shape = (row_blocks, 128, wide)
    first = call(
        first_kernel,
        [chunk] * slots
        + [shape(gm_shape, BF16), f_full, f_full, shape((total, 128), F32)]
        + [b_full] * 4 + [s_sums],
        [
            pltpu.VMEM((1, 128, wide), BF16),
            pltpu.VMEM(gm_shape, F32),
            pltpu.VMEM((total, feat), F32),
            pltpu.VMEM((1, 128, wide), F32),
        ],
        4 * matmul, 20 * size,
        pairs, blk_count, *halos, values, z, acc, out_cot, w_a, w_o, gain,
        scalars=2,
    )
    to_return = first[:slots]
    gm1, dact, normed, inv_std, agg, hidden, gpn1, gpre1, sums1 = first[slots:]
    returned = [swapped(v, k, ((1, 0),)) for k, v in enumerate(to_return)]
    cpart1 = call(
        cpart_kernel, f_full, [pltpu.VMEM(gm_shape, F32)], matmul, 10 * size,
        pairs, blk_count, out_cot, gpre1, gm1, values, w_n,
        scalars=2,
    )
    c_in = across(cpart1, 1, 0)
    share = feat // peers
    half = share // 2
    na, nb = share + half, share + half + EXTRA
    halving = peers == 8
    turned, second_outs = [], []
    if halving:
        turned = call(
            functools.partial(turn_kernel, peers),
            [shape((8 * na, total), BF16), shape((8 * half, total), BF16), shape((8 * share, total), BF16)],
            [pltpu.VMEM((feat, total), BF16)],
            size, 12 * size,
            x, agg, hidden,
        )
        second_outs = [
            shape((4, na, feat), F32), shape((4, nb, feat), F32),
            shape((4 * na, feat), BF16), shape((4 * nb, feat), BF16),
        ]
    second = call(
        second_kernel,
        second_outs + [b_full, b_full, b_full, s_sums],
        [pltpu.VMEM((rows, slots * per_peer), BF16), pltpu.VMEM((total, feat), F32)],
        4 * matmul, 20 * size,
        send_rows, *returned, c_in, dact, normed, inv_std, gpn1, gpre1, sums1, w_o, gain, *turned,
    )
    g_low, gpn, gpre, sums = second[-4:]
    if halving:
        keep_a, keep_b, send_a, send_b = second[:4]
        recv_a, recv_b = flipped(send_a, 0), flipped(send_b, 1)
    tail = call(
        tail_kernel,
        [chunk] * slots + [f_full],
        [pltpu.VMEM(gm_shape, BF16), pltpu.VMEM(gm_shape, F32), pltpu.VMEM((1, 128, wide), F32)],
        2 * matmul, 12 * size,
        pairs, blk_count, g_low, gpre, values, w_n, w_a,
        scalars=2,
    )
    to_return, cpart0 = tail[:slots], tail[slots]
    other = across(g_low, 0, 1)
    same = ((0, 0),)
    if halving:
        back_b, back_d = swapped(to_return[1], 1, same), swapped(to_return[3], 3, same)
        ride = chunk.shape[0]
        keep_a, keep_b, send_a, send_b = call(
            functools.partial(halve_kernel, (1, 0), 2),
            [
                shape((2, na, feat), F32), shape((2, nb, feat), F32),
                shape((2 * na + ride, feat), BF16), shape((2 * nb + ride, feat), BF16),
            ],
            [], size, 8 * size, keep_a, keep_b, recv_a, recv_b, to_return[2], to_return[0],
        )
        recv_a, recv_b = flipped(send_a, 1), flipped(send_b, 0)
        returned, skips = (recv_b, back_b, recv_a, back_d), (2 * nb, 0, 2 * na, 0)
        keep_a, keep_b, send_a, send_b = call(
            functools.partial(halve_kernel, (2, 2), 0),
            [
                shape((1, na, feat), F32), shape((1, nb, feat), F32),
                shape((na, feat), BF16), shape((nb, feat), BF16),
            ],
            [], size, 4 * size, keep_a, keep_b, recv_a, recv_b,
        )
        recv_a, recv_b = flipped(send_a, 2), flipped(send_b, 2)
        part, row = shape((share, feat), F32), shape((1, feat), F32)
        grad_node, grad_agg, grad_out, grad_bias, grad_gain = call(
            last_kernel, [part, part, part, row, row], [], size, 2 * size,
            keep_a, keep_b, recv_a, recv_b,
        )
    else:
        square = shape((feat, feat), F32)
        full = call(
            whole_kernel, [square] * 3, [], 3 * matmul, 12 * size, x, agg, hidden, gpn, gpre
        )
        grad_node, grad_agg, grad_out = [
            lax.psum_scatter(v, "dom", scatter_dimension=0, tiled=True) for v in full
        ]
        sums = lax.psum(sums, "dom")
        grad_bias, grad_gain = sums[0:1], sums[1:2]
        returned = [swapped(v, k, same) for k, v in enumerate(to_return)]
        skips = (0,) * slots
    cot = call(
        functools.partial(cot_kernel, skips), shape((micro, rows, feat), BF16), [], matmul // 4, 4 * size,
        send_rows, *returned, cpart0, other,
    )
    return (
        cot[None],
        grad_node[None],
        grad_agg[None],
        grad_out[None],
        grad_bias,
        grad_gain,
    )


def solution(mesh):
    placed = (
        P("segment", None, ("grp", "dom"), None),
        P(None, ("grp", "dom"), None),
        P("segment", None, None),
        P("segment", None, None),
        P("segment", None, None),
        P("segment", None),
        P("segment", None),
        P("dom", None, None),
        P("dom", None, None),
        P("dom"),
        P("dom", None, None, None),
    )
    return jax.shard_map(
        body,
        mesh=mesh,
        in_specs=placed,
        out_specs=(
            P("segment", None, ("grp", "dom"), None),
            P("segment", ("grp", "dom"), None),
            P("segment", ("grp", "dom"), None),
            P("segment", ("grp", "dom"), None),
            P("segment", "grp"),
            P("segment", "grp"),
        ),
        check_vma=False,
    )
```

time: 336 us -> 73.7 us (0.22)
  waiting for transfers between devices: 117 us -> 22.8 us
  local copies, waits for them, and re-layouts: 61.1 us -> 5.73 us
  matrix products: 44.5 us -> 0 us
  other arithmetic: 27.6 us -> 0 us
  blocking collectives: 25.3 us -> 0 us
  starting transfers between devices: 43.9 us -> 28.5 us
  Pallas kernels: 0 us -> 14.6 us
  between operations: 15.6 us -> 1.5 us
    psum x1 -> x0, waiting for transfers between devices: 87.6 us -> none  [body(): lax.psum((full_node, full_agg, full_out, bias_total, gain_total), 'dom')]
    dot_general x33 -> x0, matrix products: 44.5 us -> none  [the longest x3 8.17 us: aggregate(): summed = jnp.einsum('bk,kid->bid', onehot, products, precision=PRECISE)]
    psum x1 -> x0, blocking collectives: 25.3 us -> none  [body(): lax.psum((full_node, full_agg, full_out, bias_total, gain_total), 'dom')]
    dot_general x9 -> x0, local copies, waits for them, and re-layouts: 19.8 us -> none  [the longest x3 9.2 us: spread(): jnp.einsum('kij,kid->kjd', values, picked, preferred_element_type=jnp.flo...]
    gather x18 -> x0, local copies, waits for them, and re-layouts: 15.7 us -> none  [the longest x12 9.37 us: fetch_halo(): outgoing = x_rows[targets[slot_num]]]
    ppermute x26 -> x18, starting transfers between devices: 43.8 us -> 28.5 us  [the longest x10 19 us: swapped(): lax.ppermute(v, ('dom', 'segment'), [(2 * p + s, 2 * swap_partner(p, k) +...]
    pallas_call x0 -> x11, Pallas kernels: none -> 14.6 us  [call(): pl.pallas_call(kernel, out_shape=outs, in_specs=[SMEM] * scalars + [VMEM]...]
    scatter-add x3 -> x0, other arithmetic: 8.25 us -> none  [body(): grad_x = grad_x.at[flat_targets].add(returned.astype(jnp.float32))]
  transfers between devices with their start and end apart: 27 -> 18, of which waited for: 9 -> 10; matrix products, arithmetic and copies ran while one was open for 23% -> 0% of each run, Pallas kernels for 0% -> 8%
where the time goes in v2:
time: 73.7 us; the launch traced here: 73.1 us
  starting transfers between devices  28.5 us (39%)
  waiting for transfers between devices  22.8 us (31%)
  Pallas kernels  14.6 us (20%)
  local copies, waits for them, and re-layouts  5.73 us (8%)
  between operations  1.5 us (2%)
    ppermute x10, starting transfers between devices, swapped(): lax.ppermute(v, ('dom', 'segment'), [(2 * p + s, 2 * swap_partner(p, k) +...  19 us
    pallas_call x11, Pallas kernels, call(): pl.pallas_call(kernel, out_shape=outs, in_specs=[SMEM] * scalars + [VMEM]...  14.6 us
    ppermute x10, waiting for transfers between devices, swapped(): lax.ppermute(v, ('dom', 'segment'), [(2 * p + s, 2 * swap_partner(p, k) +...  12.3 us
    ppermute x6, waiting for transfers between devices, flipped(): return lax.ppermute(v, 'dom', [(p, p ^ 1 << bit) for p in range(peers)])  10.4 us
    ppermute x6, starting transfers between devices, flipped(): return lax.ppermute(v, 'dom', [(p, p ^ 1 << bit) for p in range(peers)])  6.84 us
    unnamed x28, local copies, waits for them, and re-layouts  5.73 us
    ppermute x2, starting transfers between devices, across(): lax.ppermute(v, ('dom', 'segment'), [(2 * p + src, 2 * p + dst) for p in...  2.6 us
  transfers between devices with their start and end apart: 18, of which 10 were waited for; matrix products, arithmetic and copies ran while one was open for 0% of the time, Pallas kernels for 8%

profile of v2, /device:TPU:0, one launch (start us, length us, event | category | flops | bytes accessed | tf_op | source)
XLA Modules:
  0.0 73.1 jit_solution(9802978592729752974)
XLA Ops:
  0.6 1.0 %copy-done.2 = bf16[1,2,256,512]{3,2,1,0:T(8,128)(2,1)S(1)} copy-done((bf16[1,2,256,512]{3,2,1,0:T(8,128)(2,1)S(1)}, bf16[1,2,256,512]{3,2,1,0:T(8,128)(2,1)}, u32[]{:S(2)}) %copy-start.2) | copy-done | bytes 524312
  1.7 0.7 copy-done.9
  2.4 0.3 shard_map.154
  2.7 3.0 %collective-permute-start = (bf16[64,512]{1,0:T(8,128)(2,1)S(1)}, bf16[64,512]{1,0:T(8,128)(2,1)S(1)}, u32[]{:S(2)}, u32[]{:S(2)}) collective-permute-start(bf16[64,512]{1,0:T(8,128)(2,1)S(1)} %get-tuple-element.52), channel_id=1, source_target_pairs={{0,2},{1,3},{2,0},{3,1},{4,6},{5,7},{6,4},{7,5},{8,10},{9,11},{10,... | collective-permute-start | bytes 196616 | tf_op jit(solution)/shard_map/ppermute | solution.py:450
  5.7 3.6 %collective-permute-start.1 = (bf16[64,512]{1,0:T(8,128)(2,1)S(1)}, bf16[64,512]{1,0:T(8,128)(2,1)S(1)}, u32[]{:S(2)}, u32[]{:S(2)}) collective-permute-start(bf16[64,512]{1,0:T(8,128)(2,1)S(1)} %get-tuple-element.53), channel_id=1, source_target_pairs={{0,14},{1,15},{2,4},{3,5},{4,2},{5,3},{6,8},{7,9},{8,6},{9,7},{10,... | collective-permute-start | bytes 196616 | tf_op jit(solution)/shard_map/ppermute | solution.py:450
  9.3 0.9 %collective-permute-start.3 = (bf16[64,512]{1,0:T(8,128)(2,1)S(1)}, bf16[64,512]{1,0:T(8,128)(2,1)S(1)}, u32[]{:S(2)}, u32[]{:S(2)}) collective-permute-start(bf16[64,512]{1,0:T(8,128)(2,1)S(1)} %get-tuple-element.55), channel_id=1, source_target_pairs={{0,12},{1,13},{2,14},{3,15},{4,8},{5,9},{6,10},{7,11},{8,4},{9,5},... | collective-permute-start | bytes 196616 | tf_op jit(solution)/shard_map/ppermute | solution.py:450
  10.8 0.0 copy-start.13
  10.8 0.0 copy-start.11
  10.9 0.7 copy-done.13
  11.5 0.0 copy-done.11
  11.5 1.0 %copy-done.5 = bf16[1,512,512]{2,1,0:T(8,128)(2,1)S(1)} copy-done((bf16[1,512,512]{2,1,0:T(8,128)(2,1)S(1)}, bf16[1,512,512]{2,1,0:T(8,128)(2,1)}, u32[]{:S(2)}) %copy-start.5) | copy-done | bytes 524312
  12.6 0.9 %copy-done.7 = bf16[1,7,128,128]{3,2,1,0:T(8,128)(2,1)S(1)} copy-done((bf16[1,7,128,128]{3,2,1,0:T(8,128)(2,1)S(1)}, bf16[1,7,128,128]{3,2,1,0:T(8,128)(2,1)}, u32[]{:S(2)}) %copy-start.7) | copy-done | bytes 229400
  13.5 1.5 %shard_map.155 = (f32[512,512]{1,0:T(8,128)S(1)}, f32[2,128,1024]{2,1,0:T(8,128)S(1)}) custom-call(s32[2,7]{1,0:T(2,128)S(1)} %bitcast.24, s32[1]{0:T(128)S(6)} %copy.17.count_ref, bf16[2,256,512]{2,1,0:T(8,128)(2,1)S(1)} %bitcast.15, bf16[7,128,128]{2,1,0:T(8,128)(2,1)S(1)} %bitcast.20, bf16[512,512]{1,0:T(8,128)(2,1)S(1)} %bitcast.17, ...), custom_call_target="tpu_custom_call" | custom-call | flops 536870912 | bytes 2097152 | tf_op jit(solution)/shard_map/pallas_call | solution.py:37
  15.0 0.0 collective-permute-done.2.h2
  15.0 0.4 collective-permute-done.3.h3
  15.5 0.7 copy-done.12
  16.1 3.3 %shard_map.156 = (bf16[64,512]{1,0:T(8,128)(2,1)S(1)}, bf16[64,512]{1,0:T(8,128)(2,1)S(1)}, bf16[64,512]{1,0:T(8,128)(2,1)S(1)}, bf16[64,512]{1,0:T(8,128)(2,1)S...) custom-call(s32[2,7]{1,0:T(2,128)S(1)} %bitcast.25, ...), custom_call_target="tpu_custom_call" | custom-call | flops 1073741824 | bytes 5242880 | tf_op jit(solution)/shard_map/pallas_call | solution.py:37
  19.5 1.6 %shard_map.157 = f32[512,512]{1,0:T(8,128)S(1)} custom-call(s32[2,7]{1,0:T(2,128)S(1)} %bitcast.26, s32[1]{0:T(128)S(6)} %copy.17.count_ref, bf16[2,256,512]{2,1,0:T(8,128)(2,1)S(1)} %copy-done.4, bf16[512,512]{1,0:T(8,128)(2,1)S(1)} %get-tuple-element.62.gpre_ref.gpre1_ref, bf16[2,128,1024]{2,1,0:T(8,128)(2,1)S(1)} %get-tuple-element.63.gm_ref, ...), custom_call_target="tpu_custom_call" | custom-call | flops 268435456 | bytes 2621440 | tf_op jit(solution)/shard_map/pallas_call | solution.py:37
  21.1 1.3 %collective-permute-start.8 = (f32[512,512]{1,0:T(8,128)S(1)}, f32[512,512]{1,0:T(8,128)S(1)}, u32[]{:S(2)}, u32[]{:S(2)}) collective-permute-start(f32[512,512]{1,0:T(8,128)S(1)} %shard_map.157), channel_id=1, source_target_pairs={{1,0},{3,2},{5,4},{7,6},{9,8},{11,10},{13,12},{15,14},{17,16},{19,... | collective-permute-start | bytes 3145736 | tf_op jit(solution)/shard_map/ppermute | solution.py:457
  22.4 1.3 %collective-permute-start.4 = (bf16[64,512]{1,0:T(8,128)(2,1)S(1)}, bf16[64,512]{1,0:T(8,128)(2,1)S(1)}, u32[]{:S(2)}, u32[]{:S(2)}) collective-permute-start(bf16[64,512]{1,0:T(8,128)(2,1)S(1)} %get-tuple-element.58), channel_id=1, source_target_pairs={{1,2},{3,0},{5,6},{7,4},{9,10},{11,8},{13,14},{15,12},{17,18},{19,... | collective-permute-start | bytes 196616 | tf_op jit(solution)/shard_map/ppermute | solution.py:450
  23.7 1.3 %collective-permute-start.5 = (bf16[64,512]{1,0:T(8,128)(2,1)S(1)}, bf16[64,512]{1,0:T(8,128)(2,1)S(1)}, u32[]{:S(2)}, u32[]{:S(2)}) collective-permute-start(bf16[64,512]{1,0:T(8,128)(2,1)S(1)} %get-tuple-element.59), channel_id=1, source_target_pairs={{1,14},{3,4},{5,2},{7,8},{9,6},{11,12},{13,10},{15,0},{17,30},{19,... | collective-permute-start | bytes 196616 | tf_op jit(solution)/shard_map/ppermute | solution.py:450
  25.0 1.3 %collective-permute-start.6 = (bf16[64,512]{1,0:T(8,128)(2,1)S(1)}, bf16[64,512]{1,0:T(8,128)(2,1)S(1)}, u32[]{:S(2)}, u32[]{:S(2)}) collective-permute-start(bf16[64,512]{1,0:T(8,128)(2,1)S(1)} %get-tuple-element.60), channel_id=1, source_target_pairs={{1,4},{3,6},{5,0},{7,2},{9,12},{11,14},{13,8},{15,10},{17,20},{19,... | collective-permute-start | bytes 196616 | tf_op jit(solution)/shard_map/ppermute | solution.py:450
  26.3 1.3 %collective-permute-start.7 = (bf16[64,512]{1,0:T(8,128)(2,1)S(1)}, bf16[64,512]{1,0:T(8,128)(2,1)S(1)}, u32[]{:S(2)}, u32[]{:S(2)}) collective-permute-start(bf16[64,512]{1,0:T(8,128)(2,1)S(1)} %get-tuple-element.61), channel_id=1, source_target_pairs={{1,12},{3,14},{5,8},{7,10},{9,4},{11,6},{13,0},{15,2},{17,28},{19,... | collective-permute-start | bytes 196616 | tf_op jit(solution)/shard_map/ppermute | solution.py:450
  27.6 0.6 shard_map.158
  28.2 0.8 %collective-permute-done.4.r0 = bf16[64,512]{1,0:T(8,128)(2,1)S(1)} collective-permute-done((bf16[64,512]{1,0:T(8,128)(2,1)S(1)}, bf16[64,512]{1,0:T(8,128)(2,1)S(1)}, u32[]{:S(2)}, u32[]{:S(2)}) %collective-permute-start.4) | collective-permute-done | bytes 65568 | tf_op jit(solution)/shard_map/ppermute | solution.py:450
  29.1 2.9 %collective-permute-done.5.r1 = bf16[64,512]{1,0:T(8,128)(2,1)S(1)} collective-permute-done((bf16[64,512]{1,0:T(8,128)(2,1)S(1)}, bf16[64,512]{1,0:T(8,128)(2,1)S(1)}, u32[]{:S(2)}, u32[]{:S(2)}) %collective-permute-start.5) | collective-permute-done | bytes 65568 | tf_op jit(solution)/shard_map/ppermute | solution.py:450
  32.0 0.7 collective-permute-done.6.r2
  32.7 1.7 %collective-permute-done.7.r3 = bf16[64,512]{1,0:T(8,128)(2,1)S(1)} collective-permute-done((bf16[64,512]{1,0:T(8,128)(2,1)S(1)}, bf16[64,512]{1,0:T(8,128)(2,1)S(1)}, u32[]{:S(2)}, u32[]{:S(2)}) %collective-permute-start.7) | collective-permute-done | bytes 65568 | tf_op jit(solution)/shard_map/ppermute | solution.py:450
  34.4 0.7 copy-done.10
  35.1 2.6 %shard_map.159 = (f32[4,96,512]{2,1,0:T(8,128)S(1)}, f32[4,104,512]{2,1,0:T(8,128)S(1)}, bf16[384,512]{1,0:T(8,128)(2,1)S(1)}, bf16[416,512]{1,0:T(8,128)(2,1)S(...) custom-call(s32[1,4,32]{2,1,0:T(4,128)S(1)} %copy-done.10, ...), custom_call_target="tpu_custom_call" | custom-call | flops 1073741824 | bytes 5242880 | tf_op jit(solution)/shard_map/pallas_call | solution.py:37
  37.7 1.9 %collective-permute-start.9 = (bf16[384,512]{1,0:T(8,128)(2,1)S(1)}, bf16[384,512]{1,0:T(8,128)(2,1)S(1)}, u32[]{:S(2)}, u32[]{:S(2)}) collective-permute-start(bf16[384,512]{1,0:T(8,128)(2,1)S(1)} %get-tuple-element.76), channel_id=1, source_target_pairs={{0,2},{2,0},{4,6},{6,4},{8,10},{10,8},{12,14},{14,12},{1,3},{3,1},... | collective-permute-start | bytes 1179656 | tf_op jit(solution)/shard_map/ppermute | solution.py:462
  39.6 1.3 %collective-permute-start.15 = (bf16[512,512]{1,0:T(8,128)(2,1)S(1)}, bf16[512,512]{1,0:T(8,128)(2,1)S(1)}, u32[]{:S(2)}, u32[]{:S(2)}) collective-permute-start(bf16[512,512]{1,0:T(8,128)(2,1)S(1)} %get-tuple-element.78.g_ref), channel_id=1, source_target_pairs={{0,1},{2,3},{4,5},{6,7},{8,9},{10,11},{12,13},{14,15},{16,17},{18,... | collective-permute-start | bytes 1572872 | tf_op jit(solution)/shard_map/ppermute | solution.py:457
  40.9 2.5 %shard_map.160 = (bf16[64,512]{1,0:T(8,128)(2,1)S(1)}, bf16[64,512]{1,0:T(8,128)(2,1)S(1)}, bf16[64,512]{1,0:T(8,128)(2,1)S(1)}, bf16[64,512]{1,0:T(8,128)(2,1)S(1)}, f32[512,512]{1,0:T(8,128)S(1)}) custom-call(s32[2,7]{1,0:T(2,128)S(1)} %bitcast.27, s32[1]{0:T(128)S(6)} %copy.17.count_ref, bf16[512,512]{1,0:T(8,128)(2,1)S(1)} %get-tuple-element.78.g_ref, ...), custom_call_target="tpu_custom_call" | custom-call | flops 536870912 | bytes 3145728 | tf_op jit(solution)/shard_map/pallas_call | solution.py:37
  43.4 5.0 %collective-permute-done.9.recv_a = bf16[384,512]{1,0:T(8,128)(2,1)S(1)} collective-permute-done((bf16[384,512]{1,0:T(8,128)(2,1)S(1)}, bf16[384,512]{1,0:T(8,128)(2,1)S(1)}, u32[]{:S(2)}, u32[]{:S(2)}) %collective-permute-start.9) | collective-permute-done | bytes 393248 | tf_op jit(solution)/shard_map/ppermute | solution.py:462
  48.4 0.2 shard_map.161
  48.5 0.9 %collective-permute-start.11 = (bf16[272,512]{1,0:T(8,128)(2,1)S(1)}, bf16[272,512]{1,0:T(8,128)(2,1)S(1)}, u32[]{:S(2)}, u32[]{:S(2)}) collective-permute-start(bf16[272,512]{1,0:T(8,128)(2,1)S(1)} %get-tuple-element.82), channel_id=1, source_target_pairs={{0,2},{2,0},{4,6},{6,4},{8,10},{10,8},{12,14},{14,12},{1,3},{3,1},... | collective-permute-start | bytes 835592 | tf_op jit(solution)/shard_map/ppermute | solution.py:462
  49.5 1.0 %collective-permute-start.13 = (bf16[256,512]{1,0:T(8,128)(2,1)S(1)}, bf16[256,512]{1,0:T(8,128)(2,1)S(1)}, u32[]{:S(2)}, u32[]{:S(2)}) collective-permute-start(bf16[256,512]{1,0:T(8,128)(2,1)S(1)} %get-tuple-element.84), channel_id=1, source_target_pairs={{0,4},{2,6},{4,0},{6,2},{8,12},{10,14},{12,8},{14,10},{1,5},{3,7},... | collective-permute-start | bytes 786440 | tf_op jit(solution)/shard_map/ppermute | solution.py:462
  50.4 5.4 %collective-permute-done.13.r2.recv_a = bf16[256,512]{1,0:T(8,128)(2,1)S(1)} collective-permute-done((bf16[256,512]{1,0:T(8,128)(2,1)S(1)}, bf16[256,512]{1,0:T(8,128)(2,1)S(1)}, u32[]{:S(2)}, u32[]{:S(2)}) %collective-permute-start.13) | collective-permute-done | bytes 262176 | tf_op jit(solution)/shard_map/ppermute | solution.py:462
  55.8 0.1 collective-permute-done.11.r0.recv_b
  55.9 0.1 shard_map.163
  56.0 1.5 %collective-permute-start.17 = (bf16[104,512]{1,0:T(8,128)(2,1)S(1)}, bf16[104,512]{1,0:T(8,128)(2,1)S(1)}, u32[]{:S(2)}, u32[]{:S(2)}) collective-permute-start(bf16[104,512]{1,0:T(8,128)(2,1)S(1)} %get-tuple-element.92), channel_id=1, source_target_pairs={{0,8},{2,10},{4,12},{6,14},{8,0},{10,2},{12,4},{14,6},{1,9},{3,11}... | collective-permute-start | bytes 319496 | tf_op jit(solution)/shard_map/ppermute | solution.py:462
  57.4 1.5 %collective-permute-start.16 = (bf16[96,512]{1,0:T(8,128)(2,1)S(1)}, bf16[96,512]{1,0:T(8,128)(2,1)S(1)}, u32[]{:S(2)}, u32[]{:S(2)}) collective-permute-start(bf16[96,512]{1,0:T(8,128)(2,1)S(1)} %get-tuple-element.91), channel_id=1, source_target_pairs={{0,8},{2,10},{4,12},{6,14},{8,0},{10,2},{12,4},{14,6},{1,9},{3,11}... | collective-permute-start | bytes 294920 | tf_op jit(solution)/shard_map/ppermute | solution.py:462
  59.0 4.2 %collective-permute-start.12 = (bf16[64,512]{1,0:T(8,128)(2,1)S(1)}, bf16[64,512]{1,0:T(8,128)(2,1)S(1)}, u32[]{:S(2)}, u32[]{:S(2)}) collective-permute-start(bf16[64,512]{1,0:T(8,128)(2,1)S(1)} %get-tuple-element.83), channel_id=1, source_target_pairs={{0,14},{2,4},{4,2},{6,8},{8,6},{10,12},{12,10},{14,0},{16,30},{18,... | collective-permute-start | bytes 196616 | tf_op jit(solution)/shard_map/ppermute | solution.py:450
  63.2 2.2 %collective-permute-start.14 = (bf16[64,512]{1,0:T(8,128)(2,1)S(1)}, bf16[64,512]{1,0:T(8,128)(2,1)S(1)}, u32[]{:S(2)}, u32[]{:S(2)}) collective-permute-start(bf16[64,512]{1,0:T(8,128)(2,1)S(1)} %get-tuple-element.85), channel_id=1, source_target_pairs={{0,12},{2,14},{4,8},{6,10},{8,4},{10,6},{12,0},{14,2},{16,28},{18,... | collective-permute-start | bytes 196616 | tf_op jit(solution)/shard_map/ppermute | solution.py:450
  65.4 2.4 %collective-permute-done.12.r1 = bf16[64,512]{1,0:T(8,128)(2,1)S(1)} collective-permute-done((bf16[64,512]{1,0:T(8,128)(2,1)S(1)}, bf16[64,512]{1,0:T(8,128)(2,1)S(1)}, u32[]{:S(2)}, u32[]{:S(2)}) %collective-permute-start.12) | collective-permute-done | bytes 65568 | tf_op jit(solution)/shard_map/ppermute | solution.py:450
  67.8 3.3 %collective-permute-done.14.r3 = bf16[64,512]{1,0:T(8,128)(2,1)S(1)} collective-permute-done((bf16[64,512]{1,0:T(8,128)(2,1)S(1)}, bf16[64,512]{1,0:T(8,128)(2,1)S(1)}, u32[]{:S(2)}, u32[]{:S(2)}) %collective-permute-start.14) | collective-permute-done | bytes 65568 | tf_op jit(solution)/shard_map/ppermute | solution.py:450
  71.1 1.1 %shard_map.162 = bf16[2,256,512]{2,1,0:T(8,128)(2,1)} custom-call(s32[1,4,32]{2,1,0:T(4,128)S(1)} %copy-done.10, bf16[272,512]{1,0:T(8,128)(2,1)S(1)} %collective-permute-done.11.r0.recv_b, bf16[64,512]{1,0:T(8,128)(2,1)S(1)} %collective-permute-done.12.r1, bf16[256,512]{1,0:T(8,128)(2,1)S(1)} %collective-permute-done.13.r2.recv_a, ...), custom_call_target="tpu_custom_call" | custom-call | flops 67108864 | bytes 1048576 | tf_op jit(solution)/shard_map/pallas_call | solution.py:37
  72.3 0.8 %shard_map.164 = (f32[64,512]{1,0:T(8,128)}, f32[64,512]{1,0:T(8,128)}, f32[64,512]{1,0:T(8,128)}, f32[1,512]{1,0:T(1,128)}, f32[1,512]{1,0:T(1,128)}) custom-call(f32[1,96,512]{2,1,0:T(8,128)S(1)} %get-tuple-element.89.keep_a, f32[1,104,512]{2,1,0:T(8,128)S(1)} %get-tuple-element.90.keep_b, bf16[96,512]{1,0:T(8,128)(2,1)S(1)} %collective-permute-done.16.recv_a, ...), custom_call_target="tpu_custom_call" | custom-call | flops 262144 | bytes 524288 | tf_op jit(solution)/shard_map/pallas_call | solution.py:37
  (27 shorter events, 0.1 us)
Async XLA Ops:
  0.6 1.0 %copy-start.2 = (bf16[1,2,256,512]{3,2,1,0:T(8,128)(2,1)S(1)}, bf16[1,2,256,512]{3,2,1,0:T(8,128)(2,1)}, u32[]{:S(2)}) copy-start(bf16[1,2,256,512]{3,2,1,0:T(8,128)(2,1)} %param.11) | copy-start | bytes 1572868
  1.7 0.7 copy-start.9
  2.4 8.5 %copy-start.3 = (bf16[1,2,256,512]{3,2,1,0:T(8,128)(2,1)S(1)}, bf16[1,2,256,512]{3,2,1,0:T(8,128)(2,1)}, u32[]{:S(2)}) copy-start(bf16[1,2,256,512]{3,2,1,0:T(8,128)(2,1)} %param.11) | copy-start | bytes 1572868
  2.7 12.3 %collective-permute-start = (bf16[64,512]{1,0:T(8,128)(2,1)S(1)}, bf16[64,512]{1,0:T(8,128)(2,1)S(1)}, u32[]{:S(2)}, u32[]{:S(2)}) collective-permute-start(bf16[64,512]{1,0:T(8,128)(2,1)S(1)} %get-tuple-element.52), channel_id=1, source_target_pairs={{0,2},{1,3},{2,0},{3,1},{4,6},{5,7},{6,4},{7,5},{8,10},{9,11},{10,... | collective-permute-start | bytes 196616 | tf_op jit(solution)/shard_map/ppermute | solution.py:450
  5.7 9.3 %collective-permute-start.1 = (bf16[64,512]{1,0:T(8,128)(2,1)S(1)}, bf16[64,512]{1,0:T(8,128)(2,1)S(1)}, u32[]{:S(2)}, u32[]{:S(2)}) collective-permute-start(bf16[64,512]{1,0:T(8,128)(2,1)S(1)} %get-tuple-element.53), channel_id=1, source_target_pairs={{0,14},{1,15},{2,4},{3,5},{4,2},{5,3},{6,8},{7,9},{8,6},{9,7},{10,... | collective-permute-start | bytes 196616 | tf_op jit(solution)/shard_map/ppermute | solution.py:450
  9.3 5.7 %collective-permute-start.2 = (bf16[64,512]{1,0:T(8,128)(2,1)S(1)}, bf16[64,512]{1,0:T(8,128)(2,1)S(1)}, u32[]{:S(2)}, u32[]{:S(2)}) collective-permute-start(bf16[64,512]{1,0:T(8,128)(2,1)S(1)} %get-tuple-element.54), channel_id=1, source_target_pairs={{0,4},{1,5},{2,6},{3,7},{4,0},{5,1},{6,2},{7,3},{8,12},{9,13},{10,... | collective-permute-start | bytes 196616 | tf_op jit(solution)/shard_map/ppermute | solution.py:450
  9.3 6.2 %collective-permute-start.3 = (bf16[64,512]{1,0:T(8,128)(2,1)S(1)}, bf16[64,512]{1,0:T(8,128)(2,1)S(1)}, u32[]{:S(2)}, u32[]{:S(2)}) collective-permute-start(bf16[64,512]{1,0:T(8,128)(2,1)S(1)} %get-tuple-element.55), channel_id=1, source_target_pairs={{0,12},{1,13},{2,14},{3,15},{4,8},{5,9},{6,10},{7,11},{8,4},{9,5},... | collective-permute-start | bytes 196616 | tf_op jit(solution)/shard_map/ppermute | solution.py:450
  10.8 0.7 copy-start.13
  10.8 0.7 copy-start.11
  11.5 1.0 %copy-start.5 = (bf16[1,512,512]{2,1,0:T(8,128)(2,1)S(1)}, bf16[1,512,512]{2,1,0:T(8,128)(2,1)}, u32[]{:S(2)}) copy-start(bf16[1,512,512]{2,1,0:T(8,128)(2,1)} %param.13) | copy-start | bytes 1572868
  12.6 0.9 %copy-start.7 = (bf16[1,7,128,128]{3,2,1,0:T(8,128)(2,1)S(1)}, bf16[1,7,128,128]{3,2,1,0:T(8,128)(2,1)}, u32[]{:S(2)}) copy-start(bf16[1,7,128,128]{3,2,1,0:T(8,128)(2,1)} %param.21) | copy-start | bytes 688132
  13.5 1.9 %copy-start = (bf16[1,512,512]{2,1,0:T(8,128)(2,1)S(1)}, bf16[1,512,512]{2,1,0:T(8,128)(2,1)}, u32[]{:S(2)}) copy-start(bf16[1,512,512]{2,1,0:T(8,128)(2,1)} %param.15) | copy-start | bytes 1572868
  13.5 1.9 %copy-start.1 = (bf16[1,512,512]{2,1,0:T(8,128)(2,1)S(1)}, bf16[1,512,512]{2,1,0:T(8,128)(2,1)}, u32[]{:S(2)}) copy-start(bf16[1,512,512]{2,1,0:T(8,128)(2,1)} %param.14) | copy-start | bytes 1572868
  13.5 1.9 %copy-start.4 = (bf16[2,256,512]{2,1,0:T(8,128)(2,1)S(1)}, bf16[2,256,512]{2,1,0:T(8,128)(2,1)}, u32[]{:S(2)}) copy-start(bf16[2,256,512]{2,1,0:T(8,128)(2,1)} %g_ref.3) | copy-start | bytes 1572868
  13.5 2.0 %copy-start.8 = (bf16[1,7,128,128]{3,2,1,0:T(8,128)(2,1)S(1)}, bf16[1,7,128,128]{3,2,1,0:T(8,128)(2,1)}, u32[]{:S(2)}) copy-start(bf16[1,7,128,128]{3,2,1,0:T(8,128)(2,1)} %param.21) | copy-start | bytes 688132
  15.4 0.7 copy-start.12
  16.1 3.3 %copy-start.6 = (bf16[1,512,512]{2,1,0:T(8,128)(2,1)S(1)}, bf16[1,512,512]{2,1,0:T(8,128)(2,1)}, u32[]{:S(2)}) copy-start(bf16[1,512,512]{2,1,0:T(8,128)(2,1)} %param.13) | copy-start | bytes 1572868
  21.1 13.3 %collective-permute-start.8 = (f32[512,512]{1,0:T(8,128)S(1)}, f32[512,512]{1,0:T(8,128)S(1)}, u32[]{:S(2)}, u32[]{:S(2)}) collective-permute-start(f32[512,512]{1,0:T(8,128)S(1)} %shard_map.157), channel_id=1, source_target_pairs={{1,0},{3,2},{5,4},{7,6},{9,8},{11,10},{13,12},{15,14},{17,16},{19,... | collective-permute-start | bytes 3145736 | tf_op jit(solution)/shard_map/ppermute | solution.py:457
  22.4 6.7 %collective-permute-start.4 = (bf16[64,512]{1,0:T(8,128)(2,1)S(1)}, bf16[64,512]{1,0:T(8,128)(2,1)S(1)}, u32[]{:S(2)}, u32[]{:S(2)}) collective-permute-start(bf16[64,512]{1,0:T(8,128)(2,1)S(1)} %get-tuple-element.58), channel_id=1, source_target_pairs={{1,2},{3,0},{5,6},{7,4},{9,10},{11,8},{13,14},{15,12},{17,18},{19,... | collective-permute-start | bytes 196616 | tf_op jit(solution)/shard_map/ppermute | solution.py:450
  23.7 8.3 %collective-permute-start.5 = (bf16[64,512]{1,0:T(8,128)(2,1)S(1)}, bf16[64,512]{1,0:T(8,128)(2,1)S(1)}, u32[]{:S(2)}, u32[]{:S(2)}) collective-permute-start(bf16[64,512]{1,0:T(8,128)(2,1)S(1)} %get-tuple-element.59), channel_id=1, source_target_pairs={{1,14},{3,4},{5,2},{7,8},{9,6},{11,12},{13,10},{15,0},{17,30},{19,... | collective-permute-start | bytes 196616 | tf_op jit(solution)/shard_map/ppermute | solution.py:450
  25.0 7.7 %collective-permute-start.6 = (bf16[64,512]{1,0:T(8,128)(2,1)S(1)}, bf16[64,512]{1,0:T(8,128)(2,1)S(1)}, u32[]{:S(2)}, u32[]{:S(2)}) collective-permute-start(bf16[64,512]{1,0:T(8,128)(2,1)S(1)} %get-tuple-element.60), channel_id=1, source_target_pairs={{1,4},{3,6},{5,0},{7,2},{9,12},{11,14},{13,8},{15,10},{17,20},{19,... | collective-permute-start | bytes 196616 | tf_op jit(solution)/shard_map/ppermute | solution.py:450
  26.3 8.1 %collective-permute-start.7 = (bf16[64,512]{1,0:T(8,128)(2,1)S(1)}, bf16[64,512]{1,0:T(8,128)(2,1)S(1)}, u32[]{:S(2)}, u32[]{:S(2)}) collective-permute-start(bf16[64,512]{1,0:T(8,128)(2,1)S(1)} %get-tuple-element.61), channel_id=1, source_target_pairs={{1,12},{3,14},{5,8},{7,10},{9,4},{11,6},{13,0},{15,2},{17,28},{19,... | collective-permute-start | bytes 196616 | tf_op jit(solution)/shard_map/ppermute | solution.py:450
  34.4 0.7 copy-start.10
  37.7 10.7 %collective-permute-start.10 = (bf16[416,512]{1,0:T(8,128)(2,1)S(1)}, bf16[416,512]{1,0:T(8,128)(2,1)S(1)}, u32[]{:S(2)}, u32[]{:S(2)}) collective-permute-start(bf16[416,512]{1,0:T(8,128)(2,1)S(1)} %get-tuple-element.77), channel_id=1, source_target_pairs={{0,4},{2,6},{4,0},{6,2},{8,12},{10,14},{12,8},{14,10},{1,5},{3,7},... | collective-permute-start | bytes 1277960 | tf_op jit(solution)/shard_map/ppermute | solution.py:462
  37.7 10.7 %collective-permute-start.9 = (bf16[384,512]{1,0:T(8,128)(2,1)S(1)}, bf16[384,512]{1,0:T(8,128)(2,1)S(1)}, u32[]{:S(2)}, u32[]{:S(2)}) collective-permute-start(bf16[384,512]{1,0:T(8,128)(2,1)S(1)} %get-tuple-element.76), channel_id=1, source_target_pairs={{0,2},{2,0},{4,6},{6,4},{8,10},{10,8},{12,14},{14,12},{1,3},{3,1},... | collective-permute-start | bytes 1179656 | tf_op jit(solution)/shard_map/ppermute | solution.py:462
  39.6 31.5 %collective-permute-start.15 = (bf16[512,512]{1,0:T(8,128)(2,1)S(1)}, bf16[512,512]{1,0:T(8,128)(2,1)S(1)}, u32[]{:S(2)}, u32[]{:S(2)}) collective-permute-start(bf16[512,512]{1,0:T(8,128)(2,1)S(1)} %get-tuple-element.78.g_ref), channel_id=1, source_target_pairs={{0,1},{2,3},{4,5},{6,7},{8,9},{10,11},{12,13},{14,15},{16,17},{18,... | collective-permute-start | bytes 1572872 | tf_op jit(solution)/shard_map/ppermute | solution.py:457
  48.5 7.4 %collective-permute-start.11 = (bf16[272,512]{1,0:T(8,128)(2,1)S(1)}, bf16[272,512]{1,0:T(8,128)(2,1)S(1)}, u32[]{:S(2)}, u32[]{:S(2)}) collective-permute-start(bf16[272,512]{1,0:T(8,128)(2,1)S(1)} %get-tuple-element.82), channel_id=1, source_target_pairs={{0,2},{2,0},{4,6},{6,4},{8,10},{10,8},{12,14},{14,12},{1,3},{3,1},... | collective-permute-start | bytes 835592 | tf_op jit(solution)/shard_map/ppermute | solution.py:462
  49.5 6.4 %collective-permute-start.13 = (bf16[256,512]{1,0:T(8,128)(2,1)S(1)}, bf16[256,512]{1,0:T(8,128)(2,1)S(1)}, u32[]{:S(2)}, u32[]{:S(2)}) collective-permute-start(bf16[256,512]{1,0:T(8,128)(2,1)S(1)} %get-tuple-element.84), channel_id=1, source_target_pairs={{0,4},{2,6},{4,0},{6,2},{8,12},{10,14},{12,8},{14,10},{1,5},{3,7},... | collective-permute-start | bytes 786440 | tf_op jit(solution)/shard_map/ppermute | solution.py:462
  56.0 16.3 %collective-permute-start.17 = (bf16[104,512]{1,0:T(8,128)(2,1)S(1)}, bf16[104,512]{1,0:T(8,128)(2,1)S(1)}, u32[]{:S(2)}, u32[]{:S(2)}) collective-permute-start(bf16[104,512]{1,0:T(8,128)(2,1)S(1)} %get-tuple-element.92), channel_id=1, source_target_pairs={{0,8},{2,10},{4,12},{6,14},{8,0},{10,2},{12,4},{14,6},{1,9},{3,11}... | collective-permute-start | bytes 319496 | tf_op jit(solution)/shard_map/ppermute | solution.py:462
  57.4 14.8 %collective-permute-start.16 = (bf16[96,512]{1,0:T(8,128)(2,1)S(1)}, bf16[96,512]{1,0:T(8,128)(2,1)S(1)}, u32[]{:S(2)}, u32[]{:S(2)}) collective-permute-start(bf16[96,512]{1,0:T(8,128)(2,1)S(1)} %get-tuple-element.91), channel_id=1, source_target_pairs={{0,8},{2,10},{4,12},{6,14},{8,0},{10,2},{12,4},{14,6},{1,9},{3,11}... | collective-permute-start | bytes 294920 | tf_op jit(solution)/shard_map/ppermute | solution.py:462
  59.0 8.8 %collective-permute-start.12 = (bf16[64,512]{1,0:T(8,128)(2,1)S(1)}, bf16[64,512]{1,0:T(8,128)(2,1)S(1)}, u32[]{:S(2)}, u32[]{:S(2)}) collective-permute-start(bf16[64,512]{1,0:T(8,128)(2,1)S(1)} %get-tuple-element.83), channel_id=1, source_target_pairs={{0,14},{2,4},{4,2},{6,8},{8,6},{10,12},{12,10},{14,0},{16,30},{18,... | collective-permute-start | bytes 196616 | tf_op jit(solution)/shard_map/ppermute | solution.py:450
  63.2 8.0 %collective-permute-start.14 = (bf16[64,512]{1,0:T(8,128)(2,1)S(1)}, bf16[64,512]{1,0:T(8,128)(2,1)S(1)}, u32[]{:S(2)}, u32[]{:S(2)}) collective-permute-start(bf16[64,512]{1,0:T(8,128)(2,1)S(1)} %get-tuple-element.85), channel_id=1, source_target_pairs={{0,12},{2,14},{4,8},{6,10},{8,4},{10,6},{12,0},{14,2},{16,28},{18,... | collective-permute-start | bytes 196616 | tf_op jit(solution)/shard_map/ppermute | solution.py:450

commit v3 on v2

--- a/solution.py
+++ b/solution.py
@@ -12,6 +12,8 @@
 BF16 = jnp.bfloat16
 VMEM = pl.BlockSpec(memory_space=pltpu.VMEM)
 SMEM = pl.BlockSpec(memory_space=pltpu.SMEM)
+HBM = pl.BlockSpec(memory_space=pltpu.HBM)
+ANY = pl.BlockSpec(memory_space=pl.ANY)
 PEERS = 4
 EXTRA = 8
 PIECE = 64
@@ -33,11 +35,15 @@
     return jax.ShapeDtypeStruct(dims, dtype)
 
 
-def call(kernel, outs, scratch, flops, byts, *args, scalars=0):
+def call(kernel, outs, scratch, flops, byts, *args, scalars=0, raw=0, after=0):
+    blocks = len(args) - scalars - raw - after
+    args = list(args)
+    for i in range(scalars, scalars + raw):
+        args[i] = pltpu.with_memory_space_constraint(args[i], pltpu.HBM)
     return pl.pallas_call(
         kernel,
         out_shape=outs,
-        in_specs=[SMEM] * scalars + [VMEM] * (len(args) - scalars),
+        in_specs=[SMEM] * scalars + [HBM] * raw + [VMEM] * blocks + [ANY] * after,
         out_specs=jax.tree.map(lambda _: VMEM, outs),
         scratch_shapes=scratch,
         compiler_params=pltpu.CompilerParams(vmem_limit_bytes=24 * 1024 * 1024),
@@ -64,32 +70,64 @@
     return (lax.broadcasted_iota(jnp.int32, (rows, ids.shape[1]), 0) == ids).astype(BF16)
 
 
-def gather_kernel(targets_ref, x_ref, *outs):
+def gather_kernel(targets_hbm, x_hbm, o0, o1, o2, o3, x_ref, onehot_ref, targets_ref, sems):
+    copies = [
+        pltpu.make_async_copy(targets_hbm, targets_ref, sems.at[0]),
+        pltpu.make_async_copy(x_hbm, x_ref, sems.at[1]),
+    ]
+    for c in copies:
+        c.start()
     micro, rows, _ = x_ref.shape
-    per_peer = outs[0].shape[0] // micro
+    per_peer = o0.shape[0] // micro
+    copies[0].wait()
     onehot = target_onehot(targets_ref, rows)
+    onehot_ref[...] = onehot
+    copies[1].wait()
     for m in range(micro):
         picked = tn_dot(onehot, x_ref[m]).astype(BF16)
-        for k, out in enumerate(outs):
+        for k, out in enumerate((o0, o1, o2, o3)):
             out[m * per_peer : (m + 1) * per_peer, :] = picked[k * per_peer : (k + 1) * per_peer]
 
 
-def node_kernel(pairs_ref, count_ref, x_ref, values_ref, w_ref, bias_ref, z_ref, acc_ref, src_ref):
+def node_kernel(
+    pairs_ref, count_ref, values_hbm, w_hbm, bias_hbm, w_agg_hbm, w_out_hbm, gain_hbm, g_hbm, x_ref,
+    z_ref, acc_ref, values_ref, turned_ref, w_ref, w_agg_ref, w_out_ref, gain_ref, g_ref,
+    src_ref, bias_ref, sems,
+):
+    copies = [
+        pltpu.make_async_copy(a, b, sems.at[i])
+        for i, (a, b) in enumerate(
+            (
+                (values_hbm, values_ref), (w_hbm, w_ref), (bias_hbm, bias_ref),
+                (w_agg_hbm, w_agg_ref), (w_out_hbm, w_out_ref), (gain_hbm, gain_ref), (g_hbm, g_ref),
+            )
+        )
+    ]
+    for c in copies:
+        c.start()
     micro, rows, feat = x_ref.shape
     row_blocks = rows // 128
+    for m in range(micro):
+        for b in range(row_blocks):
+            src_ref[b, :, m * feat : (m + 1) * feat] = x_ref[m, b * 128 : (b + 1) * 128, :]
+    acc_ref[...] = jnp.zeros_like(acc_ref)
+    copies[0].wait()
+    for k in range(values_ref.shape[0]):
+        turned_ref[k] = values_ref[k].T
+        src = pairs_ref[1, k]
+
+        @pl.when((k < count_ref[0]) & (src < row_blocks))
+        def _():
+            acc_ref[pairs_ref[0, k]] += nn_dot(values_ref[k], src_ref[src])
+
+    copies[1].wait()
+    copies[2].wait()
     for m in range(micro):
         z_ref[m * rows : (m + 1) * rows, :] = nn_dot(x_ref[m], w_ref[...]) + bias_ref[
             ...
         ].astype(F32)
-        for b in range(row_blocks):
-            src_ref[b, :, m * feat : (m + 1) * feat] = x_ref[m, b * 128 : (b + 1) * 128, :]
-    acc_ref[...] = jnp.zeros_like(acc_ref)
-    for k in range(values_ref.shape[0]):
-        src = pairs_ref[1, k]
-
-        @pl.when((k < count_ref[0]) & (src < row_blocks))
-        def _():
-            acc_ref[pairs_ref[0, k]] += nn_dot(values_ref[k], src_ref[src])
+    for c in copies[3:]:
+        c.wait()
 
 
 def pieces(part):
@@ -118,24 +156,24 @@
     ]
 
 
-def halo_spread(pairs_ref, count_ref, values_ref, gm_ref, t_ref, row_blocks):
+def halo_spread(pairs_ref, count_ref, turned_ref, gm_ref, t_ref, row_blocks):
     t_ref[...] = jnp.zeros_like(t_ref)
-    for k in range(values_ref.shape[0]):
+    for k in range(turned_ref.shape[0]):
         src = pairs_ref[1, k]
 
         @pl.when((k < count_ref[0]) & (src >= row_blocks))
         def _():
-            t_ref[src - row_blocks] += tn_dot(values_ref[k], gm_ref[pairs_ref[0, k]])
-
-
-def local_spread(pairs_ref, count_ref, values_ref, gm_ref, t_ref, row_blocks):
+            t_ref[src - row_blocks] += nn_dot(turned_ref[k], gm_ref[pairs_ref[0, k]])
+
+
+def local_spread(pairs_ref, count_ref, turned_ref, gm_ref, t_ref, row_blocks):
     t_ref[...] = jnp.zeros_like(t_ref)
-    for k in range(values_ref.shape[0]):
+    for k in range(turned_ref.shape[0]):
         src = pairs_ref[1, k]
 
         @pl.when((k < count_ref[0]) & (src < row_blocks))
         def _():
-            t_ref[src] += tn_dot(values_ref[k], gm_ref[pairs_ref[0, k]])
+            t_ref[src] += nn_dot(turned_ref[k], gm_ref[pairs_ref[0, k]])
 
 
 def put_halo_grads(t_ref, outs):
@@ -150,7 +188,7 @@
 
 
 def first_kernel(
-    pairs_ref, count_ref, h0, h1, h2, h3, values_ref, z_ref, accin_ref, g_ref, w_agg_ref,
+    pairs_ref, count_ref, h0, h1, h2, h3, values_ref, turned_ref, z_ref, accin_ref, g_ref, w_agg_ref,
     w_out_ref, gain_ref,
     o0, o1, o2, o3, gm_ref, dact_ref, normed_ref, inv_ref, agg_ref, hidden_ref, gpn_ref,
     gpre_ref, sums_ref,
@@ -210,20 +248,21 @@
         gm = nt_dot(gpre_ref[part, :], w_agg_ref[...]).astype(BF16)
         for b, at, cols in wide_blocks(part, m, feat):
             gm_ref[b, :, cols] = gm[b * 128 : (b + 1) * 128]
-    halo_spread(pairs_ref, count_ref, values_ref, gm_ref, t_ref, row_blocks)
+    halo_spread(pairs_ref, count_ref, turned_ref, gm_ref, t_ref, row_blocks)
     put_halo_grads(t_ref, (o0, o1, o2, o3))
     sums_ref[0:1, :] = bias_sum
     sums_ref[1:2, :] = gain_sum
 
 
-def cpart_kernel(pairs_ref, count_ref, g_ref, gpre_ref, gm_ref, values_ref, w_node_ref, cpart_ref, t_ref):
-    micro, rows, feat = g_ref.shape
-    local_spread(pairs_ref, count_ref, values_ref, gm_ref, t_ref, rows // 128)
-    for m, part in enumerate(parts_of(micro * rows, micro)):
+def cpart_kernel(pairs_ref, count_ref, g_ref, gpre_ref, gm_ref, turned_ref, w_node_ref, cpart_ref, t_ref):
+    total, feat = cpart_ref.shape
+    local_spread(pairs_ref, count_ref, turned_ref, gm_ref, t_ref, total // 256)
+    for m, part in enumerate(parts_of(total, 2)):
         back = nt_dot(gpre_ref[part, :], w_node_ref[...])
         for b, at, cols in wide_blocks(part, m, feat):
             here = slice(b * 128, (b + 1) * 128)
-            cpart_ref[at, :] = g_ref[m, here, :].astype(F32) + back[here] + t_ref[b, :, cols]
+            g = g_ref[m, here, :] if len(g_ref.shape) == 3 else g_ref[at, :]
+            cpart_ref[at, :] = g.astype(F32) + back[here] + t_ref[b, :, cols]
 
 
 def order_of(bit, chunks):
@@ -257,20 +296,23 @@
 
 
 def second_kernel(
-    targets_ref, r0, r1, r2, r3, cin_ref, dact_ref, normed_ref, inv_ref, gpn1_ref, gpre1_ref,
-    sums1_ref, w_out_ref, gain_ref, *rest,
+    pairs_ref, count_ref, onehot_ref, r0, r1, r2, r3, cin_ref, dact_ref, normed_ref, inv_ref, gpn1_ref,
+    gpre1_ref, sums1_ref, turned_ref, w_agg_ref, w_out_ref, gain_ref, *rest,
 ):
-    weights = len(rest) > 6
+    weights = len(rest) > 11
     if weights:
         la_ref, lb_ref, lc_ref = rest[:3]
         keep_a, keep_b, send_a, send_b = rest[3:7]
         rest = rest[7:]
-    g_ref, gpn_ref, gpre_ref, sums_ref, onehot_ref, s0_ref = rest[-6:]
+    if weights:
+        far_ref, *rest = rest
+    else:
+        o0, o1, o2, o3, *rest = rest
+    g_ref, gpn_ref, gpre_ref, gm_ref, sums_ref, s0_ref, t_ref = rest
     total, feat = dact_ref.shape
     parts = parts_of(total, 2)
     rows = total // 2
     per_peer = r0.shape[0] // 2
-    onehot_ref[...] = target_onehot(targets_ref, rows)
     gain = gain_ref[...].astype(F32)
     is_last = lax.axis_index("segment") == 1
     for m, part in enumerate(parts):
@@ -298,15 +340,31 @@
     gain_sum = jnp.where(is_last, sums1_ref[1:2, :], gain_sum)
     sums = jnp.concatenate([bias_sum, gain_sum, jnp.zeros((EXTRA - 2, feat), F32)], 0)
     sums_ref[...] = sums
+    for m, part in enumerate(parts):
+        gm = nt_dot(gpre_ref[part, :], w_agg_ref[...]).astype(BF16)
+        for b, at, cols in wide_blocks(part, m, feat):
+            gm_ref[b, :, cols] = gm[b * 128 : (b + 1) * 128]
+    halo_spread(pairs_ref, count_ref, turned_ref, gm_ref, t_ref, rows // 128)
     if not weights:
+        put_halo_grads(t_ref, (o0, o1, o2, o3))
         return
     n = keep_a.shape[0]
     na, nb = keep_a.shape[1], keep_b.shape[1]
     half = lb_ref.shape[0] // (2 * n)
     share = 2 * half
+    ride = 2 * per_peer
+    at_a, at_b = n * na, n * nb
+    put_halo_grads(
+        t_ref,
+        (
+            send_a.at[pl.ds(at_a, ride), :], send_a.at[pl.ds(at_a + ride, ride), :],
+            send_b.at[pl.ds(at_b, ride), :], far_ref,
+        ),
+    )
+    send_b[at_b + ride :, :] = send_a[at_a + ride :, :]
     mid = n * na
     keep_a[...] = nn_dot(la_ref[:mid, :], gpre_ref[...]).reshape(n, na, feat)
-    send_a[...] = nn_dot(la_ref[mid:, :], gpre_ref[...]).astype(BF16)
+    send_a[:mid, :] = nn_dot(la_ref[mid:, :], gpre_ref[...]).astype(BF16)
     for base, fill in (
         (0, lambda i, lo, v: put(keep_b, i, lo, v)),
         (n, lambda i, lo, v: put_flat(send_b, nb, i, lo, v)),
@@ -327,45 +385,29 @@
     ref[i * n + lo : i * n + lo + v.shape[0], :] = v.astype(ref.dtype)
 
 
-def tail_kernel(
-    pairs_ref, count_ref, g_ref, gpre_ref, values_ref, w_node_ref, w_agg_ref, o0, o1, o2, o3, cpart_ref,
-    gm_ref, t_ref, th_ref,
-):
-    total, feat = g_ref.shape
-    row_blocks = total // 256
-    parts = parts_of(total, 2)
-    for m, part in enumerate(parts):
-        gm = nt_dot(gpre_ref[part, :], w_agg_ref[...]).astype(BF16)
-        for b, at, cols in wide_blocks(part, m, feat):
-            gm_ref[b, :, cols] = gm[b * 128 : (b + 1) * 128]
-    halo_spread(pairs_ref, count_ref, values_ref, gm_ref, th_ref, row_blocks)
-    put_halo_grads(th_ref, (o0, o1, o2, o3))
-    local_spread(pairs_ref, count_ref, values_ref, gm_ref, t_ref, row_blocks)
-    for m, part in enumerate(parts):
-        back = nt_dot(gpre_ref[part, :], w_node_ref[...])
-        for b, at, cols in wide_blocks(part, m, feat):
-            cpart_ref[at, :] = (
-                g_ref[at, :].astype(F32) + back[b * 128 : (b + 1) * 128] + t_ref[b, :, cols]
-            )
-
-
-def halve_kernel(bits, riders, keep_a, keep_b, recv_a, recv_b, *rest):
-    extra, (keep_a2, keep_b2, send_a2, send_b2) = rest[:riders], rest[riders:]
-    jobs = (
-        (bits[0], keep_a, recv_a, keep_a2, send_a2, extra[:1]),
-        (bits[1], keep_b, recv_b, keep_b2, send_b2, extra[1:]),
-    )
-    for bit, keep, recv, keep2, send2, ride in jobs:
+def halve_kernel(bits, keep_a, keep_b, recv_a, recv_b, *rest):
+    keep_a2, keep_b2, send_a2, send_b2 = rest[-4:]
+    for bit, keep, recv, keep2, send2 in (
+        (bits[0], keep_a, recv_a, keep_a2, send_a2),
+        (bits[1], keep_b, recv_b, keep_b2, send_b2),
+    ):
         n, rows, _ = keep2.shape
         mine = dom_bit(bit)
         for i in range(n):
             d, o = 2 * i + mine, 2 * i + 1 - mine
+            at = pl.ds(pl.multiple_of(o * rows, 8), rows)
+            send2[i * rows : (i + 1) * rows, :] = (keep[o] + recv[at, :].astype(F32)).astype(BF16)
             at = pl.ds(pl.multiple_of(d * rows, 8), rows)
             keep2[i] = keep[d] + recv[at, :].astype(F32)
-            at = pl.ds(pl.multiple_of(o * rows, 8), rows)
-            send2[i * rows : (i + 1) * rows, :] = (keep[o] + recv[at, :].astype(F32)).astype(BF16)
-        for r in ride:
-            send2[n * rows :, :] = r[...]
+        carried = send2.shape[0] - n * rows
+        if carried:
+            send2[n * rows :, :] = recv[recv.shape[0] - carried :, :]
+
+
+def join_kernel(far_ref, recv_ref, out_ref):
+    n = far_ref.shape[0]
+    out_ref[:n, :] = far_ref[...]
+    out_ref[n:, :] = recv_ref[recv_ref.shape[0] - n :, :]
 
 
 def last_kernel(keep_a, keep_b, recv_a, recv_b, node_ref, agg_ref, out_ref, bias_ref, gain_ref):
@@ -381,9 +423,12 @@
     gain_ref[...] = b[half + share + 1 : half + share + 2]
 
 
-def cot_kernel(skips, targets_ref, r0, r1, r2, r3, cpart_ref, other_ref, cot_ref):
+def cot_kernel(skips, onehot_ref, *rest):
+    *sources, cpart_ref, other_ref, cot_ref = rest
     micro, rows, feat = cot_ref.shape
     is_last = lax.axis_index("segment") == 1
+    n = onehot_ref.shape[1] // PEERS
+    near = dom_bit(0) != dom_bit(1)
 
     @pl.when(is_last)
     def _():
@@ -392,13 +437,14 @@
 
     @pl.when(jnp.logical_not(is_last))
     def _():
-        onehot = target_onehot(targets_ref, rows)
-        n = onehot.shape[1] // PEERS
         for m in range(micro):
-            ret = jnp.concatenate(
-                [r[s + m * n : s + (m + 1) * n, :] for r, s in zip((r0, r1, r2, r3), skips)], 0
-            )
-            cot_ref[m] = (cpart_ref[m * rows : (m + 1) * rows, :] + nn_dot(onehot, ret)).astype(BF16)
+            got = [r[s + m * n : s + (m + 1) * n, :] for r, s in zip(sources, skips)]
+            if len(got) > PEERS:
+                got[1] = jnp.where(near, got[1], got.pop())
+            ret = jnp.concatenate(got, 0)
+            cot_ref[m] = (
+                cpart_ref[m * rows : (m + 1) * rows, :] + nn_dot(onehot_ref[...], ret)
+            ).astype(BF16)
 
 
 def whole_kernel(x_ref, agg_ref, hidden_ref, gpn_ref, gpre_ref, node_ref, agg_out, out_ref):
@@ -453,27 +499,35 @@
             [(2 * p + s, 2 * swap_partner(p, k) + d) for p in range(peers) for s, d in cores],
         )
 
-    def across(v, src, dst):
-        return lax.ppermute(
-            v, ("dom", "segment"), [(2 * p + src, 2 * p + dst) for p in range(peers)]
-        )
+    def across(v):
+        return lax.ppermute(v, "segment", [(0, 1), (1, 0)])
 
     def flipped(v, bit):
         return lax.ppermute(v, "dom", [(p, p ^ (1 << bit)) for p in range(peers)])
 
     f_full, b_full = shape((total, feat), F32), shape((total, feat), BF16)
     s_sums = shape((EXTRA, feat), F32)
-    outgoing = call(gather_kernel, [chunk] * slots, [], matmul // 8, 2 * size, send_rows, x)
-    halos = [swapped(v, k, ((0, 0), (1, 1))) for k, v in enumerate(outgoing)]
-    z, acc = call(
+    dma = pltpu.SemaphoreType.DMA
+    *outgoing, x, onehot = call(
+        gather_kernel,
+        [chunk] * slots + [shape(x.shape, BF16), shape((rows, slots * per_peer), BF16)],
+        [pltpu.VMEM(send_rows.shape, jnp.int32), dma((2,))],
+        matmul // 8, 2 * size, send_rows, x,
+        raw=2,
+    )
+    same, other_core = ((0, 0), (1, 1)), ((0, 1), (1, 0))
+    w_other = across(w_n)
+    halos = [swapped(v, k, same) for k, v in enumerate(outgoing)]
+    gm_shape = (row_blocks, 128, wide)
+    loaded = (values, values, w_n, w_a, w_o, gain, out_cot)
+    z, acc, values, turned_values, w_n, w_a, w_o, gain, g_last = call(
         node_kernel,
-        [f_full, shape((row_blocks, 128, wide), F32)],
-        [pltpu.VMEM((row_blocks, 128, wide), BF16)],
+        [f_full, shape(gm_shape, F32)] + [shape(v.shape, BF16) for v in loaded],
+        [pltpu.VMEM(gm_shape, BF16), pltpu.VMEM(bias.shape, BF16), dma((7,))],
         2 * matmul, 8 * size,
-        pairs, blk_count, x, values, w_n, bias,
-        scalars=2,
-    )
-    gm_shape = (row_blocks, 128, wide)
+        pairs, blk_count, values, w_n, bias, w_a, w_o, gain, out_cot, x,
+        scalars=2, raw=7,
+    )
     first = call(
         first_kernel,
         [chunk] * slots
@@ -486,23 +540,23 @@
             pltpu.VMEM((1, 128, wide), F32),
         ],
         4 * matmul, 20 * size,
-        pairs, blk_count, *halos, values, z, acc, out_cot, w_a, w_o, gain,
+        pairs, blk_count, *halos, values, turned_values, z, acc, g_last, w_a, w_o, gain,
         scalars=2,
     )
     to_return = first[:slots]
     gm1, dact, normed, inv_std, agg, hidden, gpn1, gpre1, sums1 = first[slots:]
-    returned = [swapped(v, k, ((1, 0),)) for k, v in enumerate(to_return)]
-    cpart1 = call(
+    returned = [swapped(v, k, other_core) for k, v in enumerate(to_return)]
+    c_in = call(
         cpart_kernel, f_full, [pltpu.VMEM(gm_shape, F32)], matmul, 10 * size,
-        pairs, blk_count, out_cot, gpre1, gm1, values, w_n,
+        pairs, blk_count, g_last, across(gpre1), across(gm1), turned_values, w_other,
         scalars=2,
     )
-    c_in = across(cpart1, 1, 0)
     share = feat // peers
     half = share // 2
     na, nb = share + half, share + half + EXTRA
     halving = peers == 8
-    turned, second_outs = [], []
+    turned, second_outs = [], [chunk] * slots
+    ride = chunk.shape[0]
     if halving:
         turned = call(
             functools.partial(turn_kernel, peers),
@@ -513,50 +567,55 @@
         )
         second_outs = [
             shape((4, na, feat), F32), shape((4, nb, feat), F32),
-            shape((4 * na, feat), BF16), shape((4 * nb, feat), BF16),
+            shape((4 * na + 2 * ride, feat), BF16), shape((4 * nb + 2 * ride, feat), BF16),
+            chunk,
         ]
     second = call(
         second_kernel,
-        second_outs + [b_full, b_full, b_full, s_sums],
-        [pltpu.VMEM((rows, slots * per_peer), BF16), pltpu.VMEM((total, feat), F32)],
-        4 * matmul, 20 * size,
-        send_rows, *returned, c_in, dact, normed, inv_std, gpn1, gpre1, sums1, w_o, gain, *turned,
-    )
-    g_low, gpn, gpre, sums = second[-4:]
+        second_outs + [b_full, b_full, b_full, shape(gm_shape, BF16), s_sums],
+        [pltpu.VMEM((total, feat), F32), pltpu.VMEM((1, 128, wide), F32)],
+        5 * matmul, 20 * size,
+        pairs, blk_count, onehot, *returned, c_in, dact, normed, inv_std, gpn1, gpre1, sums1,
+        turned_values, w_a, w_o, gain, *turned,
+        scalars=2,
+    )
+    g_low, gpn, gpre, gm, sums = second[-5:]
     if halving:
-        keep_a, keep_b, send_a, send_b = second[:4]
+        keep_a, keep_b, send_a, send_b, far = second[:5]
         recv_a, recv_b = flipped(send_a, 0), flipped(send_b, 1)
-    tail = call(
-        tail_kernel,
-        [chunk] * slots + [f_full],
-        [pltpu.VMEM(gm_shape, BF16), pltpu.VMEM(gm_shape, F32), pltpu.VMEM((1, 128, wide), F32)],
-        2 * matmul, 12 * size,
-        pairs, blk_count, g_low, gpre, values, w_n, w_a,
+    cpart0 = call(
+        cpart_kernel, f_full, [pltpu.VMEM(gm_shape, F32)], matmul, 10 * size,
+        pairs, blk_count, g_low, gpre, gm, turned_values, w_n,
         scalars=2,
     )
-    to_return, cpart0 = tail[:slots], tail[slots]
-    other = across(g_low, 0, 1)
-    same = ((0, 0),)
+    other = across(g_low)
+    cot_out = shape((micro, rows, feat), BF16)
     if halving:
-        back_b, back_d = swapped(to_return[1], 1, same), swapped(to_return[3], 3, same)
-        ride = chunk.shape[0]
+        back_a, back_c = recv_a, recv_b
+        far = call(join_kernel, shape((2 * ride, feat), BF16), [], size, size // 4, far, recv_a)
         keep_a, keep_b, send_a, send_b = call(
-            functools.partial(halve_kernel, (1, 0), 2),
+            functools.partial(halve_kernel, (1, 0)),
             [
                 shape((2, na, feat), F32), shape((2, nb, feat), F32),
-                shape((2 * na + ride, feat), BF16), shape((2 * nb + ride, feat), BF16),
+                shape((2 * na, feat), BF16), shape((2 * nb + ride, feat), BF16),
             ],
-            [], size, 8 * size, keep_a, keep_b, recv_a, recv_b, to_return[2], to_return[0],
+            [], size, 8 * size, keep_a, keep_b, recv_a, recv_b,
         )
         recv_a, recv_b = flipped(send_a, 1), flipped(send_b, 0)
-        returned, skips = (recv_b, back_b, recv_a, back_d), (2 * nb, 0, 2 * na, 0)
+        far = swapped(far, 3, same)
+        cot = call(
+            functools.partial(cot_kernel, (4 * na, 2 * nb, 4 * nb, 0, ride)),
+            cot_out, [], matmul // 4, 4 * size,
+            onehot, back_a, recv_b, back_c, far, far, cpart0, other,
+        )
         keep_a, keep_b, send_a, send_b = call(
-            functools.partial(halve_kernel, (2, 2), 0),
+            functools.partial(halve_kernel, (2, 2)),
             [
                 shape((1, na, feat), F32), shape((1, nb, feat), F32),
                 shape((na, feat), BF16), shape((nb, feat), BF16),
             ],
-            [], size, 4 * size, keep_a, keep_b, recv_a, recv_b,
+            [], size, 4 * size, keep_a, keep_b, recv_a, recv_b, cot,
+            after=1,
         )
         recv_a, recv_b = flipped(send_a, 2), flipped(send_b, 2)
         part, row = shape((share, feat), F32), shape((1, feat), F32)
@@ -574,12 +633,11 @@
         ]
         sums = lax.psum(sums, "dom")
         grad_bias, grad_gain = sums[0:1], sums[1:2]
-        returned = [swapped(v, k, same) for k, v in enumerate(to_return)]
-        skips = (0,) * slots
-    cot = call(
-        functools.partial(cot_kernel, skips), shape((micro, rows, feat), BF16), [], matmul // 4, 4 * size,
-        send_rows, *returned, cpart0, other,
-    )
+        returned = [swapped(v, k, same) for k, v in enumerate(second[:slots])]
+        cot = call(
+            functools.partial(cot_kernel, (0,) * slots), cot_out, [], matmul // 4, 4 * size,
+            onehot, *returned, cpart0, other,
+        )
     return (
         cot[None],
         grad_node[None],

time: 73.7 us -> 71.1 us (0.965)
  starting transfers between devices: 28.5 us -> 21.3 us
  waiting for transfers between devices: 22.8 us -> 28 us
  local copies, waits for them, and re-layouts: 5.73 us -> 1.72 us
  Pallas kernels: 14.6 us -> 18 us
    ppermute x6, waiting for transfers between devices: 10.4 us -> 19.8 us  [flipped(): return lax.ppermute(v, 'dom', [(p, p ^ 1 << bit) for p in range(peers)])]
    ppermute x10 -> x9, starting transfers between devices: 19 us -> 14.8 us  [swapped(): lax.ppermute(v, ('dom', 'segment'), [(2 * p + s, 2 * swap_partner(p, k) +...]
    ppermute x10 -> x9, waiting for transfers between devices: 12.3 us -> 8.27 us  [swapped(): lax.ppermute(v, ('dom', 'segment'), [(2 * p + s, 2 * swap_partner(p, k) +...]
    unnamed x28 -> x6, local copies, waits for them, and re-layouts: 5.73 us -> 1.72 us
    pallas_call x11 -> x12, Pallas kernels: 14.6 us -> 18 us  [call(): pl.pallas_call(kernel, out_shape=outs, in_specs=[SMEM] * scalars + [HBM]...]
    ppermute x2 -> x4, starting transfers between devices: 2.6 us -> 0.57 us  [across(): return lax.ppermute(v, 'segment', [(0, 1), (1, 0)])]
    ppermute x6, starting transfers between devices: 6.84 us -> 5.96 us  [flipped(): return lax.ppermute(v, 'dom', [(p, p ^ 1 << bit) for p in range(peers)])]
  transfers between devices with their start and end apart: 18 -> 19, of which waited for: 10 -> 7; matrix products, arithmetic and copies ran while one was open for 0% -> 0% of each run, Pallas kernels for 8% -> 17%
where the time goes in v3:
time: 71.1 us; the launch traced here: 70.5 us
  waiting for transfers between devices  28 us (39%)
  starting transfers between devices  21.3 us (30%)
  Pallas kernels  18 us (25%)
  local copies, waits for them, and re-layouts  1.72 us (2%)
  between operations  1.44 us (2%)
    ppermute x6, waiting for transfers between devices, flipped(): return lax.ppermute(v, 'dom', [(p, p ^ 1 << bit) for p in range(peers)])  19.8 us
    pallas_call x12, Pallas kernels, call(): pl.pallas_call(kernel, out_shape=outs, in_specs=[SMEM] * scalars + [HBM]...  18 us
    ppermute x9, starting transfers between devices, swapped(): lax.ppermute(v, ('dom', 'segment'), [(2 * p + s, 2 * swap_partner(p, k) +...  14.8 us
    ppermute x9, waiting for transfers between devices, swapped(): lax.ppermute(v, ('dom', 'segment'), [(2 * p + s, 2 * swap_partner(p, k) +...  8.27 us
    ppermute x6, starting transfers between devices, flipped(): return lax.ppermute(v, 'dom', [(p, p ^ 1 << bit) for p in range(peers)])  5.96 us
    unnamed x6, local copies, waits for them, and re-layouts  1.72 us
  transfers between devices with their start and end apart: 19, of which 7 were waited for; matrix products, arithmetic and copies ran while one was open for 0% of the time, Pallas kernels for 17%

profile of v3, /device:TPU:0, one launch (start us, length us, event | category | flops | bytes accessed | tf_op | source)
XLA Modules:
  0.0 70.5 jit_solution(13907534285890029051)
XLA Ops:
  0.6 0.0 copy-start.2
  0.6 1.4 %shard_map.154 = (bf16[64,512]{1,0:T(8,128)(2,1)S(1)}, bf16[64,512]{1,0:T(8,128)(2,1)S(1)}, bf16[64,512]{1,0:T(8,128)(2,1)S(1)}, bf16[64,512]{1,0:T(8,128)(2,1)S...) custom-call(s32[1,4,32]{2,1,0:T(4,128)} %targets_hbm.1, bf16[2,256,512]{2,1,0:T(8,128)(2,1)} %bitcast.16), custom_call_target="tpu_custom_call" | custom-call | flops 33554432 | bytes 524288 | tf_op jit(solution)/shard_map/pallas_call | solution.py:43
  2.0 3.0 %collective-permute-start = (bf16[64,512]{1,0:T(8,128)(2,1)S(1)}, bf16[64,512]{1,0:T(8,128)(2,1)S(1)}, u32[]{:S(2)}, u32[]{:S(2)}) collective-permute-start(bf16[64,512]{1,0:T(8,128)(2,1)S(1)} %get-tuple-element.59), channel_id=1, source_target_pairs={{0,2},{1,3},{2,0},{3,1},{4,6},{5,7},{6,4},{7,5},{8,10},{9,11},{10,... | collective-permute-start | bytes 196616 | tf_op jit(solution)/shard_map/ppermute | solution.py:496
  5.0 3.6 %collective-permute-start.1 = (bf16[64,512]{1,0:T(8,128)(2,1)S(1)}, bf16[64,512]{1,0:T(8,128)(2,1)S(1)}, u32[]{:S(2)}, u32[]{:S(2)}) collective-permute-start(bf16[64,512]{1,0:T(8,128)(2,1)S(1)} %get-tuple-element.60), channel_id=1, source_target_pairs={{0,14},{1,15},{2,4},{3,5},{4,2},{5,3},{6,8},{7,9},{8,6},{9,7},{10,... | collective-permute-start | bytes 196616 | tf_op jit(solution)/shard_map/ppermute | solution.py:496
  8.6 0.0 collective-permute-start.2
  8.6 0.9 %collective-permute-start.3 = (bf16[64,512]{1,0:T(8,128)(2,1)S(1)}, bf16[64,512]{1,0:T(8,128)(2,1)S(1)}, u32[]{:S(2)}, u32[]{:S(2)}) collective-permute-start(bf16[64,512]{1,0:T(8,128)(2,1)S(1)} %get-tuple-element.62), channel_id=1, source_target_pairs={{0,12},{1,13},{2,14},{3,15},{4,8},{5,9},{6,10},{7,11},{8,4},{9,5},... | collective-permute-start | bytes 196616 | tf_op jit(solution)/shard_map/ppermute | solution.py:496
  9.5 0.0 collective-permute-start.10
  10.2 0.0 copy-start.1
  10.2 0.7 copy-done.1
  10.9 3.1 %shard_map.155 = (f32[512,512]{1,0:T(8,128)S(1)}, f32[2,128,1024]{2,1,0:T(8,128)S(1)}, bf16[7,128,128]{2,1,0:T(8,128)(2,1)S(1)}, bf16[7,128,128]{2,1,0:T(8,128)(...) custom-call(s32[2,7]{1,0:T(2,128)S(1)} %bitcast.11, ...), custom_call_target="tpu_custom_call" | custom-call | flops 536870912 | bytes 2097152 | tf_op jit(solution)/shard_map/pallas_call | solution.py:43
  14.0 0.0 collective-permute-done.h0
  14.0 0.0 collective-permute-done.2.h2
  14.0 0.8 %collective-permute-done.3.h3 = bf16[64,512]{1,0:T(8,128)(2,1)S(1)} collective-permute-done((bf16[64,512]{1,0:T(8,128)(2,1)S(1)}, bf16[64,512]{1,0:T(8,128)(2,1)S(1)}, u32[]{:S(2)}, u32[]{:S(2)}) %collective-permute-start.3) | collective-permute-done | bytes 65568 | tf_op jit(solution)/shard_map/ppermute | solution.py:496
  14.8 3.3 %shard_map.156 = (bf16[64,512]{1,0:T(8,128)(2,1)S(1)}, bf16[64,512]{1,0:T(8,128)(2,1)S(1)}, bf16[64,512]{1,0:T(8,128)(2,1)S(1)}, bf16[64,512]{1,0:T(8,128)(2,1)S...) custom-call(s32[2,7]{1,0:T(2,128)S(1)} %bitcast.12, ...), custom_call_target="tpu_custom_call" | custom-call | flops 1073741824 | bytes 5242880 | tf_op jit(solution)/shard_map/pallas_call | solution.py:43
  18.1 0.1 collective-permute-start.9
  18.2 0.5 collective-permute-start.8
  18.7 1.8 %collective-permute-start.4 = (bf16[64,512]{1,0:T(8,128)(2,1)S(1)}, bf16[64,512]{1,0:T(8,128)(2,1)S(1)}, u32[]{:S(2)}, u32[]{:S(2)}) collective-permute-start(bf16[64,512]{1,0:T(8,128)(2,1)S(1)} %get-tuple-element.72), channel_id=1, source_target_pairs={{0,3},{1,2},{2,1},{3,0},{4,7},{5,6},{6,5},{7,4},{8,11},{9,10},{10,... | collective-permute-start | bytes 196616 | tf_op jit(solution)/shard_map/ppermute | solution.py:496
  20.4 1.4 %collective-permute-start.5 = (bf16[64,512]{1,0:T(8,128)(2,1)S(1)}, bf16[64,512]{1,0:T(8,128)(2,1)S(1)}, u32[]{:S(2)}, u32[]{:S(2)}) collective-permute-start(bf16[64,512]{1,0:T(8,128)(2,1)S(1)} %get-tuple-element.73), channel_id=1, source_target_pairs={{0,15},{1,14},{2,5},{3,4},{4,3},{5,2},{6,9},{7,8},{8,7},{9,6},{10,... | collective-permute-start | bytes 196616 | tf_op jit(solution)/shard_map/ppermute | solution.py:496
  21.9 0.0 collective-permute-start.6
  21.9 0.0 collective-permute-done.9.gm_ref
  21.9 2.7 %collective-permute-start.7 = (bf16[64,512]{1,0:T(8,128)(2,1)S(1)}, bf16[64,512]{1,0:T(8,128)(2,1)S(1)}, u32[]{:S(2)}, u32[]{:S(2)}) collective-permute-start(bf16[64,512]{1,0:T(8,128)(2,1)S(1)} %get-tuple-element.75), channel_id=1, source_target_pairs={{0,13},{1,12},{2,15},{3,14},{4,9},{5,8},{6,11},{7,10},{8,5},{9,4},... | collective-permute-start | bytes 196616 | tf_op jit(solution)/shard_map/ppermute | solution.py:496
  24.6 0.6 shard_map.158
  25.2 0.0 collective-permute-done.8.gpre_ref
  25.2 1.8 %shard_map.157.cin_ref = f32[512,512]{1,0:T(8,128)S(1)} custom-call(s32[2,7]{1,0:T(2,128)S(1)} %bitcast.13, s32[1]{0:T(128)S(6)} %copy.17.count_ref, bf16[2,256,512]{2,1,0:T(8,128)(2,1)S(1)} %get-tuple-element.68.g_ref, bf16[512,512]{1,0:T(8,128)(2,1)S(1)} %collective-permute-done.8.gpre_ref, bf16[2,128,1024]{2,1,0:T(8,128)(2,1)S(1)} %collective-permute-done.9.gm_ref, ...), custom_call_target="tpu_custom_call" | custom-call | flops 268435456 | bytes 2621440 | tf_op jit(solution)/shard_map/pallas_call | solution.py:43
  27.0 0.0 collective-permute-done.4.r0
  27.0 0.3 collective-permute-done.5.r1
  27.4 0.0 collective-permute-done.6.r2
  27.4 2.3 %collective-permute-done.7.r3 = bf16[64,512]{1,0:T(8,128)(2,1)S(1)} collective-permute-done((bf16[64,512]{1,0:T(8,128)(2,1)S(1)}, bf16[64,512]{1,0:T(8,128)(2,1)S(1)}, u32[]{:S(2)}, u32[]{:S(2)}) %collective-permute-start.7) | collective-permute-done | bytes 65568 | tf_op jit(solution)/shard_map/ppermute | solution.py:496
  29.7 3.9 %shard_map.159 = (f32[4,96,512]{2,1,0:T(8,128)S(1)}, f32[4,104,512]{2,1,0:T(8,128)S(1)}, bf16[512,512]{1,0:T(8,128)(2,1)S(1)}, bf16[544,512]{1,0:T(8,128)(2,1)S(...) custom-call(s32[2,7]{1,0:T(2,128)S(1)} %bitcast.14, ...), custom_call_target="tpu_custom_call" | custom-call | flops 1342177280 | bytes 5242880 | tf_op jit(solution)/shard_map/pallas_call | solution.py:43
  33.6 0.0 collective-permute-start.12
  33.6 0.9 %collective-permute-start.11 = (bf16[512,512]{1,0:T(8,128)(2,1)S(1)}, bf16[512,512]{1,0:T(8,128)(2,1)S(1)}, u32[]{:S(2)}, u32[]{:S(2)}) collective-permute-start(bf16[512,512]{1,0:T(8,128)(2,1)S(1)} %get-tuple-element.88), channel_id=1, source_target_pairs={{0,2},{2,0},{4,6},{6,4},{8,10},{10,8},{12,14},{14,12},{1,3},{3,1},... | collective-permute-start | bytes 1572872 | tf_op jit(solution)/shard_map/ppermute | solution.py:506
  34.6 0.0 collective-permute-start.15
  34.6 13.0 %collective-permute-done.11.recv_a.recv_ref.rest_0_ = bf16[512,512]{1,0:T(8,128)(2,1)S(1)} collective-permute-done((bf16[512,512]{1,0:T(8,128)(2,1)S(1)}, bf16[512,512]{1,0:T(8,128)(2,1)S(1)}, u32[]{:S(2)}, u32[]{:S(2)}) %collective-permute-start.11) | collective-permute-done | bytes 524320 | tf_op jit(solution)/shard_map/ppermute | solution.py:506
  47.6 0.7 collective-permute-done.12.recv_b.rest_2_
  48.3 0.2 shard_map.160
  48.5 1.0 %collective-permute-start.13 = (bf16[272,512]{1,0:T(8,128)(2,1)S(1)}, bf16[272,512]{1,0:T(8,128)(2,1)S(1)}, u32[]{:S(2)}, u32[]{:S(2)}) collective-permute-start(bf16[272,512]{1,0:T(8,128)(2,1)S(1)} %get-tuple-element.92), channel_id=1, source_target_pairs={{0,2},{2,0},{4,6},{6,4},{8,10},{10,8},{12,14},{14,12},{1,3},{3,1},... | collective-permute-start | bytes 835592 | tf_op jit(solution)/shard_map/ppermute | solution.py:506
  49.5 1.0 %collective-permute-start.16 = (bf16[192,512]{1,0:T(8,128)(2,1)S(1)}, bf16[192,512]{1,0:T(8,128)(2,1)S(1)}, u32[]{:S(2)}, u32[]{:S(2)}) collective-permute-start(bf16[192,512]{1,0:T(8,128)(2,1)S(1)} %get-tuple-element.100), channel_id=1, source_target_pairs={{0,4},{2,6},{4,0},{6,2},{8,12},{10,14},{12,8},{14,10},{1,5},{3,7},... | collective-permute-start | bytes 589832 | tf_op jit(solution)/shard_map/ppermute | solution.py:506
  50.5 1.4 %collective-permute-start.14 = (bf16[128,512]{1,0:T(8,128)(2,1)S(1)}, bf16[128,512]{1,0:T(8,128)(2,1)S(1)}, u32[]{:S(2)}, u32[]{:S(2)}) collective-permute-start(bf16[128,512]{1,0:T(8,128)(2,1)S(1)} %shard_map.161), channel_id=1, source_target_pairs={{0,12},{1,13},{2,14},{3,15},{4,8},{5,9},{6,10},{7,11},{8,4},{9,5},... | collective-permute-start | bytes 393224 | tf_op jit(solution)/shard_map/ppermute | solution.py:496
  51.9 1.8 %shard_map.162.rest_5_ = f32[512,512]{1,0:T(8,128)S(1)} custom-call(s32[2,7]{1,0:T(2,128)S(1)} %bitcast.15, s32[1]{0:T(128)S(6)} %copy.17.count_ref, bf16[512,512]{1,0:T(8,128)(2,1)S(1)} %get-tuple-element.94.g_ref, bf16[512,512]{1,0:T(8,128)(2,1)S(1)} %get-tuple-element.95.gpre_ref, bf16[2,128,1024]{2,1,0:T(8,128)(2,1)S(1)} %get-tuple-element.96.gm_ref, ...), custom_call_target="tpu_custom_call" | custom-call | flops 268435456 | bytes 2621440 | tf_op jit(solution)/shard_map/pallas_call | solution.py:43
  53.7 4.8 %collective-permute-done.14.rest_3_.rest_4_ = bf16[128,512]{1,0:T(8,128)(2,1)S(1)} collective-permute-done((bf16[128,512]{1,0:T(8,128)(2,1)S(1)}, bf16[128,512]{1,0:T(8,128)(2,1)S(1)}, u32[]{:S(2)}, u32[]{:S(2)}) %collective-permute-start.14) | collective-permute-done | bytes 131104 | tf_op jit(solution)/shard_map/ppermute | solution.py:496
  58.5 1.1 %shard_map.163.rest_0_ = bf16[2,256,512]{2,1,0:T(8,128)(2,1)} custom-call(bf16[256,128]{1,0:T(8,128)(2,1)S(1)} %get-tuple-element.58.onehot_ref, bf16[512,512]{1,0:T(8,128)(2,1)S(1)} %collective-permute-done.11.recv_a.recv_ref.rest_0_, bf16[272,512]{1,0:T(8,128)(2,1)S(1)} %collective-permute-done.13.rest_1_.recv_b, ...), custom_call_target="tpu_custom_call" | custom-call | flops 67108864 | bytes 1048576 | tf_op jit(solution)/shard_map/pallas_call | solution.py:43
  59.6 1.0 %copy-done = bf16[2,256,512]{2,1,0:T(8,128)(2,1)S(1)} copy-done((bf16[2,256,512]{2,1,0:T(8,128)(2,1)S(1)}, bf16[2,256,512]{2,1,0:T(8,128)(2,1)}, u32[]{:S(2)}) %copy-start) | copy-done | bytes 524312
  60.6 0.1 shard_map.164
  60.7 0.1 collective-permute-start.18
  60.8 2.9 %collective-permute-start.17 = (bf16[96,512]{1,0:T(8,128)(2,1)S(1)}, bf16[96,512]{1,0:T(8,128)(2,1)S(1)}, u32[]{:S(2)}, u32[]{:S(2)}) collective-permute-start(bf16[96,512]{1,0:T(8,128)(2,1)S(1)} %get-tuple-element.103), channel_id=1, source_target_pairs={{0,8},{2,10},{4,12},{6,14},{8,0},{10,2},{12,4},{14,6},{1,9},{3,11}... | collective-permute-start | bytes 294920 | tf_op jit(solution)/shard_map/ppermute | solution.py:506
  63.7 6.0 %collective-permute-done.17.recv_a = bf16[96,512]{1,0:T(8,128)(2,1)S(1)} collective-permute-done((bf16[96,512]{1,0:T(8,128)(2,1)S(1)}, bf16[96,512]{1,0:T(8,128)(2,1)S(1)}, u32[]{:S(2)}, u32[]{:S(2)}) %collective-permute-start.17) | collective-permute-done | bytes 98336 | tf_op jit(solution)/shard_map/ppermute | solution.py:506
  69.7 0.0 collective-permute-done.18.recv_b
  69.7 0.8 %shard_map.165 = (f32[64,512]{1,0:T(8,128)}, f32[64,512]{1,0:T(8,128)}, f32[64,512]{1,0:T(8,128)}, f32[1,512]{1,0:T(1,128)}, f32[1,512]{1,0:T(1,128)}) custom-call(f32[1,96,512]{2,1,0:T(8,128)S(1)} %get-tuple-element.101.keep_a, f32[1,104,512]{2,1,0:T(8,128)S(1)} %get-tuple-element.102.keep_b, bf16[96,512]{1,0:T(8,128)(2,1)S(1)} %collective-permute-done.17.recv_a, ...), custom_call_target="tpu_custom_call" | custom-call | flops 262144 | bytes 524288 | tf_op jit(solution)/shard_map/pallas_call | solution.py:43
  (8 shorter events, 0.0 us)
Async XLA Ops:
  0.6 8.9 %copy-start.2 = (bf16[1,512,512]{2,1,0:T(8,128)(2,1)S(1)}, bf16[1,512,512]{2,1,0:T(8,128)(2,1)}, u32[]{:S(2)}) copy-start(bf16[1,512,512]{2,1,0:T(8,128)(2,1)} %param.13) | copy-start | bytes 1572868
  2.0 11.9 %collective-permute-start = (bf16[64,512]{1,0:T(8,128)(2,1)S(1)}, bf16[64,512]{1,0:T(8,128)(2,1)S(1)}, u32[]{:S(2)}, u32[]{:S(2)}) collective-permute-start(bf16[64,512]{1,0:T(8,128)(2,1)S(1)} %get-tuple-element.59), channel_id=1, source_target_pairs={{0,2},{1,3},{2,0},{3,1},{4,6},{5,7},{6,4},{7,5},{8,10},{9,11},{10,... | collective-permute-start | bytes 196616 | tf_op jit(solution)/shard_map/ppermute | solution.py:496
  5.0 8.9 %collective-permute-start.1 = (bf16[64,512]{1,0:T(8,128)(2,1)S(1)}, bf16[64,512]{1,0:T(8,128)(2,1)S(1)}, u32[]{:S(2)}, u32[]{:S(2)}) collective-permute-start(bf16[64,512]{1,0:T(8,128)(2,1)S(1)} %get-tuple-element.60), channel_id=1, source_target_pairs={{0,14},{1,15},{2,4},{3,5},{4,2},{5,3},{6,8},{7,9},{8,6},{9,7},{10,... | collective-permute-start | bytes 196616 | tf_op jit(solution)/shard_map/ppermute | solution.py:496
  8.6 5.4 %collective-permute-start.2 = (bf16[64,512]{1,0:T(8,128)(2,1)S(1)}, bf16[64,512]{1,0:T(8,128)(2,1)S(1)}, u32[]{:S(2)}, u32[]{:S(2)}) collective-permute-start(bf16[64,512]{1,0:T(8,128)(2,1)S(1)} %get-tuple-element.61), channel_id=1, source_target_pairs={{0,4},{1,5},{2,6},{3,7},{4,0},{5,1},{6,2},{7,3},{8,12},{9,13},{10,... | collective-permute-start | bytes 196616 | tf_op jit(solution)/shard_map/ppermute | solution.py:496
  8.6 6.2 %collective-permute-start.3 = (bf16[64,512]{1,0:T(8,128)(2,1)S(1)}, bf16[64,512]{1,0:T(8,128)(2,1)S(1)}, u32[]{:S(2)}, u32[]{:S(2)}) collective-permute-start(bf16[64,512]{1,0:T(8,128)(2,1)S(1)} %get-tuple-element.62), channel_id=1, source_target_pairs={{0,12},{1,13},{2,14},{3,15},{4,8},{5,9},{6,10},{7,11},{8,4},{9,5},... | collective-permute-start | bytes 196616 | tf_op jit(solution)/shard_map/ppermute | solution.py:496
  9.5 12.4 %collective-permute-start.10 = (bf16[512,512]{1,0:T(8,128)(2,1)S(1)}, bf16[512,512]{1,0:T(8,128)(2,1)S(1)}, u32[]{:S(2)}, u32[]{:S(2)}) collective-permute-start(bf16[512,512]{1,0:T(8,128)(2,1)S(1)} %bitcast.20), channel_id=1, source_target_pairs={{0,1},{1,0},{2,3},{3,2},{4,5},{5,4},{6,7},{7,6},{8,9},{9,8},{10,11... | collective-permute-start | bytes 1572872 | tf_op jit(solution)/shard_map/ppermute | solution.py:503
  10.2 0.7 copy-start.1
  18.1 3.8 %collective-permute-start.9 = (bf16[2,128,1024]{2,1,0:T(8,128)(2,1)S(1)}, bf16[2,128,1024]{2,1,0:T(8,128)(2,1)S(1)}, u32[]{:S(2)}, u32[]{:S(2)}) collective-permute-start(bf16[2,128,1024]{2,1,0:T(8,128)(2,1)S(1)} %get-tuple-element.77), channel_id=1, source_target_pairs={{0,1},{1,0},{2,3},{3,2},{4,5},{5,4},{6,7},{7,6},{8,9},{9,8},{10,11... | collective-permute-start | bytes 1572872 | tf_op jit(solution)/shard_map/ppermute | solution.py:503
  18.2 7.1 %collective-permute-start.8 = (bf16[512,512]{1,0:T(8,128)(2,1)S(1)}, bf16[512,512]{1,0:T(8,128)(2,1)S(1)}, u32[]{:S(2)}, u32[]{:S(2)}) collective-permute-start(bf16[512,512]{1,0:T(8,128)(2,1)S(1)} %get-tuple-element.76.gpre1_ref), channel_id=1, source_target_pairs={{0,1},{1,0},{2,3},{3,2},{4,5},{5,4},{6,7},{7,6},{8,9},{9,8},{10,11... | collective-permute-start | bytes 1572872 | tf_op jit(solution)/shard_map/ppermute | solution.py:503
  18.7 8.4 %collective-permute-start.4 = (bf16[64,512]{1,0:T(8,128)(2,1)S(1)}, bf16[64,512]{1,0:T(8,128)(2,1)S(1)}, u32[]{:S(2)}, u32[]{:S(2)}) collective-permute-start(bf16[64,512]{1,0:T(8,128)(2,1)S(1)} %get-tuple-element.72), channel_id=1, source_target_pairs={{0,3},{1,2},{2,1},{3,0},{4,7},{5,6},{6,5},{7,4},{8,11},{9,10},{10,... | collective-permute-start | bytes 196616 | tf_op jit(solution)/shard_map/ppermute | solution.py:496
  20.4 6.9 %collective-permute-start.5 = (bf16[64,512]{1,0:T(8,128)(2,1)S(1)}, bf16[64,512]{1,0:T(8,128)(2,1)S(1)}, u32[]{:S(2)}, u32[]{:S(2)}) collective-permute-start(bf16[64,512]{1,0:T(8,128)(2,1)S(1)} %get-tuple-element.73), channel_id=1, source_target_pairs={{0,15},{1,14},{2,5},{3,4},{4,3},{5,2},{6,9},{7,8},{8,7},{9,6},{10,... | collective-permute-start | bytes 196616 | tf_op jit(solution)/shard_map/ppermute | solution.py:496
  21.9 5.5 %collective-permute-start.6 = (bf16[64,512]{1,0:T(8,128)(2,1)S(1)}, bf16[64,512]{1,0:T(8,128)(2,1)S(1)}, u32[]{:S(2)}, u32[]{:S(2)}) collective-permute-start(bf16[64,512]{1,0:T(8,128)(2,1)S(1)} %get-tuple-element.74), channel_id=1, source_target_pairs={{0,5},{1,4},{2,7},{3,6},{4,1},{5,0},{6,3},{7,2},{8,13},{9,12},{10,... | collective-permute-start | bytes 196616 | tf_op jit(solution)/shard_map/ppermute | solution.py:496
  21.9 7.8 %collective-permute-start.7 = (bf16[64,512]{1,0:T(8,128)(2,1)S(1)}, bf16[64,512]{1,0:T(8,128)(2,1)S(1)}, u32[]{:S(2)}, u32[]{:S(2)}) collective-permute-start(bf16[64,512]{1,0:T(8,128)(2,1)S(1)} %get-tuple-element.75), channel_id=1, source_target_pairs={{0,13},{1,12},{2,15},{3,14},{4,9},{5,8},{6,11},{7,10},{8,5},{9,4},... | collective-permute-start | bytes 196616 | tf_op jit(solution)/shard_map/ppermute | solution.py:496
  33.6 14.6 %collective-permute-start.12 = (bf16[544,512]{1,0:T(8,128)(2,1)S(1)}, bf16[544,512]{1,0:T(8,128)(2,1)S(1)}, u32[]{:S(2)}, u32[]{:S(2)}) collective-permute-start(bf16[544,512]{1,0:T(8,128)(2,1)S(1)} %get-tuple-element.91), channel_id=1, source_target_pairs={{0,4},{2,6},{4,0},{6,2},{8,12},{10,14},{12,8},{14,10},{1,5},{3,7},... | collective-permute-start | bytes 1671176 | tf_op jit(solution)/shard_map/ppermute | solution.py:506
  33.6 13.9 %collective-permute-start.11 = (bf16[512,512]{1,0:T(8,128)(2,1)S(1)}, bf16[512,512]{1,0:T(8,128)(2,1)S(1)}, u32[]{:S(2)}, u32[]{:S(2)}) collective-permute-start(bf16[512,512]{1,0:T(8,128)(2,1)S(1)} %get-tuple-element.88), channel_id=1, source_target_pairs={{0,2},{2,0},{4,6},{6,4},{8,10},{10,8},{12,14},{14,12},{1,3},{3,1},... | collective-permute-start | bytes 1572872 | tf_op jit(solution)/shard_map/ppermute | solution.py:506
  34.6 19.1 %collective-permute-start.15 = (bf16[512,512]{1,0:T(8,128)(2,1)S(1)}, bf16[512,512]{1,0:T(8,128)(2,1)S(1)}, u32[]{:S(2)}, u32[]{:S(2)}) collective-permute-start(bf16[512,512]{1,0:T(8,128)(2,1)S(1)} %get-tuple-element.94.g_ref), channel_id=1, source_target_pairs={{0,1},{1,0},{2,3},{3,2},{4,5},{5,4},{6,7},{7,6},{8,9},{9,8},{10,11... | collective-permute-start | bytes 1572872 | tf_op jit(solution)/shard_map/ppermute | solution.py:503
  48.5 10.0 %collective-permute-start.13 = (bf16[272,512]{1,0:T(8,128)(2,1)S(1)}, bf16[272,512]{1,0:T(8,128)(2,1)S(1)}, u32[]{:S(2)}, u32[]{:S(2)}) collective-permute-start(bf16[272,512]{1,0:T(8,128)(2,1)S(1)} %get-tuple-element.92), channel_id=1, source_target_pairs={{0,2},{2,0},{4,6},{6,4},{8,10},{10,8},{12,14},{14,12},{1,3},{3,1},... | collective-permute-start | bytes 835592 | tf_op jit(solution)/shard_map/ppermute | solution.py:506
  49.5 10.1 %collective-permute-start.16 = (bf16[192,512]{1,0:T(8,128)(2,1)S(1)}, bf16[192,512]{1,0:T(8,128)(2,1)S(1)}, u32[]{:S(2)}, u32[]{:S(2)}) collective-permute-start(bf16[192,512]{1,0:T(8,128)(2,1)S(1)} %get-tuple-element.100), channel_id=1, source_target_pairs={{0,4},{2,6},{4,0},{6,2},{8,12},{10,14},{12,8},{14,10},{1,5},{3,7},... | collective-permute-start | bytes 589832 | tf_op jit(solution)/shard_map/ppermute | solution.py:506
  50.5 8.0 %collective-permute-start.14 = (bf16[128,512]{1,0:T(8,128)(2,1)S(1)}, bf16[128,512]{1,0:T(8,128)(2,1)S(1)}, u32[]{:S(2)}, u32[]{:S(2)}) collective-permute-start(bf16[128,512]{1,0:T(8,128)(2,1)S(1)} %shard_map.161), channel_id=1, source_target_pairs={{0,12},{1,13},{2,14},{3,15},{4,8},{5,9},{6,10},{7,11},{8,4},{9,5},... | collective-permute-start | bytes 393224 | tf_op jit(solution)/shard_map/ppermute | solution.py:496
  59.6 1.0 %copy-start = (bf16[2,256,512]{2,1,0:T(8,128)(2,1)S(1)}, bf16[2,256,512]{2,1,0:T(8,128)(2,1)}, u32[]{:S(2)}) copy-start(bf16[2,256,512]{2,1,0:T(8,128)(2,1)} %shard_map.163.rest_0_) | copy-start | bytes 1572868
  60.7 9.0 %collective-permute-start.18 = (bf16[104,512]{1,0:T(8,128)(2,1)S(1)}, bf16[104,512]{1,0:T(8,128)(2,1)S(1)}, u32[]{:S(2)}, u32[]{:S(2)}) collective-permute-start(bf16[104,512]{1,0:T(8,128)(2,1)S(1)} %get-tuple-element.104), channel_id=1, source_target_pairs={{0,8},{2,10},{4,12},{6,14},{8,0},{10,2},{12,4},{14,6},{1,9},{3,11}... | collective-permute-start | bytes 319496 | tf_op jit(solution)/shard_map/ppermute | solution.py:506
  60.8 8.9 %collective-permute-start.17 = (bf16[96,512]{1,0:T(8,128)(2,1)S(1)}, bf16[96,512]{1,0:T(8,128)(2,1)S(1)}, u32[]{:S(2)}, u32[]{:S(2)}) collective-permute-start(bf16[96,512]{1,0:T(8,128)(2,1)S(1)} %get-tuple-element.103), channel_id=1, source_target_pairs={{0,8},{2,10},{4,12},{6,14},{8,0},{10,2},{12,4},{14,6},{1,9},{3,11}... | collective-permute-start | bytes 294920 | tf_op jit(solution)/shard_map/ppermute | solution.py:506

commit v4 on v3

v4 whole, which is shorter than its diff:
```python
import functools

import jax
import jax.numpy as jnp
from jax import lax
from jax.experimental import pallas as pl
from jax.experimental.pallas import tpu as pltpu
from jax.sharding import PartitionSpec as P

EPSILON = 1e-05
F32 = jnp.float32
BF16 = jnp.bfloat16
VMEM = pl.BlockSpec(memory_space=pltpu.VMEM)
SMEM = pl.BlockSpec(memory_space=pltpu.SMEM)
HBM = pl.BlockSpec(memory_space=pltpu.HBM)
ANY = pl.BlockSpec(memory_space=pl.ANY)
PEERS = 4
EXTRA = 8
PIECE = 64


def nn_dot(a, b):
    return jnp.dot(a, b, preferred_element_type=F32)


def nt_dot(a, b):
    return lax.dot_general(a, b, (((1,), (1,)), ((), ())), preferred_element_type=F32)


def tn_dot(a, b):
    return lax.dot_general(a, b, (((0,), (0,)), ((), ())), preferred_element_type=F32)


def shape(dims, dtype):
    return jax.ShapeDtypeStruct(dims, dtype)


def call(kernel, outs, scratch, flops, byts, *args, scalars=0, raw=0, after=0):
    blocks = len(args) - scalars - raw - after
    args = list(args)
    for i in range(scalars, scalars + raw):
        args[i] = pltpu.with_memory_space_constraint(args[i], pltpu.HBM)
    return pl.pallas_call(
        kernel,
        out_shape=outs,
        in_specs=[SMEM] * scalars + [HBM] * raw + [VMEM] * blocks + [ANY] * after,
        out_specs=jax.tree.map(lambda _: VMEM, outs),
        scratch_shapes=scratch,
        compiler_params=pltpu.CompilerParams(vmem_limit_bytes=24 * 1024 * 1024),
        cost_estimate=pl.CostEstimate(flops=flops, bytes_accessed=byts, transcendentals=0),
    )(*args)


def on_core(core):
    return pl.when(lax.axis_index("segment") == core)


def two_dot(pair_ref, b):
    return nn_dot(pair_ref[0], b) + nn_dot(pair_ref[1], b)


def dom_bit(i):
    return (lax.axis_index("dom") >> i) & 1


def sent_slots():
    x, z = dom_bit(0), dom_bit(1)
    return x, 1 - x, 2 + z, 3 - z


def read_slots():
    x, z = dom_bit(0), dom_bit(1)
    return 1 - x, x, 3 - z, 2 + z


def target_onehot(targets_ref, rows):
    ids = jnp.concatenate([targets_ref[0, pl.ds(s, 1), :] for s in sent_slots()], 1)
    return (lax.broadcasted_iota(jnp.int32, (rows, ids.shape[1]), 0) == ids).astype(BF16)


def gather_kernel(targets_hbm, x_hbm, o0, o1, o2, o3, x_ref, onehot_ref, targets_ref, sems):
    copies = [
        pltpu.make_async_copy(targets_hbm, targets_ref, sems.at[0]),
        pltpu.make_async_copy(x_hbm, x_ref, sems.at[1]),
    ]
    for c in copies:
        c.start()
    micro, rows, _ = x_ref.shape
    per_peer = o0.shape[0] // micro
    copies[0].wait()
    onehot = target_onehot(targets_ref, rows)
    onehot_ref[...] = onehot
    copies[1].wait()
    for m in range(micro):
        picked = tn_dot(onehot, x_ref[m]).astype(BF16)
        for k, out in enumerate((o0, o1, o2, o3)):
            out[m * per_peer : (m + 1) * per_peer, :] = picked[k * per_peer : (k + 1) * per_peer]


def node_kernel(
    pairs_ref, count_ref, values_hbm, w_hbm, bias_hbm, w_agg_hbm, w_out_hbm, gain_hbm, g_hbm, x_ref,
    z_ref, acc_ref, halo_in_ref, local_back_ref, halo_back_ref, w_ref, w_agg_ref, w_out_ref, gain_ref,
    g_ref,
    values_ref, src_ref, bias_ref, dense_ref, local_ref, sems,
):
    copies = [
        pltpu.make_async_copy(a, b, sems.at[i])
        for i, (a, b) in enumerate(
            (
                (values_hbm, values_ref), (w_hbm, w_ref), (bias_hbm, bias_ref),
                (w_agg_hbm, w_agg_ref), (w_out_hbm, w_out_ref), (gain_hbm, gain_ref), (g_hbm, g_ref),
            )
        )
    ]
    for c in copies:
        c.start()
    micro, rows, feat = x_ref.shape
    row_blocks, blocks = dense_ref.shape[:2]
    for m in range(micro):
        src_ref[:, m * feat : (m + 1) * feat] = x_ref[m]
    dense_ref[...] = jnp.zeros_like(dense_ref)
    copies[0].wait()
    for k in range(values_ref.shape[0]):

        @pl.when(k < count_ref[0])
        def _():
            dense_ref[pairs_ref[0, 0, k], pairs_ref[0, 1, k]] += values_ref[k].astype(F32)

    copies[1].wait()
    copies[2].wait()
    for m in range(micro):
        z_ref[m * rows : (m + 1) * rows, :] = nn_dot(x_ref[m], w_ref[...]) + bias_ref[
            ...
        ].astype(F32)
    for d in range(row_blocks):
        down = slice(d * 128, (d + 1) * 128)
        for c in range(blocks):
            block = dense_ref[d, c]
            high = block.astype(BF16)
            for i, v in enumerate((high, (block - high.astype(F32)).astype(BF16))):
                if c < row_blocks:
                    across_to = slice(c * 128, (c + 1) * 128)
                    local_ref[i, down, across_to] = v
                    local_back_ref[i, across_to, down] = v.T
                else:
                    halo_in_ref[i, down, :] = v
                    halo_back_ref[i, :, down] = v.T
    acc_ref[...] = two_dot(local_ref, src_ref[...])
    for c in copies[3:]:
        c.wait()


def pieces(part):
    return [slice(r, r + PIECE) for r in range(part.start, part.stop, PIECE)]


def row_mean(v):
    return jnp.mean(v, axis=1, keepdims=True)


def norm_back(g, normed, inv_std, gain):
    e = g * gain
    return (inv_std * (e - row_mean(e) - normed * row_mean(e * normed))).astype(BF16)


def parts_of(total, micro):
    rows = total // micro
    return [slice(m * rows, (m + 1) * rows) for m in range(micro)]


def put_halo_grads(t_ref, outs):
    feat = outs[0].shape[1]
    per_peer = outs[0].shape[0] // 2
    for slot, out in zip(read_slots(), outs):
        for m in range(2):
            at = pl.ds(pl.multiple_of(slot * per_peer, per_peer), per_peer)
            out[m * per_peer : (m + 1) * per_peer, :] = t_ref[
                at, m * feat : (m + 1) * feat
            ].astype(BF16)


def first_kernel(
    h0, h1, h2, h3, halo_in_ref, halo_back_ref, z_ref, acc_ref, g_ref, w_agg_ref, w_out_ref, gain_ref, _,
    o0, o1, o2, o3, both_ref, dact_ref, normed_ref, inv_ref, agg_ref, hidden_ref, gpn_ref,
    gpre_ref, sums_ref,
    src_ref, s0_ref, t_ref,
):
    micro, rows, feat = g_ref.shape
    per_peer = h0.shape[0] // micro
    for slot, h in zip(read_slots(), (h0, h1, h2, h3)):
        for m in range(micro):
            at = pl.ds(pl.multiple_of(slot * per_peer, per_peer), per_peer)
            src_ref[at, m * feat : (m + 1) * feat] = h[m * per_peer : (m + 1) * per_peer, :]
    gain = gain_ref[...].astype(F32)
    parts = parts_of(micro * rows, micro)
    for m, part in enumerate(parts):
        cols = slice(m * feat, (m + 1) * feat)
        agg_ref[part, :] = (acc_ref[:, cols] + two_dot(halo_in_ref, src_ref[:, cols])).astype(BF16)
    for part in parts:
        s0_ref[part, :] = nn_dot(agg_ref[part, :], w_agg_ref[...])
    for part in parts:
        for at in pieces(part):
            preact = z_ref[at, :] + s0_ref[at, :]
            sig = 1.0 / (1.0 + jnp.exp(-preact))
            hidden_ref[at, :] = (preact * sig).astype(BF16)
            dact_ref[at, :] = sig * (1.0 + preact * (1.0 - sig))
    for part in parts:
        s0_ref[part, :] = nn_dot(hidden_ref[part, :], w_out_ref[...])
    gain_sum = jnp.zeros((1, feat), F32)
    for m, part in enumerate(parts):
        for at in pieces(part):
            output = s0_ref[at, :]
            centred = output - row_mean(output)
            inv_std = lax.rsqrt(row_mean(centred * centred) + EPSILON)
            normed = centred * inv_std
            normed_ref[at, :] = normed
            inv_ref[at, :] = jnp.broadcast_to(inv_std, (PIECE, 128))
            g = g_ref[m, at.start - part.start : at.stop - part.start, :].astype(F32)
            gpn_ref[at, :] = norm_back(g, normed, inv_std, gain)
            gain_sum += jnp.sum(g * normed, axis=0, keepdims=True)
    for part in parts:
        s0_ref[part, :] = nt_dot(gpn_ref[part, :], w_out_ref[...])
    bias_sum = jnp.zeros((1, feat), F32)
    for part in parts:
        for at in pieces(part):
            gpre = (s0_ref[at, :] * dact_ref[at, :]).astype(BF16)
            gpre_ref[at, :] = gpre
            bias_sum += jnp.sum(gpre.astype(F32), axis=0, keepdims=True)
    for m, part in enumerate(parts):
        cols = slice(m * feat, (m + 1) * feat)
        gm = nt_dot(gpre_ref[part, :], w_agg_ref[...]).astype(BF16)
        both_ref[:rows, cols] = gm
        both_ref[rows:, cols] = gpre_ref[part, :]
        t_ref[:, cols] = two_dot(halo_back_ref, gm)
    put_halo_grads(t_ref, (o0, o1, o2, o3))
    sums_ref[...] = jnp.concatenate([bias_sum, gain_sum, jnp.zeros((EXTRA - 2, feat), F32)], 0)


def lower_kernel(g_ref, gpre_ref, gm_ref, back_ref, w_node_ref, cpart_ref, g_out):
    feat = g_ref.shape[1]

    @on_core(0)
    def _():
        g_out[...] = g_ref[...]
        for m, part in enumerate(parts_of(g_ref.shape[0], 2)):
            back = nt_dot(gpre_ref[part, :], w_node_ref[...])
            spread = two_dot(back_ref, gm_ref[:, m * feat : (m + 1) * feat])
            cpart_ref[part, :] = g_ref[part, :].astype(F32) + back + spread


def upper_kernel(g_ref, both_ref, back_ref, w_node_ref, cpart_ref):
    micro, rows, feat = g_ref.shape

    @on_core(0)
    def _():
        for m, part in enumerate(parts_of(micro * rows, micro)):
            cols = slice(m * feat, (m + 1) * feat)
            back = nt_dot(both_ref[rows:, cols], w_node_ref[...])
            spread = two_dot(back_ref, both_ref[:rows, cols])
            cpart_ref[part, :] = g_ref[m].astype(F32) + back + spread


def first_bit():
    return (lax.axis_index("dom") >> (1 - lax.axis_index("segment"))) & 1


def second_bit():
    return (lax.axis_index("dom") >> lax.axis_index("segment")) & 1


def chunk_order(chunks):
    core = lax.axis_index("segment")
    low = [d for d in range(chunks) if not d & 2]
    high = [d for d in range(chunks) if not d & 1]
    starts = [a + core * (b - a) for a, b in zip(low, high)]
    step, mine = 2 - core, first_bit()
    return [d + mine * step for d in starts] + [d + (1 - mine) * step for d in starts]


def weight_products(la_ref, lb_ref, gpre_ref, gpn_ref, sums, keep_ref, send_ref):
    n, rows, feat = keep_ref.shape
    share = (rows - EXTRA) // 3
    for base in (n, 0):
        a = nn_dot(la_ref[base * 2 * share : (base + n) * 2 * share, :], gpre_ref[...])
        b = nn_dot(lb_ref[base * share : (base + n) * share, :], gpn_ref[...])
        for i in range(n):
            for lo, v in (
                (0, a[i * 2 * share : (i + 1) * 2 * share]),
                (2 * share, b[i * share : (i + 1) * share]),
                (3 * share, sums),
            ):
                if base:
                    at = i * rows + lo
                    send_ref[at : at + v.shape[0], :] = v.astype(BF16)
                else:
                    keep_ref[i, lo : lo + v.shape[0], :] = v


def turn_kernel(
    chunks, x_ref, agg_ref, hidden_ref, gpre_ref, gpn_ref, sums_ref, la_ref, lb_ref,
    keep_ref, send_ref, turned_ref,
):
    micro, rows, feat = x_ref.shape
    share = feat // chunks
    for m in range(micro):
        turned_ref[:, m * rows : (m + 1) * rows] = x_ref[m].T
    places = [
        pl.ds(pl.multiple_of(d * share, share), share) for d in chunk_order(chunks)
    ]
    for i, at in enumerate(places):
        la_ref[2 * i * share : (2 * i + 1) * share, :] = turned_ref[at, :]
    turned_ref[...] = agg_ref[...].T
    for i, at in enumerate(places):
        la_ref[(2 * i + 1) * share : (2 * i + 2) * share, :] = turned_ref[at, :]
    turned_ref[...] = hidden_ref[...].T
    for i, at in enumerate(places):
        lb_ref[i * share : (i + 1) * share, :] = turned_ref[at, :]

    @on_core(1)
    def _():
        weight_products(la_ref, lb_ref, gpre_ref, gpn_ref, sums_ref[...], keep_ref, send_ref)


def second_kernel(*refs):
    @on_core(0)
    def _():
        second_layer(*refs)


def second_layer(
    onehot_ref, r0, r1, r2, r3, cin_ref, dact_ref, normed_ref, inv_ref, w_out_ref, gain_ref,
    g_ref, gpn_ref, gpre_ref, sums_ref, s0_ref,
):
    total, feat = dact_ref.shape
    parts = parts_of(total, 2)
    per_peer = r0.shape[0] // 2
    gain = gain_ref[...].astype(F32)
    for m, part in enumerate(parts):
        ret = jnp.concatenate([r[m * per_peer : (m + 1) * per_peer, :] for r in (r0, r1, r2, r3)], 0)
        s0_ref[part, :] = nn_dot(onehot_ref[...], ret)
    gain_sum = jnp.zeros((1, feat), F32)
    for part in parts:
        for at in pieces(part):
            g16 = (cin_ref[at, :] + s0_ref[at, :]).astype(BF16)
            g_ref[at, :] = g16
            g = g16.astype(F32)
            normed = normed_ref[at, :]
            gpn_ref[at, :] = norm_back(g, normed, inv_ref[at, 0:1], gain)
            gain_sum += jnp.sum(g * normed, axis=0, keepdims=True)
    for part in parts:
        s0_ref[part, :] = nt_dot(gpn_ref[part, :], w_out_ref[...])
    bias_sum = jnp.zeros((1, feat), F32)
    for part in parts:
        for at in pieces(part):
            gpre = (s0_ref[at, :] * dact_ref[at, :]).astype(BF16)
            gpre_ref[at, :] = gpre
            bias_sum += jnp.sum(gpre.astype(F32), axis=0, keepdims=True)
    sums_ref[...] = jnp.concatenate([bias_sum, gain_sum, jnp.zeros((EXTRA - 2, feat), F32)], 0)


def message_grads(gpre_ref, back_ref, w_agg_ref, gm_ref, t_ref):
    total, feat = gpre_ref.shape
    for m, part in enumerate(parts_of(total, 2)):
        cols = slice(m * feat, (m + 1) * feat)
        gm = nt_dot(gpre_ref[part, :], w_agg_ref[...]).astype(BF16)
        gm_ref[:, cols] = gm
        t_ref[:, cols] = two_dot(back_ref, gm)


def third_kernel(
    gpre_ref, gpn_ref, sums_ref, back_ref, w_agg_ref, la_ref, lb_ref, keep1_ref, send1_ref,
    keep_ref, send_ref, far_ref, near_ref, gm_ref, t_ref,
):
    ride = near_ref.shape[0]
    first = send1_ref.shape[0]

    @on_core(0)
    def _():
        weight_products(la_ref, lb_ref, gpre_ref, gpn_ref, sums_ref[...], keep_ref, send_ref)
        message_grads(gpre_ref, back_ref, w_agg_ref, gm_ref, t_ref)
        cross_ref = send_ref.at[pl.ds(first + ride, ride), :]
        put_halo_grads(
            t_ref,
            (near_ref, cross_ref, send_ref.at[pl.ds(first, ride), :], far_ref.at[pl.ds(0, ride), :]),
        )
        far_ref[ride:, :] = send_ref[first + ride :, :]

    @on_core(1)
    def _():
        keep_ref[...] = keep1_ref[...]
        send_ref[:first, :] = send1_ref[...]


def plain_third_kernel(gpre_ref, back_ref, w_agg_ref, o0, o1, o2, o3, gm_ref, t_ref):
    message_grads(gpre_ref, back_ref, w_agg_ref, gm_ref, t_ref)
    put_halo_grads(t_ref, (o0, o1, o2, o3))


def halve_job(mine, keep, recv, keep2, send2):
    n, rows, _ = keep2.shape
    for i in range(n):
        d, o = 2 * i + mine, 2 * i + 1 - mine
        at = pl.ds(pl.multiple_of(o * rows, 8), rows)
        send2[i * rows : (i + 1) * rows, :] = (keep[o] + recv[at, :].astype(F32)).astype(BF16)
        at = pl.ds(pl.multiple_of(d * rows, 8), rows)
        keep2[i] = keep[d] + recv[at, :].astype(F32)


def carry_kernel(keep, recv, near_ref, far_ref, _, keep2, send2):
    ride = near_ref.shape[0]
    halve_job(second_bit(), keep, recv, keep2, send2)
    at = keep2.shape[0] * keep2.shape[1]
    inner = dom_bit(0) == dom_bit(1)

    @on_core(0)
    def _():
        send2[at : at + ride, :] = near_ref[...]

        @pl.when(inner)
        def _():
            send2[at + ride :, :] = recv[recv.shape[0] - ride :, :]

        @pl.when(jnp.logical_not(inner))
        def _():
            send2[at + ride :, :] = far_ref[ride:, :]


def halve_kernel(keep, recv, keep2, send2):
    halve_job(dom_bit(2), keep, recv, keep2, send2)


def last_kernel(keep, recv, node_ref, agg_ref, out_ref, bias_ref, gain_ref):
    share = node_ref.shape[0]
    total = keep[0] + recv[...].astype(F32)
    node_ref[...] = total[0:share]
    agg_ref[...] = total[share : 2 * share]
    out_ref[...] = total[2 * share : 3 * share]
    bias_ref[...] = total[3 * share : 3 * share + 1]
    gain_ref[...] = total[3 * share + 1 : 3 * share + 2]


def cot_kernel(skips, onehot_ref, r0, r1, r2, r3, cpart_ref, other_ref, cot_ref):
    micro, rows, feat = cot_ref.shape
    n = onehot_ref.shape[1] // PEERS

    @on_core(1)
    def _():
        for m in range(micro):
            cot_ref[m] = other_ref[m * rows : (m + 1) * rows, :]

    @on_core(0)
    def _():
        for m in range(micro):
            ret = jnp.concatenate(
                [r[s + m * n : s + (m + 1) * n, :] for r, s in zip((r0, r1, r2, r3), skips)], 0
            )
            cot_ref[m] = (
                cpart_ref[m * rows : (m + 1) * rows, :] + nn_dot(onehot_ref[...], ret)
            ).astype(BF16)


def whole_kernel(x_ref, agg_ref, hidden_ref, gpn_ref, gpre_ref, node_ref, agg_out, out_ref):
    rows = x_ref.shape[1]
    gpre = gpre_ref[...]
    node_ref[...] = tn_dot(x_ref[0], gpre[:rows]) + tn_dot(x_ref[1], gpre[rows:])
    agg_out[...] = tn_dot(agg_ref[...], gpre)
    out_ref[...] = tn_dot(hidden_ref[...], gpn_ref[...])


def body(
    section_inputs,
    out_cot,
    w_node,
    w_agg,
    w_out,
    bias,
    gain,
    send_rows,
    blk_pairs,
    blk_count,
    blk_values,
):
    peers = lax.axis_size("dom")
    segment = lax.axis_index("segment")
    assert lax.axis_size("segment") == 2 and peers % 4 == 0
    x = section_inputs[0]
    micro, rows, feat = x.shape
    _, slots, per_peer = send_rows.shape
    assert slots * per_peer == 128 and slots == PEERS and micro == 2
    total = micro * rows
    values = blk_values[0]
    row_blocks = rows // 128
    wide = micro * feat
    w_n, w_a, w_o = w_node[0], w_agg[0], w_out[0]
    matmul = 2 * total * feat * feat
    size = total * feat
    chunk = shape((micro * per_peer, feat), BF16)

    def swap_partner(p, k):
        if k == 0:
            return p ^ 1
        if k == 1:
            return (p + 1 if p & 1 else p - 1) % peers
        up = (p >> 1) & 1
        return (p + 2 if up == (k == 3) else p - 2) % peers

    def swapped(v, k, cores):
        return lax.ppermute(
            v,
            ("dom", "segment"),
            [(2 * p + s, 2 * swap_partner(p, k) + d) for p in range(peers) for s, d in cores],
        )

    def across(v):
        return lax.ppermute(v, "segment", [(0, 1), (1, 0)])

    def flipped(v, bits):
        return lax.ppermute(
            v,
            ("dom", "segment"),
            [(2 * p + s, 2 * (p ^ (1 << bits[s])) + s) for p in range(peers) for s in (0, 1)],
        )

    f_full, b_full = shape((total, feat), F32), shape((total, feat), BF16)
    s_sums = shape((EXTRA, feat), F32)
    dma = pltpu.SemaphoreType.DMA
    *outgoing, x, onehot = call(
        gather_kernel,
        [chunk] * slots + [shape(x.shape, BF16), shape((rows, slots * per_peer), BF16)],
        [pltpu.VMEM(send_rows.shape, jnp.int32), dma((2,))],
        matmul // 8, 2 * size, send_rows, x,
        raw=2,
    )
    same, other_core = ((0, 0), (1, 1)), ((0, 1), (1, 0))
    w_other = across(w_n)
    halos = [swapped(v, k, same) for k, v in enumerate(outgoing)]
    halo_rows = slots * per_peer
    loaded = (w_n, w_a, w_o, gain, out_cot)
    z, acc, halo_in, local_back, halo_back, w_n, w_a, w_o, gain, g_last = call(
        node_kernel,
        [f_full, shape((rows, wide), F32), shape((2, rows, halo_rows), BF16)]
        + [shape((2, rows, rows), BF16), shape((2, halo_rows, rows), BF16)]
        + [shape(v.shape, BF16) for v in loaded],
        [
            pltpu.VMEM(values.shape, BF16), pltpu.VMEM((rows, wide), BF16), pltpu.VMEM(bias.shape, BF16),
            pltpu.VMEM((row_blocks, row_blocks + 1, 128, 128), F32), pltpu.VMEM((2, rows, rows), BF16),
            dma((7,)),
        ],
        2 * matmul, 8 * size,
        blk_pairs, blk_count, values, w_n, bias, w_a, w_o, gain, out_cot, x,
        scalars=2, raw=7,
    )
    first = call(
        first_kernel,
        [chunk] * slots
        + [shape((2 * rows, wide), BF16), f_full, f_full, shape((total, 128), F32)]
        + [b_full] * 4 + [s_sums],
        [
            pltpu.VMEM((halo_rows, wide), BF16),
            pltpu.VMEM((total, feat), F32),
            pltpu.VMEM((halo_rows, wide), F32),
        ],
        4 * matmul, 20 * size,
        *halos, halo_in, halo_back, z, acc, g_last, w_a, w_o, gain, w_other,
        after=1,
    )
    to_return = first[:slots]
    both, dact, normed, inv_std, agg, hidden, gpn1, gpre1, sums1 = first[slots:]
    returned = [swapped(v, k, other_core) for k, v in enumerate(to_return)]
    c_in = call(
        upper_kernel, f_full, [], matmul, 10 * size, g_last, across(both), local_back, w_other
    )
    share = feat // peers
    rows_each = 3 * share + EXTRA
    halving = peers == 8

    def kept(n, extra=0):
        return [shape((n, rows_each, feat), F32), shape((n * rows_each + extra, feat), BF16)]

    if halving:
        turned = call(
            functools.partial(turn_kernel, peers),
            [shape((16 * share, total), BF16), shape((8 * share, total), BF16)] + kept(4),
            [pltpu.VMEM((feat, total), BF16)],
            3 * matmul, 20 * size,
            x, agg, hidden, gpre1, gpn1, sums1,
        )
    g_low, gpn, gpre, sums = call(
        second_kernel,
        [b_full, b_full, b_full, s_sums],
        [pltpu.VMEM((total, feat), F32)],
        2 * matmul, 16 * size,
        onehot, *returned, c_in, dact, normed, inv_std, w_o, gain,
    )
    scr_t, gm_out = pltpu.VMEM((halo_rows, wide), F32), shape((rows, wide), BF16)
    if halving:
        ride = chunk.shape[0]
        keep, send, far, near, gm = call(
            third_kernel,
            kept(4, 2 * ride) + [shape((2 * ride, feat), BF16), chunk, gm_out],
            [scr_t], 4 * matmul, 16 * size,
            gpre, gpn, sums, halo_back, w_a, *turned,
        )
        recv = flipped(send, (1, 0))
        far = swapped(far, 3, ((0, 0),))
    else:
        *to_return, gm = call(
            plain_third_kernel, [chunk] * slots + [gm_out], [scr_t],
            2 * matmul, 8 * size, gpre, halo_back, w_a,
        )
    cpart0, g_low = call(
        lower_kernel, [f_full, b_full], [], matmul, 10 * size, g_low, gpre, gm, local_back, w_n
    )
    other = across(g_low)
    skips = (0,) * slots
    if halving:
        up = recv
        keep, send = call(
            carry_kernel, kept(2, 2 * ride), [], size, 8 * size, keep, recv, near, far, cpart0,
            after=1,
        )
        recv = flipped(send, (0, 1))
        first = 2 * rows_each
        returned, skips = (recv, recv, up, far), (first, first + ride, 2 * first, 0)
        keep, send = call(halve_kernel, kept(1), [], size, 4 * size, keep, recv)
        recv = flipped(send, (2, 2))
        part, row = shape((share, feat), F32), shape((1, feat), F32)
        grad_node, grad_agg, grad_out, grad_bias, grad_gain = call(
            last_kernel, [part, part, part, row, row], [], size, 2 * size, keep, recv,
        )
    else:
        is_last = segment == 1
        gpn, gpre = jnp.where(is_last, gpn1, gpn), jnp.where(is_last, gpre1, gpre)
        sums = jnp.where(is_last, sums1, sums)
        square = shape((feat, feat), F32)
        full = call(
            whole_kernel, [square] * 3, [], 3 * matmul, 12 * size, x, agg, hidden, gpn, gpre
        )
        grad_node, grad_agg, grad_out = [
            lax.psum_scatter(v, "dom", scatter_dimension=0, tiled=True) for v in full
        ]
        sums = lax.psum(sums, "dom")
        grad_bias, grad_gain = sums[0:1], sums[1:2]
        returned = [swapped(v, k, ((0, 0),)) for k, v in enumerate(to_return)]
    cot = call(
        functools.partial(cot_kernel, skips), shape((micro, rows, feat), BF16), [], matmul // 4, 4 * size,
        onehot, *returned, cpart0, other,
    )
    return (
        cot[None],
        grad_node[None],
        grad_agg[None],
        grad_out[None],
        grad_bias,
        grad_gain,
    )


def solution(mesh):
    placed = (
        P("segment", None, ("grp", "dom"), None),
        P(None, ("grp", "dom"), None),
        P("segment", None, None),
        P("segment", None, None),
        P("segment", None, None),
        P("segment", None),
        P("segment", None),
        P("dom", None, None),
        P("dom", None, None),
        P("dom"),
        P("dom", None, None, None),
    )
    return jax.shard_map(
        body,
        mesh=mesh,
        in_specs=placed,
        out_specs=(
            P("segment", None, ("grp", "dom"), None),
            P("segment", ("grp", "dom"), None),
            P("segment", ("grp", "dom"), None),
            P("segment", ("grp", "dom"), None),
            P("segment", "grp"),
            P("segment", "grp"),
        ),
        check_vma=False,
    )
```

time: 71.1 us -> 68.2 us (0.959)
  waiting for transfers between devices: 28 us -> 32.6 us
  Pallas kernels: 18 us -> 14 us
  starting transfers between devices: 21.3 us -> 19.2 us
  local copies, waits for them, and re-layouts: 1.72 us -> 0.67 us
    ppermute x9, waiting for transfers between devices: 8.27 us -> 17 us  [swapped(): lax.ppermute(v, ('dom', 'segment'), [(2 * p + s, 2 * swap_partner(p, k) +...]
    ppermute x6 -> x3, waiting for transfers between devices: 19.8 us -> 15.6 us  [flipped(): lax.ppermute(v, ('dom', 'segment'), [(2 * p + s, 2 * (p ^ 1 << bits[s]) +...]
    pallas_call x12, Pallas kernels: 18 us -> 14 us  [call(): pl.pallas_call(kernel, out_shape=outs, in_specs=[SMEM] * scalars + [HBM]...]
    ppermute x6 -> x3, starting transfers between devices: 5.96 us -> 3.32 us  [flipped(): lax.ppermute(v, ('dom', 'segment'), [(2 * p + s, 2 * (p ^ 1 << bits[s]) +...]
    unnamed x6 -> x2, local copies, waits for them, and re-layouts: 1.72 us -> 0.67 us
  transfers between devices with their start and end apart: 19 -> 15, of which waited for: 7 -> 6; matrix products, arithmetic and copies ran while one was open for 0% -> 0% of each run, Pallas kernels for 17% -> 11%
where the time goes in v4:
time: 68.2 us; the launch traced here: 67.9 us
  waiting for transfers between devices  32.6 us (48%)
  starting transfers between devices  19.2 us (28%)
  Pallas kernels  14 us (21%)
  between operations  1.45 us (2%)
    ppermute x9, waiting for transfers between devices, swapped(): lax.ppermute(v, ('dom', 'segment'), [(2 * p + s, 2 * swap_partner(p, k) +...  17 us
    ppermute x3, waiting for transfers between devices, flipped(): lax.ppermute(v, ('dom', 'segment'), [(2 * p + s, 2 * (p ^ 1 << bits[s]) +...  15.6 us
    ppermute x9, starting transfers between devices, swapped(): lax.ppermute(v, ('dom', 'segment'), [(2 * p + s, 2 * swap_partner(p, k) +...  15.3 us
    pallas_call x12, Pallas kernels, call(): pl.pallas_call(kernel, out_shape=outs, in_specs=[SMEM] * scalars + [HBM]...  14 us
    ppermute x3, starting transfers between devices, flipped(): lax.ppermute(v, ('dom', 'segment'), [(2 * p + s, 2 * (p ^ 1 << bits[s]) +...  3.32 us
  transfers between devices with their start and end apart: 15, of which 6 were waited for; matrix products, arithmetic and copies ran while one was open for 0% of the time, Pallas kernels for 11%

profile of v4, /device:TPU:0, one launch (start us, length us, event | category | flops | bytes accessed | tf_op | source)
XLA Modules:
  0.0 67.9 jit_solution(779886612945933220)
XLA Ops:
  0.6 0.5 collective-permute-start.4
  1.1 1.3 %shard_map.154 = (bf16[64,512]{1,0:T(8,128)(2,1)S(1)}, bf16[64,512]{1,0:T(8,128)(2,1)S(1)}, bf16[64,512]{1,0:T(8,128)(2,1)S(1)}, bf16[64,512]{1,0:T(8,128)(2,1)S...) custom-call(s32[1,4,32]{2,1,0:T(4,128)} %targets_hbm.1, bf16[2,256,512]{2,1,0:T(8,128)(2,1)} %bitcast.10), custom_call_target="tpu_custom_call" | custom-call | flops 33554432 | bytes 524288 | tf_op jit(solution)/shard_map/pallas_call | solution.py:43
  2.5 2.6 %collective-permute-start = (bf16[64,512]{1,0:T(8,128)(2,1)S(1)}, bf16[64,512]{1,0:T(8,128)(2,1)S(1)}, u32[]{:S(2)}, u32[]{:S(2)}) collective-permute-start(bf16[64,512]{1,0:T(8,128)(2,1)S(1)} %get-tuple-element.60), channel_id=1, source_target_pairs={{0,2},{1,3},{2,0},{3,1},{4,6},{5,7},{6,4},{7,5},{8,10},{9,11},{10,... | collective-permute-start | bytes 196616 | tf_op jit(solution)/shard_map/ppermute | solution.py:508
  5.1 3.6 %collective-permute-start.1 = (bf16[64,512]{1,0:T(8,128)(2,1)S(1)}, bf16[64,512]{1,0:T(8,128)(2,1)S(1)}, u32[]{:S(2)}, u32[]{:S(2)}) collective-permute-start(bf16[64,512]{1,0:T(8,128)(2,1)S(1)} %get-tuple-element.61), channel_id=1, source_target_pairs={{0,14},{1,15},{2,4},{3,5},{4,2},{5,3},{6,8},{7,9},{8,6},{9,7},{10,... | collective-permute-start | bytes 196616 | tf_op jit(solution)/shard_map/ppermute | solution.py:508
  8.6 0.0 collective-permute-start.2
  8.6 0.9 %collective-permute-start.3 = (bf16[64,512]{1,0:T(8,128)(2,1)S(1)}, bf16[64,512]{1,0:T(8,128)(2,1)S(1)}, u32[]{:S(2)}, u32[]{:S(2)}) collective-permute-start(bf16[64,512]{1,0:T(8,128)(2,1)S(1)} %get-tuple-element.63), channel_id=1, source_target_pairs={{0,12},{1,13},{2,14},{3,15},{4,8},{5,9},{6,10},{7,11},{8,4},{9,5},... | collective-permute-start | bytes 196616 | tf_op jit(solution)/shard_map/ppermute | solution.py:508
  10.2 0.0 copy-start
  10.2 0.7 copy-done
  10.9 2.5 %shard_map.155 = (f32[512,512]{1,0:T(8,128)S(1)}, f32[256,1024]{1,0:T(8,128)S(1)}, bf16[2,256,128]{2,1,0:T(8,128)(2,1)S(1)}, bf16[2,256,256]{2,1,0:T(8,128)(2,1)...) custom-call(s32[1,2,7]{2,1,0:T(2,128)S(1)} %copy-done, ...), custom_call_target="tpu_custom_call" | custom-call | flops 536870912 | bytes 2097152 | tf_op jit(solution)/shard_map/pallas_call | solution.py:43
  13.4 0.0 collective-permute-done.h0
  13.4 0.0 collective-permute-done.1.h1
  13.4 0.0 collective-permute-done.2.h2
  13.4 1.3 %collective-permute-done.3.h3 = bf16[64,512]{1,0:T(8,128)(2,1)S(1)} collective-permute-done((bf16[64,512]{1,0:T(8,128)(2,1)S(1)}, bf16[64,512]{1,0:T(8,128)(2,1)S(1)}, u32[]{:S(2)}, u32[]{:S(2)}) %collective-permute-start.3) | collective-permute-done | bytes 65568 | tf_op jit(solution)/shard_map/ppermute | solution.py:508
  14.8 0.0 collective-permute-done.4._.w_node_ref
  14.8 2.9 %shard_map.156 = (bf16[64,512]{1,0:T(8,128)(2,1)S(1)}, bf16[64,512]{1,0:T(8,128)(2,1)S(1)}, bf16[64,512]{1,0:T(8,128)(2,1)S(1)}, bf16[64,512]{1,0:T(8,128)(2,1)S...) custom-call(bf16[64,512]{1,0:T(8,128)(2,1)S(1)} %collective-permute-, ...), custom_call_target="tpu_custom_call" | custom-call | flops 1073741824 | bytes 5242880 | tf_op jit(solution)/shard_map/pallas_call | solution.py:43
  17.7 0.1 collective-permute-start.9
  17.8 1.4 %collective-permute-start.5 = (bf16[64,512]{1,0:T(8,128)(2,1)S(1)}, bf16[64,512]{1,0:T(8,128)(2,1)S(1)}, u32[]{:S(2)}, u32[]{:S(2)}) collective-permute-start(bf16[64,512]{1,0:T(8,128)(2,1)S(1)} %get-tuple-element.73), channel_id=1, source_target_pairs={{0,3},{1,2},{2,1},{3,0},{4,7},{5,6},{6,5},{7,4},{8,11},{9,10},{10,... | collective-permute-start | bytes 196616 | tf_op jit(solution)/shard_map/ppermute | solution.py:508
  19.2 2.5 %collective-permute-start.6 = (bf16[64,512]{1,0:T(8,128)(2,1)S(1)}, bf16[64,512]{1,0:T(8,128)(2,1)S(1)}, u32[]{:S(2)}, u32[]{:S(2)}) collective-permute-start(bf16[64,512]{1,0:T(8,128)(2,1)S(1)} %get-tuple-element.74), channel_id=1, source_target_pairs={{0,15},{1,14},{2,5},{3,4},{4,3},{5,2},{6,9},{7,8},{8,7},{9,6},{10,... | collective-permute-start | bytes 196616 | tf_op jit(solution)/shard_map/ppermute | solution.py:508
  21.7 0.0 collective-permute-start.7
  21.7 0.9 %collective-permute-start.8 = (bf16[64,512]{1,0:T(8,128)(2,1)S(1)}, bf16[64,512]{1,0:T(8,128)(2,1)S(1)}, u32[]{:S(2)}, u32[]{:S(2)}) collective-permute-start(bf16[64,512]{1,0:T(8,128)(2,1)S(1)} %get-tuple-element.76), channel_id=1, source_target_pairs={{0,13},{1,12},{2,15},{3,14},{4,9},{5,8},{6,11},{7,10},{8,5},{9,4},... | collective-permute-start | bytes 196616 | tf_op jit(solution)/shard_map/ppermute | solution.py:508
  22.6 0.6 shard_map.159
  23.2 0.0 collective-permute-done.9.both_ref
  23.2 0.8 %shard_map.157.refs_5_ = f32[512,512]{1,0:T(8,128)S(1)} custom-call(bf16[2,256,512]{2,1,0:T(8,128)(2,1)S(1)} %get-tuple-element.69.g_ref, bf16[512,1024]{1,0:T(8,128)(2,1)S(1)} %collective-permute-done.9.both_ref, bf16[2,256,256]{2,1,0:T(8,128)(2,1)S(1)} %get-tuple-element.78.back_ref, bf16[512,512]{1,0:T(8,128)(2,1)S(1)} %collective-permute-done.4._.w_node_ref), custom_call_target="tpu_custom_call" | custom-call | flops 268435456 | bytes 2621440 | tf_op jit(solution)/shard_map/pallas_call | solution.py:43
  24.0 0.0 collective-permute-done.5.refs_1_
  24.0 2.1 %collective-permute-done.6.refs_2_ = bf16[64,512]{1,0:T(8,128)(2,1)S(1)} collective-permute-done((bf16[64,512]{1,0:T(8,128)(2,1)S(1)}, bf16[64,512]{1,0:T(8,128)(2,1)S(1)}, u32[]{:S(2)}, u32[]{:S(2)}) %collective-permute-start.6) | collective-permute-done | bytes 65568 | tf_op jit(solution)/shard_map/ppermute | solution.py:508
  26.1 0.0 collective-permute-done.7.refs_3_
  26.2 1.3 %collective-permute-done.8.refs_4_ = bf16[64,512]{1,0:T(8,128)(2,1)S(1)} collective-permute-done((bf16[64,512]{1,0:T(8,128)(2,1)S(1)}, bf16[64,512]{1,0:T(8,128)(2,1)S(1)}, u32[]{:S(2)}, u32[]{:S(2)}) %collective-permute-start.8) | collective-permute-done | bytes 65568 | tf_op jit(solution)/shard_map/ppermute | solution.py:508
  27.5 1.2 %shard_map.158 = (bf16[512,512]{1,0:T(8,128)(2,1)S(1)}, bf16[512,512]{1,0:T(8,128)(2,1)S(1)}, bf16[512,512]{1,0:T(8,128)(2,1)S(1)}, f32[8,512]{1,0:T(8,128)S(1)}) custom-call(bf16[256,128]{1,0:T(8,128)(2,1)S(1)} %get-tuple-element.59.refs_0_.onehot_ref, bf16[64,512]{1,0:T(8,128)(2,1)S(1)} %collective-permute-done.5.refs_1_, ...), custom_call_target="tpu_custom_call" | custom-call | flops 536870912 | bytes 4194304 | tf_op jit(solution)/shard_map/pallas_call | solution.py:43
  28.6 1.8 %shard_map.160 = (f32[4,200,512]{2,1,0:T(8,128)S(1)}, bf16[928,512]{1,0:T(8,128)(2,1)S(1)}, bf16[128,512]{1,0:T(8,128)(2,1)S(1)}, bf16[64,512]{1,0:T(8,128)(2,1)S(1)}, bf16[256,1024]{1,0:T(8,128)(2,1)S(1)}) custom-call(bf16[512,512]{1,0:T(8,128)(2,1)S(1)} %get-tuple-element.82.gpre_ref, bf16[512,512]{1,0:T(8,128)(2,1)S(1)} %get-tuple-element.83.gpn_ref, ...), custom_call_target="tpu_custom_call" | custom-call | flops 1073741824 | bytes 4194304 | tf_op jit(solution)/shard_map/pallas_call | solution.py:43
  30.5 2.0 %collective-permute-start.10 = (bf16[928,512]{1,0:T(8,128)(2,1)S(1)}, bf16[928,512]{1,0:T(8,128)(2,1)S(1)}, u32[]{:S(2)}, u32[]{:S(2)}) collective-permute-start(bf16[928,512]{1,0:T(8,128)(2,1)S(1)} %get-tuple-element.95), channel_id=1, source_target_pairs={{0,4},{1,3},{2,6},{3,1},{4,0},{5,7},{6,2},{7,5},{8,12},{9,11},{10,... | collective-permute-start | bytes 2850824 | tf_op jit(solution)/shard_map/ppermute | solution.py:518
  32.4 3.4 %collective-permute-start.11 = (bf16[128,512]{1,0:T(8,128)(2,1)S(1)}, bf16[128,512]{1,0:T(8,128)(2,1)S(1)}, u32[]{:S(2)}, u32[]{:S(2)}) collective-permute-start(bf16[128,512]{1,0:T(8,128)(2,1)S(1)} %get-tuple-element.97), channel_id=1, source_target_pairs={{0,12},{2,14},{4,8},{6,10},{8,4},{10,6},{12,0},{14,2},{16,28},{18,... | collective-permute-start | bytes 393224 | tf_op jit(solution)/shard_map/ppermute | solution.py:508
  35.8 0.8 %shard_map.161 = (f32[512,512]{1,0:T(8,128)S(1)}, bf16[512,512]{1,0:T(8,128)(2,1)S(1)}) custom-call(bf16[512,512]{1,0:T(8,128)(2,1)S(1)} %get-tuple-element.98.g_ref, bf16[512,512]{1,0:T(8,128)(2,1)S(1)} %get-tuple-element.82.gpre_ref, bf16[256,1024]{1,0:T(8,128)(2,1)S(1)} %get-tuple-element.99.gm_ref, bf16[2,256,256]{2,1,0:T(8,128)(2,1)S(1)} %get-tuple-element.78.back_ref, ...), custom_call_target="tpu_custom_call" | custom-call | flops 268435456 | bytes 2621440 | tf_op jit(solution)/shard_map/pallas_call | solution.py:43
  36.6 12.2 %collective-permute-done.11.far_ref.r3 = bf16[128,512]{1,0:T(8,128)(2,1)S(1)} collective-permute-done((bf16[128,512]{1,0:T(8,128)(2,1)S(1)}, bf16[128,512]{1,0:T(8,128)(2,1)S(1)}, u32[]{:S(2)}, u32[]{:S(2)}) %collective-permute-start.11) | collective-permute-done | bytes 131104 | tf_op jit(solution)/shard_map/ppermute | solution.py:508
  48.9 0.0 collective-permute-done.10.recv.r2
  48.9 0.2 shard_map.162
  49.0 1.3 %collective-permute-start.12 = (bf16[528,512]{1,0:T(8,128)(2,1)S(1)}, bf16[528,512]{1,0:T(8,128)(2,1)S(1)}, u32[]{:S(2)}, u32[]{:S(2)}) collective-permute-start(bf16[528,512]{1,0:T(8,128)(2,1)S(1)} %get-tuple-element.102), channel_id=1, source_target_pairs={{0,2},{1,5},{2,0},{3,7},{4,6},{5,1},{6,4},{7,3},{8,10},{9,13},{10,... | collective-permute-start | bytes 1622024 | tf_op jit(solution)/shard_map/ppermute | solution.py:518
  50.3 0.0 collective-permute-start.13
  50.3 8.1 %collective-permute-done.12.r0.r1.recv = bf16[528,512]{1,0:T(8,128)(2,1)S(1)} collective-permute-done((bf16[528,512]{1,0:T(8,128)(2,1)S(1)}, bf16[528,512]{1,0:T(8,128)(2,1)S(1)}, u32[]{:S(2)}, u32[]{:S(2)}) %collective-permute-start.12) | collective-permute-done | bytes 540704 | tf_op jit(solution)/shard_map/ppermute | solution.py:518
  58.5 0.1 shard_map.164
  58.5 0.1 collective-permute-start.14
  58.6 0.0 collective-permute-done.13.other_ref
  58.6 1.1 %shard_map.163 = bf16[2,256,512]{2,1,0:T(8,128)(2,1)} custom-call(bf16[256,128]{1,0:T(8,128)(2,1)S(1)} %get-tuple-element.59.refs_0_.onehot_ref, bf16[528,512]{1,0:T(8,128)(2,1)S(1)} %collective-permute-done.12.r0.r1.recv, bf16[528,512]{1,0:T(8,128)(2,1)S(1)} %collective-permute-done.12.r0.r1.recv, bf16[928,512]{1,0:T(8,128)(2,1)S(1)} %collective-permute-done.10.recv.r2, ...), custom_call_target="tpu_custom_call" | custom-call | flops 67108864 | bytes 1048576 | tf_op jit(solution)/shard_map/pallas_call | solution.py:43
  59.7 7.4 %collective-permute-done.14.recv = bf16[200,512]{1,0:T(8,128)(2,1)S(1)} collective-permute-done((bf16[200,512]{1,0:T(8,128)(2,1)S(1)}, bf16[200,512]{1,0:T(8,128)(2,1)S(1)}, u32[]{:S(2)}, u32[]{:S(2)}) %collective-permute-start.14) | collective-permute-done | bytes 204832 | tf_op jit(solution)/shard_map/ppermute | solution.py:518
  67.2 0.8 %shard_map.165 = (f32[64,512]{1,0:T(8,128)}, f32[64,512]{1,0:T(8,128)}, f32[64,512]{1,0:T(8,128)}, f32[1,512]{1,0:T(1,128)}, f32[1,512]{1,0:T(1,128)}) custom-call(f32[1,200,512]{2,1,0:T(8,128)S(1)} %get-tuple-element.105.keep, bf16[200,512]{1,0:T(8,128)(2,1)S(1)} %collective-permute-done.14.recv), custom_call_target="tpu_custom_call" | custom-call | flops 262144 | bytes 524288 | tf_op jit(solution)/shard_map/pallas_call | solution.py:43
Async XLA Ops:
  0.6 14.1 %collective-permute-start.4 = (bf16[512,512]{1,0:T(8,128)(2,1)}, bf16[512,512]{1,0:T(8,128)(2,1)S(1)}, u32[]{:S(2)}, u32[]{:S(2)}) collective-permute-start(bf16[512,512]{1,0:T(8,128)(2,1)} %bitcast.13), channel_id=1, source_target_pairs={{0,1},{1,0},{2,3},{3,2},{4,5},{5,4},{6,7},{7,6},{8,9},{9,8},{10,11... | collective-permute-start | bytes 1572872 | tf_op jit(solution)/shard_map/ppermute | solution.py:515
  2.5 10.9 %collective-permute-start = (bf16[64,512]{1,0:T(8,128)(2,1)S(1)}, bf16[64,512]{1,0:T(8,128)(2,1)S(1)}, u32[]{:S(2)}, u32[]{:S(2)}) collective-permute-start(bf16[64,512]{1,0:T(8,128)(2,1)S(1)} %get-tuple-element.60), channel_id=1, source_target_pairs={{0,2},{1,3},{2,0},{3,1},{4,6},{5,7},{6,4},{7,5},{8,10},{9,11},{10,... | collective-permute-start | bytes 196616 | tf_op jit(solution)/shard_map/ppermute | solution.py:508
  5.1 8.3 %collective-permute-start.1 = (bf16[64,512]{1,0:T(8,128)(2,1)S(1)}, bf16[64,512]{1,0:T(8,128)(2,1)S(1)}, u32[]{:S(2)}, u32[]{:S(2)}) collective-permute-start(bf16[64,512]{1,0:T(8,128)(2,1)S(1)} %get-tuple-element.61), channel_id=1, source_target_pairs={{0,14},{1,15},{2,4},{3,5},{4,2},{5,3},{6,8},{7,9},{8,6},{9,7},{10,... | collective-permute-start | bytes 196616 | tf_op jit(solution)/shard_map/ppermute | solution.py:508
  8.6 4.8 %collective-permute-start.2 = (bf16[64,512]{1,0:T(8,128)(2,1)S(1)}, bf16[64,512]{1,0:T(8,128)(2,1)S(1)}, u32[]{:S(2)}, u32[]{:S(2)}) collective-permute-start(bf16[64,512]{1,0:T(8,128)(2,1)S(1)} %get-tuple-element.62), channel_id=1, source_target_pairs={{0,4},{1,5},{2,6},{3,7},{4,0},{5,1},{6,2},{7,3},{8,12},{9,13},{10,... | collective-permute-start | bytes 196616 | tf_op jit(solution)/shard_map/ppermute | solution.py:508
  8.6 6.1 %collective-permute-start.3 = (bf16[64,512]{1,0:T(8,128)(2,1)S(1)}, bf16[64,512]{1,0:T(8,128)(2,1)S(1)}, u32[]{:S(2)}, u32[]{:S(2)}) collective-permute-start(bf16[64,512]{1,0:T(8,128)(2,1)S(1)} %get-tuple-element.63), channel_id=1, source_target_pairs={{0,12},{1,13},{2,14},{3,15},{4,8},{5,9},{6,10},{7,11},{8,4},{9,5},... | collective-permute-start | bytes 196616 | tf_op jit(solution)/shard_map/ppermute | solution.py:508
  10.2 0.7 %copy-start = (s32[1,2,7]{2,1,0:T(2,128)S(1)}, s32[1,2,7]{2,1,0:T(2,128)}, u32[]{:S(2)}) copy-start(s32[1,2,7]{2,1,0:T(2,128)} %pairs_ref.1) | copy-start | bytes 172
  17.7 5.5 %collective-permute-start.9 = (bf16[512,1024]{1,0:T(8,128)(2,1)S(1)}, bf16[512,1024]{1,0:T(8,128)(2,1)S(1)}, u32[]{:S(2)}, u32[]{:S(2)}) collective-permute-start(bf16[512,1024]{1,0:T(8,128)(2,1)S(1)} %get-tuple-element.77), channel_id=1, source_target_pairs={{0,1},{1,0},{2,3},{3,2},{4,5},{5,4},{6,7},{7,6},{8,9},{9,8},{10,11... | collective-permute-start | bytes 3145736 | tf_op jit(solution)/shard_map/ppermute | solution.py:515
  17.8 6.2 %collective-permute-start.5 = (bf16[64,512]{1,0:T(8,128)(2,1)S(1)}, bf16[64,512]{1,0:T(8,128)(2,1)S(1)}, u32[]{:S(2)}, u32[]{:S(2)}) collective-permute-start(bf16[64,512]{1,0:T(8,128)(2,1)S(1)} %get-tuple-element.73), channel_id=1, source_target_pairs={{0,3},{1,2},{2,1},{3,0},{4,7},{5,6},{6,5},{7,4},{8,11},{9,10},{10,... | collective-permute-start | bytes 196616 | tf_op jit(solution)/shard_map/ppermute | solution.py:508
  19.2 6.9 %collective-permute-start.6 = (bf16[64,512]{1,0:T(8,128)(2,1)S(1)}, bf16[64,512]{1,0:T(8,128)(2,1)S(1)}, u32[]{:S(2)}, u32[]{:S(2)}) collective-permute-start(bf16[64,512]{1,0:T(8,128)(2,1)S(1)} %get-tuple-element.74), channel_id=1, source_target_pairs={{0,15},{1,14},{2,5},{3,4},{4,3},{5,2},{6,9},{7,8},{8,7},{9,6},{10,... | collective-permute-start | bytes 196616 | tf_op jit(solution)/shard_map/ppermute | solution.py:508
  21.7 4.4 %collective-permute-start.7 = (bf16[64,512]{1,0:T(8,128)(2,1)S(1)}, bf16[64,512]{1,0:T(8,128)(2,1)S(1)}, u32[]{:S(2)}, u32[]{:S(2)}) collective-permute-start(bf16[64,512]{1,0:T(8,128)(2,1)S(1)} %get-tuple-element.75), channel_id=1, source_target_pairs={{0,5},{1,4},{2,7},{3,6},{4,1},{5,0},{6,3},{7,2},{8,13},{9,12},{10,... | collective-permute-start | bytes 196616 | tf_op jit(solution)/shard_map/ppermute | solution.py:508
  21.7 5.7 %collective-permute-start.8 = (bf16[64,512]{1,0:T(8,128)(2,1)S(1)}, bf16[64,512]{1,0:T(8,128)(2,1)S(1)}, u32[]{:S(2)}, u32[]{:S(2)}) collective-permute-start(bf16[64,512]{1,0:T(8,128)(2,1)S(1)} %get-tuple-element.76), channel_id=1, source_target_pairs={{0,13},{1,12},{2,15},{3,14},{4,9},{5,8},{6,11},{7,10},{8,5},{9,4},... | collective-permute-start | bytes 196616 | tf_op jit(solution)/shard_map/ppermute | solution.py:508
  30.5 18.4 %collective-permute-start.10 = (bf16[928,512]{1,0:T(8,128)(2,1)S(1)}, bf16[928,512]{1,0:T(8,128)(2,1)S(1)}, u32[]{:S(2)}, u32[]{:S(2)}) collective-permute-start(bf16[928,512]{1,0:T(8,128)(2,1)S(1)} %get-tuple-element.95), channel_id=1, source_target_pairs={{0,4},{1,3},{2,6},{3,1},{4,0},{5,7},{6,2},{7,5},{8,12},{9,11},{10,... | collective-permute-start | bytes 2850824 | tf_op jit(solution)/shard_map/ppermute | solution.py:518
  32.4 16.4 %collective-permute-start.11 = (bf16[128,512]{1,0:T(8,128)(2,1)S(1)}, bf16[128,512]{1,0:T(8,128)(2,1)S(1)}, u32[]{:S(2)}, u32[]{:S(2)}) collective-permute-start(bf16[128,512]{1,0:T(8,128)(2,1)S(1)} %get-tuple-element.97), channel_id=1, source_target_pairs={{0,12},{2,14},{4,8},{6,10},{8,4},{10,6},{12,0},{14,2},{16,28},{18,... | collective-permute-start | bytes 393224 | tf_op jit(solution)/shard_map/ppermute | solution.py:508
  49.0 9.4 %collective-permute-start.12 = (bf16[528,512]{1,0:T(8,128)(2,1)S(1)}, bf16[528,512]{1,0:T(8,128)(2,1)S(1)}, u32[]{:S(2)}, u32[]{:S(2)}) collective-permute-start(bf16[528,512]{1,0:T(8,128)(2,1)S(1)} %get-tuple-element.102), channel_id=1, source_target_pairs={{0,2},{1,5},{2,0},{3,7},{4,6},{5,1},{6,4},{7,3},{8,10},{9,13},{10,... | collective-permute-start | bytes 1622024 | tf_op jit(solution)/shard_map/ppermute | solution.py:518
  50.3 8.3 %collective-permute-start.13 = (bf16[512,512]{1,0:T(8,128)(2,1)S(1)}, bf16[512,512]{1,0:T(8,128)(2,1)S(1)}, u32[]{:S(2)}, u32[]{:S(2)}) collective-permute-start(bf16[512,512]{1,0:T(8,128)(2,1)S(1)} %get-tuple-element.103), channel_id=1, source_target_pairs={{0,1},{1,0},{2,3},{3,2},{4,5},{5,4},{6,7},{7,6},{8,9},{9,8},{10,11... | collective-permute-start | bytes 1572872 | tf_op jit(solution)/shard_map/ppermute | solution.py:515
  58.5 8.6 %collective-permute-start.14 = (bf16[200,512]{1,0:T(8,128)(2,1)S(1)}, bf16[200,512]{1,0:T(8,128)(2,1)S(1)}, u32[]{:S(2)}, u32[]{:S(2)}) collective-permute-start(bf16[200,512]{1,0:T(8,128)(2,1)S(1)} %get-tuple-element.106), channel_id=1, source_target_pairs={{0,8},{1,9},{2,10},{3,11},{4,12},{5,13},{6,14},{7,15},{8,0},{9,1},... | collective-permute-start | bytes 614408 | tf_op jit(solution)/shard_map/ppermute | solution.py:518

commit v5 on v4

--- a/solution.py
+++ b/solution.py
@@ -369,7 +369,7 @@
 
 def third_kernel(
     gpre_ref, gpn_ref, sums_ref, back_ref, w_agg_ref, la_ref, lb_ref, keep1_ref, send1_ref,
-    keep_ref, send_ref, far_ref, near_ref, gm_ref, t_ref,
+    keep_ref, send_ref, near_ref, far_ref, gm_ref, t_ref,
 ):
     ride = near_ref.shape[0]
     first = send1_ref.shape[0]
@@ -378,11 +378,8 @@
     def _():
         weight_products(la_ref, lb_ref, gpre_ref, gpn_ref, sums_ref[...], keep_ref, send_ref)
         message_grads(gpre_ref, back_ref, w_agg_ref, gm_ref, t_ref)
-        cross_ref = send_ref.at[pl.ds(first + ride, ride), :]
-        put_halo_grads(
-            t_ref,
-            (near_ref, cross_ref, send_ref.at[pl.ds(first, ride), :], far_ref.at[pl.ds(0, ride), :]),
-        )
+        below, cross = (send_ref.at[pl.ds(first + i * ride, ride), :] for i in (0, 1))
+        put_halo_grads(t_ref, (near_ref, cross, below, far_ref.at[pl.ds(0, ride), :]))
         far_ref[ride:, :] = send_ref[first + ride :, :]
 
     @on_core(1)
@@ -406,30 +403,22 @@
         keep2[i] = keep[d] + recv[at, :].astype(F32)
 
 
-def carry_kernel(keep, recv, near_ref, far_ref, _, keep2, send2):
+def carry_kernel(keep, recv, near_ref, _, keep2, send2):
     ride = near_ref.shape[0]
     halve_job(second_bit(), keep, recv, keep2, send2)
     at = keep2.shape[0] * keep2.shape[1]
-    inner = dom_bit(0) == dom_bit(1)
 
     @on_core(0)
     def _():
         send2[at : at + ride, :] = near_ref[...]
-
-        @pl.when(inner)
-        def _():
-            send2[at + ride :, :] = recv[recv.shape[0] - ride :, :]
-
-        @pl.when(jnp.logical_not(inner))
-        def _():
-            send2[at + ride :, :] = far_ref[ride:, :]
-
-
-def halve_kernel(keep, recv, keep2, send2):
+        send2[at + ride :, :] = recv[recv.shape[0] - ride :, :]
+
+
+def halve_kernel(keep, recv, _, keep2, send2):
     halve_job(dom_bit(2), keep, recv, keep2, send2)
 
 
-def last_kernel(keep, recv, node_ref, agg_ref, out_ref, bias_ref, gain_ref):
+def sums_out(keep, recv, node_ref, agg_ref, out_ref, bias_ref, gain_ref):
     share = node_ref.shape[0]
     total = keep[0] + recv[...].astype(F32)
     node_ref[...] = total[0:share]
@@ -439,9 +428,10 @@
     gain_ref[...] = total[3 * share + 1 : 3 * share + 2]
 
 
-def cot_kernel(skips, onehot_ref, r0, r1, r2, r3, cpart_ref, other_ref, cot_ref):
+def cot_out(skips, onehot_ref, sources, cpart_ref, other_ref, cot_ref):
     micro, rows, feat = cot_ref.shape
     n = onehot_ref.shape[1] // PEERS
+    inner = dom_bit(0) != dom_bit(1)
 
     @on_core(1)
     def _():
@@ -451,12 +441,24 @@
     @on_core(0)
     def _():
         for m in range(micro):
-            ret = jnp.concatenate(
-                [r[s + m * n : s + (m + 1) * n, :] for r, s in zip((r0, r1, r2, r3), skips)], 0
-            )
+            got = [r[s + m * n : s + (m + 1) * n, :] for r, s in zip(sources, skips)]
+            if len(got) > PEERS:
+                got[1] = jnp.where(inner, got[1], got.pop())
+            ret = jnp.concatenate(got, 0)
             cot_ref[m] = (
                 cpart_ref[m * rows : (m + 1) * rows, :] + nn_dot(onehot_ref[...], ret)
             ).astype(BF16)
+
+
+def final_kernel(skips, onehot_ref, *rest):
+    *sources, cpart_ref, other_ref, keep, recv, cot_ref, node_ref, agg_ref, out_ref, bias_ref, gain_ref = rest
+    cot_out(skips, onehot_ref, sources, cpart_ref, other_ref, cot_ref)
+    sums_out(keep, recv, node_ref, agg_ref, out_ref, bias_ref, gain_ref)
+
+
+def cot_kernel(skips, onehot_ref, *rest):
+    *sources, cpart_ref, other_ref, cot_ref = rest
+    cot_out(skips, onehot_ref, sources, cpart_ref, other_ref, cot_ref)
 
 
 def whole_kernel(x_ref, agg_ref, hidden_ref, gpn_ref, gpre_ref, node_ref, agg_out, out_ref):
@@ -595,9 +597,10 @@
     scr_t, gm_out = pltpu.VMEM((halo_rows, wide), F32), shape((rows, wide), BF16)
     if halving:
         ride = chunk.shape[0]
-        keep, send, far, near, gm = call(
+        ride = chunk.shape[0]
+        keep, send, near, far, gm = call(
             third_kernel,
-            kept(4, 2 * ride) + [shape((2 * ride, feat), BF16), chunk, gm_out],
+            kept(4, 2 * ride) + [chunk, shape((2 * ride, feat), BF16), gm_out],
             [scr_t], 4 * matmul, 16 * size,
             gpre, gpn, sums, halo_back, w_a, *turned,
         )
@@ -612,21 +615,28 @@
         lower_kernel, [f_full, b_full], [], matmul, 10 * size, g_low, gpre, gm, local_back, w_n
     )
     other = across(g_low)
-    skips = (0,) * slots
+    cot_shape = shape((micro, rows, feat), BF16)
     if halving:
         up = recv
         keep, send = call(
-            carry_kernel, kept(2, 2 * ride), [], size, 8 * size, keep, recv, near, far, cpart0,
+            carry_kernel, kept(2, 2 * ride), [], size, 8 * size, keep, recv, near, cpart0,
             after=1,
         )
         recv = flipped(send, (0, 1))
+        hop = swapped(far, 0, ((0, 0),))
         first = 2 * rows_each
-        returned, skips = (recv, recv, up, far), (first, first + ride, 2 * first, 0)
-        keep, send = call(halve_kernel, kept(1), [], size, 4 * size, keep, recv)
+        returned = (recv, recv, up, far, hop)
+        skips = (first, first + ride, 2 * first, 0, ride)
+        keep, send = call(
+            halve_kernel, kept(1), [], size, 4 * size, keep, recv, far,
+            after=1,
+        )
         recv = flipped(send, (2, 2))
         part, row = shape((share, feat), F32), shape((1, feat), F32)
-        grad_node, grad_agg, grad_out, grad_bias, grad_gain = call(
-            last_kernel, [part, part, part, row, row], [], size, 2 * size, keep, recv,
+        cot, grad_node, grad_agg, grad_out, grad_bias, grad_gain = call(
+            functools.partial(final_kernel, skips), [cot_shape, part, part, part, row, row],
+            [], matmul // 4, 6 * size,
+            onehot, *returned, cpart0, other, keep, recv,
         )
     else:
         is_last = segment == 1
@@ -642,10 +652,10 @@
         sums = lax.psum(sums, "dom")
         grad_bias, grad_gain = sums[0:1], sums[1:2]
         returned = [swapped(v, k, ((0, 0),)) for k, v in enumerate(to_return)]
-    cot = call(
-        functools.partial(cot_kernel, skips), shape((micro, rows, feat), BF16), [], matmul // 4, 4 * size,
-        onehot, *returned, cpart0, other,
-    )
+        cot = call(
+            functools.partial(cot_kernel, (0,) * slots), cot_shape, [], matmul // 4, 4 * size,
+            onehot, *returned, cpart0, other,
+        )
     return (
         cot[None],
         grad_node[None],

time: 68.2 us -> 66.4 us (0.974)
  waiting for transfers between devices: 32.6 us -> 25.8 us
  starting transfers between devices: 19.2 us -> 24.9 us
    ppermute x9 -> x10, starting transfers between devices: 15.3 us -> 19.9 us  [swapped(): lax.ppermute(v, ('dom', 'segment'), [(2 * p + s, 2 * swap_partner(p, k) +...]
    ppermute x3, waiting for transfers between devices: 15.6 us -> 12 us  [flipped(): lax.ppermute(v, ('dom', 'segment'), [(2 * p + s, 2 * (p ^ 1 << bits[s]) +...]
    ppermute x9 -> x10, waiting for transfers between devices: 17 us -> 13.7 us  [swapped(): lax.ppermute(v, ('dom', 'segment'), [(2 * p + s, 2 * swap_partner(p, k) +...]
    ppermute x3, starting transfers between devices: 3.32 us -> 4.34 us  [flipped(): lax.ppermute(v, ('dom', 'segment'), [(2 * p + s, 2 * (p ^ 1 << bits[s]) +...]
    pallas_call x12 -> x11, Pallas kernels: 14 us -> 13.4 us  [call(): pl.pallas_call(kernel, out_shape=outs, in_specs=[SMEM] * scalars + [HBM]...]
  transfers between devices with their start and end apart: 15 -> 16, of which waited for: 6 -> 7; matrix products, arithmetic and copies ran while one was open for 0% -> 0% of each run, Pallas kernels for 11% -> 9%
where the time goes in v5:
time: 66.4 us; the launch traced here: 66.2 us
  waiting for transfers between devices  25.8 us (39%)
  starting transfers between devices  24.9 us (38%)
  Pallas kernels  13.4 us (20%)
  between operations  1.44 us (2%)
  local copies, waits for them, and re-layouts  0.67 us (1%)
    ppermute x10, starting transfers between devices, swapped(): lax.ppermute(v, ('dom', 'segment'), [(2 * p + s, 2 * swap_partner(p, k) +...  19.9 us
    ppermute x10, waiting for transfers between devices, swapped(): lax.ppermute(v, ('dom', 'segment'), [(2 * p + s, 2 * swap_partner(p, k) +...  13.7 us
    pallas_call x11, Pallas kernels, call(): pl.pallas_call(kernel, out_shape=outs, in_specs=[SMEM] * scalars + [HBM]...  13.4 us
    ppermute x3, waiting for transfers between devices, flipped(): lax.ppermute(v, ('dom', 'segment'), [(2 * p + s, 2 * (p ^ 1 << bits[s]) +...  12 us
    ppermute x3, starting transfers between devices, flipped(): lax.ppermute(v, ('dom', 'segment'), [(2 * p + s, 2 * (p ^ 1 << bits[s]) +...  4.34 us
  transfers between devices with their start and end apart: 16, of which 7 were waited for; matrix products, arithmetic and copies ran while one was open for 0% of the time, Pallas kernels for 9%

profile of v5, /device:TPU:0, one launch (start us, length us, event | category | flops | bytes accessed | tf_op | source)
XLA Modules:
  0.0 66.2 jit_solution(2257071916801456131)
XLA Ops:
  0.6 0.5 collective-permute-start.4
  1.1 1.3 %shard_map.154 = (bf16[64,512]{1,0:T(8,128)(2,1)S(1)}, bf16[64,512]{1,0:T(8,128)(2,1)S(1)}, bf16[64,512]{1,0:T(8,128)(2,1)S(1)}, bf16[64,512]{1,0:T(8,128)(2,1)S...) custom-call(s32[1,4,32]{2,1,0:T(4,128)} %targets_hbm.1, bf16[2,256,512]{2,1,0:T(8,128)(2,1)} %bitcast.9), custom_call_target="tpu_custom_call" | custom-call | flops 33554432 | bytes 524288 | tf_op jit(solution)/shard_map/pallas_call | solution.py:43
  2.5 2.6 %collective-permute-start = (bf16[64,512]{1,0:T(8,128)(2,1)S(1)}, bf16[64,512]{1,0:T(8,128)(2,1)S(1)}, u32[]{:S(2)}, u32[]{:S(2)}) collective-permute-start(bf16[64,512]{1,0:T(8,128)(2,1)S(1)} %get-tuple-element.61), channel_id=1, source_target_pairs={{0,2},{1,3},{2,0},{3,1},{4,6},{5,7},{6,4},{7,5},{8,10},{9,11},{10,... | collective-permute-start | bytes 196616 | tf_op jit(solution)/shard_map/ppermute | solution.py:510
  5.1 3.6 %collective-permute-start.1 = (bf16[64,512]{1,0:T(8,128)(2,1)S(1)}, bf16[64,512]{1,0:T(8,128)(2,1)S(1)}, u32[]{:S(2)}, u32[]{:S(2)}) collective-permute-start(bf16[64,512]{1,0:T(8,128)(2,1)S(1)} %get-tuple-element.62), channel_id=1, source_target_pairs={{0,14},{1,15},{2,4},{3,5},{4,2},{5,3},{6,8},{7,9},{8,6},{9,7},{10,... | collective-permute-start | bytes 196616 | tf_op jit(solution)/shard_map/ppermute | solution.py:510
  8.6 0.0 collective-permute-start.2
  8.6 0.9 %collective-permute-start.3 = (bf16[64,512]{1,0:T(8,128)(2,1)S(1)}, bf16[64,512]{1,0:T(8,128)(2,1)S(1)}, u32[]{:S(2)}, u32[]{:S(2)}) collective-permute-start(bf16[64,512]{1,0:T(8,128)(2,1)S(1)} %get-tuple-element.64), channel_id=1, source_target_pairs={{0,12},{1,13},{2,14},{3,15},{4,8},{5,9},{6,10},{7,11},{8,4},{9,5},... | collective-permute-start | bytes 196616 | tf_op jit(solution)/shard_map/ppermute | solution.py:510
  10.2 0.0 copy-start
  10.2 0.7 %copy-done = s32[1,2,7]{2,1,0:T(2,128)S(1)} copy-done((s32[1,2,7]{2,1,0:T(2,128)S(1)}, s32[1,2,7]{2,1,0:T(2,128)}, u32[]{:S(2)}) %copy-start) | copy-done | bytes 80
  10.9 2.5 %shard_map.155 = (f32[512,512]{1,0:T(8,128)S(1)}, f32[256,1024]{1,0:T(8,128)S(1)}, bf16[2,256,128]{2,1,0:T(8,128)(2,1)S(1)}, bf16[2,256,256]{2,1,0:T(8,128)(2,1)...) custom-call(s32[1,2,7]{2,1,0:T(2,128)S(1)} %copy-done, ...), custom_call_target="tpu_custom_call" | custom-call | flops 536870912 | bytes 2097152 | tf_op jit(solution)/shard_map/pallas_call | solution.py:43
  13.4 0.0 collective-permute-done.h0
  13.4 0.0 collective-permute-done.1.h1
  13.4 0.0 collective-permute-done.2.h2
  13.4 1.3 %collective-permute-done.3.h3 = bf16[64,512]{1,0:T(8,128)(2,1)S(1)} collective-permute-done((bf16[64,512]{1,0:T(8,128)(2,1)S(1)}, bf16[64,512]{1,0:T(8,128)(2,1)S(1)}, u32[]{:S(2)}, u32[]{:S(2)}) %collective-permute-start.3) | collective-permute-done | bytes 65568 | tf_op jit(solution)/shard_map/ppermute | solution.py:510
  14.8 0.0 collective-permute-done.4._.w_node_ref
  14.8 2.9 %shard_map.156 = (bf16[64,512]{1,0:T(8,128)(2,1)S(1)}, bf16[64,512]{1,0:T(8,128)(2,1)S(1)}, bf16[64,512]{1,0:T(8,128)(2,1)S(1)}, bf16[64,512]{1,0:T(8,128)(2,1)S...) custom-call(bf16[64,512]{1,0:T(8,128)(2,1)S(1)} %collective-permute-, ...), custom_call_target="tpu_custom_call" | custom-call | flops 1073741824 | bytes 5242880 | tf_op jit(solution)/shard_map/pallas_call | solution.py:43
  17.7 0.1 collective-permute-start.9
  17.8 1.4 %collective-permute-start.5 = (bf16[64,512]{1,0:T(8,128)(2,1)S(1)}, bf16[64,512]{1,0:T(8,128)(2,1)S(1)}, u32[]{:S(2)}, u32[]{:S(2)}) collective-permute-start(bf16[64,512]{1,0:T(8,128)(2,1)S(1)} %get-tuple-element.74), channel_id=1, source_target_pairs={{0,3},{1,2},{2,1},{3,0},{4,7},{5,6},{6,5},{7,4},{8,11},{9,10},{10,... | collective-permute-start | bytes 196616 | tf_op jit(solution)/shard_map/ppermute | solution.py:510
  19.2 2.5 %collective-permute-start.6 = (bf16[64,512]{1,0:T(8,128)(2,1)S(1)}, bf16[64,512]{1,0:T(8,128)(2,1)S(1)}, u32[]{:S(2)}, u32[]{:S(2)}) collective-permute-start(bf16[64,512]{1,0:T(8,128)(2,1)S(1)} %get-tuple-element.75), channel_id=1, source_target_pairs={{0,15},{1,14},{2,5},{3,4},{4,3},{5,2},{6,9},{7,8},{8,7},{9,6},{10,... | collective-permute-start | bytes 196616 | tf_op jit(solution)/shard_map/ppermute | solution.py:510
  21.7 0.0 collective-permute-start.7
  21.7 0.9 %collective-permute-start.8 = (bf16[64,512]{1,0:T(8,128)(2,1)S(1)}, bf16[64,512]{1,0:T(8,128)(2,1)S(1)}, u32[]{:S(2)}, u32[]{:S(2)}) collective-permute-start(bf16[64,512]{1,0:T(8,128)(2,1)S(1)} %get-tuple-element.77), channel_id=1, source_target_pairs={{0,13},{1,12},{2,15},{3,14},{4,9},{5,8},{6,11},{7,10},{8,5},{9,4},... | collective-permute-start | bytes 196616 | tf_op jit(solution)/shard_map/ppermute | solution.py:510
  22.6 0.6 shard_map.159
  23.2 0.0 collective-permute-done.9.both_ref
  23.2 0.8 %shard_map.157.refs_5_ = f32[512,512]{1,0:T(8,128)S(1)} custom-call(bf16[2,256,512]{2,1,0:T(8,128)(2,1)S(1)} %get-tuple-element.70.g_ref, bf16[512,1024]{1,0:T(8,128)(2,1)S(1)} %collective-permute-done.9.both_ref, bf16[2,256,256]{2,1,0:T(8,128)(2,1)S(1)} %get-tuple-element.79.back_ref, bf16[512,512]{1,0:T(8,128)(2,1)S(1)} %collective-permute-done.4._.w_node_ref), custom_call_target="tpu_custom_call" | custom-call | flops 268435456 | bytes 2621440 | tf_op jit(solution)/shard_map/pallas_call | solution.py:43
  24.0 0.0 collective-permute-done.5.refs_1_
  24.0 2.1 %collective-permute-done.6.refs_2_ = bf16[64,512]{1,0:T(8,128)(2,1)S(1)} collective-permute-done((bf16[64,512]{1,0:T(8,128)(2,1)S(1)}, bf16[64,512]{1,0:T(8,128)(2,1)S(1)}, u32[]{:S(2)}, u32[]{:S(2)}) %collective-permute-start.6) | collective-permute-done | bytes 65568 | tf_op jit(solution)/shard_map/ppermute | solution.py:510
  26.1 0.0 collective-permute-done.7.refs_3_
  26.2 1.3 %collective-permute-done.8.refs_4_ = bf16[64,512]{1,0:T(8,128)(2,1)S(1)} collective-permute-done((bf16[64,512]{1,0:T(8,128)(2,1)S(1)}, bf16[64,512]{1,0:T(8,128)(2,1)S(1)}, u32[]{:S(2)}, u32[]{:S(2)}) %collective-permute-start.8) | collective-permute-done | bytes 65568 | tf_op jit(solution)/shard_map/ppermute | solution.py:510
  27.5 1.2 %shard_map.158 = (bf16[512,512]{1,0:T(8,128)(2,1)S(1)}, bf16[512,512]{1,0:T(8,128)(2,1)S(1)}, bf16[512,512]{1,0:T(8,128)(2,1)S(1)}, f32[8,512]{1,0:T(8,128)S(1)}) custom-call(bf16[256,128]{1,0:T(8,128)(2,1)S(1)} %get-tuple-element.60.refs_0_.onehot_ref, bf16[64,512]{1,0:T(8,128)(2,1)S(1)} %collective-permute-done.5.refs_1_, ...), custom_call_target="tpu_custom_call" | custom-call | flops 536870912 | bytes 4194304 | tf_op jit(solution)/shard_map/pallas_call | solution.py:43
  28.6 1.8 %shard_map.160 = (f32[4,200,512]{2,1,0:T(8,128)S(1)}, bf16[928,512]{1,0:T(8,128)(2,1)S(1)}, bf16[64,512]{1,0:T(8,128)(2,1)S(1)}, bf16[128,512]{1,0:T(8,128)(2,1)S(1)}, bf16[256,1024]{1,0:T(8,128)(2,1)S(1)}) custom-call(bf16[512,512]{1,0:T(8,128)(2,1)S(1)} %get-tuple-element.83.gpre_ref, bf16[512,512]{1,0:T(8,128)(2,1)S(1)} %get-tuple-element.84.gpn_ref, ...), custom_call_target="tpu_custom_call" | custom-call | flops 1073741824 | bytes 4194304 | tf_op jit(solution)/shard_map/pallas_call | solution.py:43
  30.5 2.0 %collective-permute-start.10 = (bf16[928,512]{1,0:T(8,128)(2,1)S(1)}, bf16[928,512]{1,0:T(8,128)(2,1)S(1)}, u32[]{:S(2)}, u32[]{:S(2)}) collective-permute-start(bf16[928,512]{1,0:T(8,128)(2,1)S(1)} %get-tuple-element.96), channel_id=1, source_target_pairs={{0,4},{1,3},{2,6},{3,1},{4,0},{5,7},{6,2},{7,5},{8,12},{9,11},{10,... | collective-permute-start | bytes 2850824 | tf_op jit(solution)/shard_map/ppermute | solution.py:520
  32.4 0.8 %shard_map.161 = (f32[512,512]{1,0:T(8,128)S(1)}, bf16[512,512]{1,0:T(8,128)(2,1)S(1)}) custom-call(bf16[512,512]{1,0:T(8,128)(2,1)S(1)} %get-tuple-element.98.g_ref, bf16[512,512]{1,0:T(8,128)(2,1)S(1)} %get-tuple-element.83.gpre_ref, bf16[256,1024]{1,0:T(8,128)(2,1)S(1)} %get-tuple-element.99.gm_ref, bf16[2,256,256]{2,1,0:T(8,128)(2,1)S(1)} %get-tuple-element.79.back_ref, ...), custom_call_target="tpu_custom_call" | custom-call | flops 268435456 | bytes 2621440 | tf_op jit(solution)/shard_map/pallas_call | solution.py:43
  33.2 11.5 %collective-permute-done.10.recv.rest_2_ = bf16[928,512]{1,0:T(8,128)(2,1)S(1)} collective-permute-done((bf16[928,512]{1,0:T(8,128)(2,1)S(1)}, bf16[928,512]{1,0:T(8,128)(2,1)S(1)}, u32[]{:S(2)}, u32[]{:S(2)}) %collective-permute-start.10) | collective-permute-done | bytes 950304 | tf_op jit(solution)/shard_map/ppermute | solution.py:520
  44.7 0.2 shard_map.162
  44.9 2.3 %collective-permute-start.11 = (bf16[528,512]{1,0:T(8,128)(2,1)S(1)}, bf16[528,512]{1,0:T(8,128)(2,1)S(1)}, u32[]{:S(2)}, u32[]{:S(2)}) collective-permute-start(bf16[528,512]{1,0:T(8,128)(2,1)S(1)} %get-tuple-element.102), channel_id=1, source_target_pairs={{0,2},{1,5},{2,0},{3,7},{4,6},{5,1},{6,4},{7,3},{8,10},{9,13},{10,... | collective-permute-start | bytes 1622024 | tf_op jit(solution)/shard_map/ppermute | solution.py:520
  47.2 0.0 collective-permute-start.14
  47.2 3.4 %collective-permute-start.12 = (bf16[128,512]{1,0:T(8,128)(2,1)S(1)}, bf16[128,512]{1,0:T(8,128)(2,1)S(1)}, u32[]{:S(2)}, u32[]{:S(2)}) collective-permute-start(bf16[128,512]{1,0:T(8,128)(2,1)S(1)} %get-tuple-element.103), channel_id=1, source_target_pairs={{0,12},{2,14},{4,8},{6,10},{8,4},{10,6},{12,0},{14,2},{16,28},{18,... | collective-permute-start | bytes 393224 | tf_op jit(solution)/shard_map/ppermute | solution.py:510
  50.6 6.0 %collective-permute-done.12._.rest_3_ = bf16[128,512]{1,0:T(8,128)(2,1)S(1)} collective-permute-done((bf16[128,512]{1,0:T(8,128)(2,1)S(1)}, bf16[128,512]{1,0:T(8,128)(2,1)S(1)}, u32[]{:S(2)}, u32[]{:S(2)}) %collective-permute-start.12) | collective-permute-done | bytes 131104 | tf_op jit(solution)/shard_map/ppermute | solution.py:510
  56.6 0.0 collective-permute-done.11.recv.rest_0_.rest_1_
  56.6 0.1 shard_map.163
  56.7 0.1 collective-permute-start.15
  56.8 4.6 %collective-permute-start.13 = (bf16[128,512]{1,0:T(8,128)(2,1)S(1)}, bf16[128,512]{1,0:T(8,128)(2,1)S(1)}, u32[]{:S(2)}, u32[]{:S(2)}) collective-permute-start(bf16[128,512]{1,0:T(8,128)(2,1)S(1)} %collective-permute-done.12._.rest_3_), channel_id=1, source_target_pairs={{0,2},{2,0},{4,6},{6,4},{8,10},{10,8},{12,14},{14,12},{16,18},{18,... | collective-permute-start | bytes 393224 | tf_op jit(solution)/shard_map/ppermute | solution.py:510
  61.4 2.9 %collective-permute-done.13.rest_4_ = bf16[128,512]{1,0:T(8,128)(2,1)S(1)} collective-permute-done((bf16[128,512]{1,0:T(8,128)(2,1)S(1)}, bf16[128,512]{1,0:T(8,128)(2,1)S(1)}, u32[]{:S(2)}, u32[]{:S(2)}) %collective-permute-start.13) | collective-permute-done | bytes 131104 | tf_op jit(solution)/shard_map/ppermute | solution.py:510
  64.3 0.0 collective-permute-done.14.rest_6_
  64.3 0.6 collective-permute-done.15.rest_8_
  64.9 1.3 %shard_map.164 = (bf16[2,256,512]{2,1,0:T(8,128)(2,1)}, f32[64,512]{1,0:T(8,128)}, f32[64,512]{1,0:T(8,128)}, f32[64,512]{1,0:T(8,128)}, f32[1,512]{1,0:T(1,128)}, /*index=5*/f32[1,512]{1,0:T(1,128)}) custom-call(bf16[256,128]{1,0:T(8,128)(2,1)S(1)} %get-tuple-element.60.refs_0_.onehot_ref, ...), custom_call_target="tpu_custom_call" | custom-call | flops 67108864 | bytes 1572864 | tf_op jit(solution)/shard_map/pallas_call | solution.py:43
Async XLA Ops:
  0.6 14.1 %collective-permute-start.4 = (bf16[512,512]{1,0:T(8,128)(2,1)}, bf16[512,512]{1,0:T(8,128)(2,1)S(1)}, u32[]{:S(2)}, u32[]{:S(2)}) collective-permute-start(bf16[512,512]{1,0:T(8,128)(2,1)} %bitcast.12), channel_id=1, source_target_pairs={{0,1},{1,0},{2,3},{3,2},{4,5},{5,4},{6,7},{7,6},{8,9},{9,8},{10,11... | collective-permute-start | bytes 1572872 | tf_op jit(solution)/shard_map/ppermute | solution.py:517
  2.5 10.9 %collective-permute-start = (bf16[64,512]{1,0:T(8,128)(2,1)S(1)}, bf16[64,512]{1,0:T(8,128)(2,1)S(1)}, u32[]{:S(2)}, u32[]{:S(2)}) collective-permute-start(bf16[64,512]{1,0:T(8,128)(2,1)S(1)} %get-tuple-element.61), channel_id=1, source_target_pairs={{0,2},{1,3},{2,0},{3,1},{4,6},{5,7},{6,4},{7,5},{8,10},{9,11},{10,... | collective-permute-start | bytes 196616 | tf_op jit(solution)/shard_map/ppermute | solution.py:510
  5.1 8.3 %collective-permute-start.1 = (bf16[64,512]{1,0:T(8,128)(2,1)S(1)}, bf16[64,512]{1,0:T(8,128)(2,1)S(1)}, u32[]{:S(2)}, u32[]{:S(2)}) collective-permute-start(bf16[64,512]{1,0:T(8,128)(2,1)S(1)} %get-tuple-element.62), channel_id=1, source_target_pairs={{0,14},{1,15},{2,4},{3,5},{4,2},{5,3},{6,8},{7,9},{8,6},{9,7},{10,... | collective-permute-start | bytes 196616 | tf_op jit(solution)/shard_map/ppermute | solution.py:510
  8.6 4.8 %collective-permute-start.2 = (bf16[64,512]{1,0:T(8,128)(2,1)S(1)}, bf16[64,512]{1,0:T(8,128)(2,1)S(1)}, u32[]{:S(2)}, u32[]{:S(2)}) collective-permute-start(bf16[64,512]{1,0:T(8,128)(2,1)S(1)} %get-tuple-element.63), channel_id=1, source_target_pairs={{0,4},{1,5},{2,6},{3,7},{4,0},{5,1},{6,2},{7,3},{8,12},{9,13},{10,... | collective-permute-start | bytes 196616 | tf_op jit(solution)/shard_map/ppermute | solution.py:510
  8.6 6.1 %collective-permute-start.3 = (bf16[64,512]{1,0:T(8,128)(2,1)S(1)}, bf16[64,512]{1,0:T(8,128)(2,1)S(1)}, u32[]{:S(2)}, u32[]{:S(2)}) collective-permute-start(bf16[64,512]{1,0:T(8,128)(2,1)S(1)} %get-tuple-element.64), channel_id=1, source_target_pairs={{0,12},{1,13},{2,14},{3,15},{4,8},{5,9},{6,10},{7,11},{8,4},{9,5},... | collective-permute-start | bytes 196616 | tf_op jit(solution)/shard_map/ppermute | solution.py:510
  10.2 0.7 %copy-start = (s32[1,2,7]{2,1,0:T(2,128)S(1)}, s32[1,2,7]{2,1,0:T(2,128)}, u32[]{:S(2)}) copy-start(s32[1,2,7]{2,1,0:T(2,128)} %pairs_ref.1) | copy-start | bytes 172
  17.7 5.5 %collective-permute-start.9 = (bf16[512,1024]{1,0:T(8,128)(2,1)S(1)}, bf16[512,1024]{1,0:T(8,128)(2,1)S(1)}, u32[]{:S(2)}, u32[]{:S(2)}) collective-permute-start(bf16[512,1024]{1,0:T(8,128)(2,1)S(1)} %get-tuple-element.78), channel_id=1, source_target_pairs={{0,1},{1,0},{2,3},{3,2},{4,5},{5,4},{6,7},{7,6},{8,9},{9,8},{10,11... | collective-permute-start | bytes 3145736 | tf_op jit(solution)/shard_map/ppermute | solution.py:517
  17.8 6.2 %collective-permute-start.5 = (bf16[64,512]{1,0:T(8,128)(2,1)S(1)}, bf16[64,512]{1,0:T(8,128)(2,1)S(1)}, u32[]{:S(2)}, u32[]{:S(2)}) collective-permute-start(bf16[64,512]{1,0:T(8,128)(2,1)S(1)} %get-tuple-element.74), channel_id=1, source_target_pairs={{0,3},{1,2},{2,1},{3,0},{4,7},{5,6},{6,5},{7,4},{8,11},{9,10},{10,... | collective-permute-start | bytes 196616 | tf_op jit(solution)/shard_map/ppermute | solution.py:510
  19.2 6.9 %collective-permute-start.6 = (bf16[64,512]{1,0:T(8,128)(2,1)S(1)}, bf16[64,512]{1,0:T(8,128)(2,1)S(1)}, u32[]{:S(2)}, u32[]{:S(2)}) collective-permute-start(bf16[64,512]{1,0:T(8,128)(2,1)S(1)} %get-tuple-element.75), channel_id=1, source_target_pairs={{0,15},{1,14},{2,5},{3,4},{4,3},{5,2},{6,9},{7,8},{8,7},{9,6},{10,... | collective-permute-start | bytes 196616 | tf_op jit(solution)/shard_map/ppermute | solution.py:510
  21.7 4.4 %collective-permute-start.7 = (bf16[64,512]{1,0:T(8,128)(2,1)S(1)}, bf16[64,512]{1,0:T(8,128)(2,1)S(1)}, u32[]{:S(2)}, u32[]{:S(2)}) collective-permute-start(bf16[64,512]{1,0:T(8,128)(2,1)S(1)} %get-tuple-element.76), channel_id=1, source_target_pairs={{0,5},{1,4},{2,7},{3,6},{4,1},{5,0},{6,3},{7,2},{8,13},{9,12},{10,... | collective-permute-start | bytes 196616 | tf_op jit(solution)/shard_map/ppermute | solution.py:510
  21.7 5.7 %collective-permute-start.8 = (bf16[64,512]{1,0:T(8,128)(2,1)S(1)}, bf16[64,512]{1,0:T(8,128)(2,1)S(1)}, u32[]{:S(2)}, u32[]{:S(2)}) collective-permute-start(bf16[64,512]{1,0:T(8,128)(2,1)S(1)} %get-tuple-element.77), channel_id=1, source_target_pairs={{0,13},{1,12},{2,15},{3,14},{4,9},{5,8},{6,11},{7,10},{8,5},{9,4},... | collective-permute-start | bytes 196616 | tf_op jit(solution)/shard_map/ppermute | solution.py:510
  30.5 14.2 %collective-permute-start.10 = (bf16[928,512]{1,0:T(8,128)(2,1)S(1)}, bf16[928,512]{1,0:T(8,128)(2,1)S(1)}, u32[]{:S(2)}, u32[]{:S(2)}) collective-permute-start(bf16[928,512]{1,0:T(8,128)(2,1)S(1)} %get-tuple-element.96), channel_id=1, source_target_pairs={{0,4},{1,3},{2,6},{3,1},{4,0},{5,7},{6,2},{7,5},{8,12},{9,11},{10,... | collective-permute-start | bytes 2850824 | tf_op jit(solution)/shard_map/ppermute | solution.py:520
  44.9 11.7 %collective-permute-start.11 = (bf16[528,512]{1,0:T(8,128)(2,1)S(1)}, bf16[528,512]{1,0:T(8,128)(2,1)S(1)}, u32[]{:S(2)}, u32[]{:S(2)}) collective-permute-start(bf16[528,512]{1,0:T(8,128)(2,1)S(1)} %get-tuple-element.102), channel_id=1, source_target_pairs={{0,2},{1,5},{2,0},{3,7},{4,6},{5,1},{6,4},{7,3},{8,10},{9,13},{10,... | collective-permute-start | bytes 1622024 | tf_op jit(solution)/shard_map/ppermute | solution.py:520
  47.2 17.2 %collective-permute-start.14 = (bf16[512,512]{1,0:T(8,128)(2,1)S(1)}, bf16[512,512]{1,0:T(8,128)(2,1)S(1)}, u32[]{:S(2)}, u32[]{:S(2)}) collective-permute-start(bf16[512,512]{1,0:T(8,128)(2,1)S(1)} %get-tuple-element.104), channel_id=1, source_target_pairs={{0,1},{1,0},{2,3},{3,2},{4,5},{5,4},{6,7},{7,6},{8,9},{9,8},{10,11... | collective-permute-start | bytes 1572872 | tf_op jit(solution)/shard_map/ppermute | solution.py:517
  47.2 9.4 %collective-permute-start.12 = (bf16[128,512]{1,0:T(8,128)(2,1)S(1)}, bf16[128,512]{1,0:T(8,128)(2,1)S(1)}, u32[]{:S(2)}, u32[]{:S(2)}) collective-permute-start(bf16[128,512]{1,0:T(8,128)(2,1)S(1)} %get-tuple-element.103), channel_id=1, source_target_pairs={{0,12},{2,14},{4,8},{6,10},{8,4},{10,6},{12,0},{14,2},{16,28},{18,... | collective-permute-start | bytes 393224 | tf_op jit(solution)/shard_map/ppermute | solution.py:510
  56.7 8.2 %collective-permute-start.15 = (bf16[200,512]{1,0:T(8,128)(2,1)S(1)}, bf16[200,512]{1,0:T(8,128)(2,1)S(1)}, u32[]{:S(2)}, u32[]{:S(2)}) collective-permute-start(bf16[200,512]{1,0:T(8,128)(2,1)S(1)} %get-tuple-element.107), channel_id=1, source_target_pairs={{0,8},{1,9},{2,10},{3,11},{4,12},{5,13},{6,14},{7,15},{8,0},{9,1},... | collective-permute-start | bytes 614408 | tf_op jit(solution)/shard_map/ppermute | solution.py:520
  56.8 7.6 %collective-permute-start.13 = (bf16[128,512]{1,0:T(8,128)(2,1)S(1)}, bf16[128,512]{1,0:T(8,128)(2,1)S(1)}, u32[]{:S(2)}, u32[]{:S(2)}) collective-permute-start(bf16[128,512]{1,0:T(8,128)(2,1)S(1)} %collective-permute-done.12._.rest_3_), channel_id=1, source_target_pairs={{0,2},{2,0},{4,6},{6,4},{8,10},{10,8},{12,14},{14,12},{16,18},{18,... | collective-permute-start | bytes 393224 | tf_op jit(solution)/shard_map/ppermute | solution.py:510

commit v6 on v5

--- a/solution.py
+++ b/solution.py
@@ -206,34 +206,46 @@
             dact_ref[at, :] = sig * (1.0 + preact * (1.0 - sig))
     for part in parts:
         s0_ref[part, :] = nn_dot(hidden_ref[part, :], w_out_ref[...])
-    gain_sum = jnp.zeros((1, feat), F32)
-    for m, part in enumerate(parts):
-        for at in pieces(part):
-            output = s0_ref[at, :]
-            centred = output - row_mean(output)
-            inv_std = lax.rsqrt(row_mean(centred * centred) + EPSILON)
-            normed = centred * inv_std
-            normed_ref[at, :] = normed
-            inv_ref[at, :] = jnp.broadcast_to(inv_std, (PIECE, 128))
-            g = g_ref[m, at.start - part.start : at.stop - part.start, :].astype(F32)
-            gpn_ref[at, :] = norm_back(g, normed, inv_std, gain)
-            gain_sum += jnp.sum(g * normed, axis=0, keepdims=True)
-    for part in parts:
-        s0_ref[part, :] = nt_dot(gpn_ref[part, :], w_out_ref[...])
-    bias_sum = jnp.zeros((1, feat), F32)
-    for part in parts:
-        for at in pieces(part):
-            gpre = (s0_ref[at, :] * dact_ref[at, :]).astype(BF16)
-            gpre_ref[at, :] = gpre
-            bias_sum += jnp.sum(gpre.astype(F32), axis=0, keepdims=True)
-    for m, part in enumerate(parts):
-        cols = slice(m * feat, (m + 1) * feat)
-        gm = nt_dot(gpre_ref[part, :], w_agg_ref[...]).astype(BF16)
-        both_ref[:rows, cols] = gm
-        both_ref[rows:, cols] = gpre_ref[part, :]
-        t_ref[:, cols] = two_dot(halo_back_ref, gm)
-    put_halo_grads(t_ref, (o0, o1, o2, o3))
-    sums_ref[...] = jnp.concatenate([bias_sum, gain_sum, jnp.zeros((EXTRA - 2, feat), F32)], 0)
+    def normalize(at):
+        output = s0_ref[at, :]
+        centred = output - row_mean(output)
+        inv_std = lax.rsqrt(row_mean(centred * centred) + EPSILON)
+        normed = centred * inv_std
+        normed_ref[at, :] = normed
+        inv_ref[at, :] = jnp.broadcast_to(inv_std, (PIECE, 128))
+        return normed, inv_std
+
+    @on_core(0)
+    def _():
+        for part in parts:
+            for at in pieces(part):
+                normalize(at)
+
+    @on_core(1)
+    def _():
+        gain_sum = jnp.zeros((1, feat), F32)
+        for m, part in enumerate(parts):
+            for at in pieces(part):
+                normed, inv_std = normalize(at)
+                g = g_ref[m, at.start - part.start : at.stop - part.start, :].astype(F32)
+                gpn_ref[at, :] = norm_back(g, normed, inv_std, gain)
+                gain_sum += jnp.sum(g * normed, axis=0, keepdims=True)
+        for part in parts:
+            s0_ref[part, :] = nt_dot(gpn_ref[part, :], w_out_ref[...])
+        bias_sum = jnp.zeros((1, feat), F32)
+        for part in parts:
+            for at in pieces(part):
+                gpre = (s0_ref[at, :] * dact_ref[at, :]).astype(BF16)
+                gpre_ref[at, :] = gpre
+                bias_sum += jnp.sum(gpre.astype(F32), axis=0, keepdims=True)
+        for m, part in enumerate(parts):
+            cols = slice(m * feat, (m + 1) * feat)
+            gm = nt_dot(gpre_ref[part, :], w_agg_ref[...]).astype(BF16)
+            both_ref[:rows, cols] = gm
+            both_ref[rows:, cols] = gpre_ref[part, :]
+            t_ref[:, cols] = two_dot(halo_back_ref, gm)
+        put_halo_grads(t_ref, (o0, o1, o2, o3))
+        sums_ref[...] = jnp.concatenate([bias_sum, gain_sum, jnp.zeros((EXTRA - 2, feat), F32)], 0)
 
 
 def lower_kernel(g_ref, gpre_ref, gm_ref, back_ref, w_node_ref, cpart_ref, g_out):

time: 66.4 us -> 64.7 us (0.974)
  starting transfers between devices: 24.9 us -> 21.6 us
  waiting for transfers between devices: 25.8 us -> 28.8 us
  Pallas kernels: 13.4 us -> 12 us
    ppermute x3, starting transfers between devices: 4.34 us -> 1.93 us  [flipped(): lax.ppermute(v, ('dom', 'segment'), [(2 * p + s, 2 * (p ^ 1 << bits[s]) +...]
    ppermute x3, waiting for transfers between devices: 12 us -> 13.8 us  [flipped(): lax.ppermute(v, ('dom', 'segment'), [(2 * p + s, 2 * (p ^ 1 << bits[s]) +...]
    pallas_call x11, Pallas kernels: 13.4 us -> 12 us  [call(): pl.pallas_call(kernel, out_shape=outs, in_specs=[SMEM] * scalars + [HBM]...]
    ppermute x10, starting transfers between devices: 19.9 us -> 18.6 us  [swapped(): lax.ppermute(v, ('dom', 'segment'), [(2 * p + s, 2 * swap_partner(p, k) +...]
    ppermute x10, waiting for transfers between devices: 13.7 us -> 14.9 us  [swapped(): lax.ppermute(v, ('dom', 'segment'), [(2 * p + s, 2 * swap_partner(p, k) +...]
  transfers between devices with their start and end apart: 16 -> 16, of which waited for: 7 -> 8; matrix products, arithmetic and copies ran while one was open for 0% -> 0% of each run, Pallas kernels for 9% -> 9%
where the time goes in v6:
time: 64.7 us; the launch traced here: 64.4 us
  waiting for transfers between devices  28.8 us (45%)
  starting transfers between devices  21.6 us (33%)
  Pallas kernels  12 us (19%)
  between operations  1.44 us (2%)
  local copies, waits for them, and re-layouts  0.67 us (1%)
    ppermute x10, starting transfers between devices, swapped(): lax.ppermute(v, ('dom', 'segment'), [(2 * p + s, 2 * swap_partner(p, k) +...  18.6 us
    ppermute x10, waiting for transfers between devices, swapped(): lax.ppermute(v, ('dom', 'segment'), [(2 * p + s, 2 * swap_partner(p, k) +...  14.9 us
    ppermute x3, waiting for transfers between devices, flipped(): lax.ppermute(v, ('dom', 'segment'), [(2 * p + s, 2 * (p ^ 1 << bits[s]) +...  13.8 us
    pallas_call x11, Pallas kernels, call(): pl.pallas_call(kernel, out_shape=outs, in_specs=[SMEM] * scalars + [HBM]...  12 us
    ppermute x3, starting transfers between devices, flipped(): lax.ppermute(v, ('dom', 'segment'), [(2 * p + s, 2 * (p ^ 1 << bits[s]) +...  1.93 us
  transfers between devices with their start and end apart: 16, of which 8 were waited for; matrix products, arithmetic and copies ran while one was open for 0% of the time, Pallas kernels for 9%

profile of v6, /device:TPU:0, one launch (start us, length us, event | category | flops | bytes accessed | tf_op | source)
XLA Modules:
  0.0 64.4 jit_solution(13793707773566459225)
XLA Ops:
  0.6 0.5 collective-permute-start.4
  1.1 1.3 %shard_map.154 = (bf16[64,512]{1,0:T(8,128)(2,1)S(1)}, bf16[64,512]{1,0:T(8,128)(2,1)S(1)}, bf16[64,512]{1,0:T(8,128)(2,1)S(1)}, bf16[64,512]{1,0:T(8,128)(2,1)S...) custom-call(s32[1,4,32]{2,1,0:T(4,128)} %targets_hbm.1, bf16[2,256,512]{2,1,0:T(8,128)(2,1)} %bitcast.9), custom_call_target="tpu_custom_call" | custom-call | flops 33554432 | bytes 524288 | tf_op jit(solution)/shard_map/pallas_call | solution.py:43
  2.5 2.6 %collective-permute-start = (bf16[64,512]{1,0:T(8,128)(2,1)S(1)}, bf16[64,512]{1,0:T(8,128)(2,1)S(1)}, u32[]{:S(2)}, u32[]{:S(2)}) collective-permute-start(bf16[64,512]{1,0:T(8,128)(2,1)S(1)} %get-tuple-element.61), channel_id=1, source_target_pairs={{0,2},{1,3},{2,0},{3,1},{4,6},{5,7},{6,4},{7,5},{8,10},{9,11},{10,... | collective-permute-start | bytes 196616 | tf_op jit(solution)/shard_map/ppermute | solution.py:522
  5.1 3.6 %collective-permute-start.1 = (bf16[64,512]{1,0:T(8,128)(2,1)S(1)}, bf16[64,512]{1,0:T(8,128)(2,1)S(1)}, u32[]{:S(2)}, u32[]{:S(2)}) collective-permute-start(bf16[64,512]{1,0:T(8,128)(2,1)S(1)} %get-tuple-element.62), channel_id=1, source_target_pairs={{0,14},{1,15},{2,4},{3,5},{4,2},{5,3},{6,8},{7,9},{8,6},{9,7},{10,... | collective-permute-start | bytes 196616 | tf_op jit(solution)/shard_map/ppermute | solution.py:522
  8.6 0.0 collective-permute-start.2
  8.6 0.9 %collective-permute-start.3 = (bf16[64,512]{1,0:T(8,128)(2,1)S(1)}, bf16[64,512]{1,0:T(8,128)(2,1)S(1)}, u32[]{:S(2)}, u32[]{:S(2)}) collective-permute-start(bf16[64,512]{1,0:T(8,128)(2,1)S(1)} %get-tuple-element.64), channel_id=1, source_target_pairs={{0,12},{1,13},{2,14},{3,15},{4,8},{5,9},{6,10},{7,11},{8,4},{9,5},... | collective-permute-start | bytes 196616 | tf_op jit(solution)/shard_map/ppermute | solution.py:522
  10.2 0.0 copy-start
  10.2 0.7 %copy-done = s32[1,2,7]{2,1,0:T(2,128)S(1)} copy-done((s32[1,2,7]{2,1,0:T(2,128)S(1)}, s32[1,2,7]{2,1,0:T(2,128)}, u32[]{:S(2)}) %copy-start) | copy-done | bytes 80
  10.9 2.5 %shard_map.155 = (f32[512,512]{1,0:T(8,128)S(1)}, f32[256,1024]{1,0:T(8,128)S(1)}, bf16[2,256,128]{2,1,0:T(8,128)(2,1)S(1)}, bf16[2,256,256]{2,1,0:T(8,128)(2,1)...) custom-call(s32[1,2,7]{2,1,0:T(2,128)S(1)} %copy-done, ...), custom_call_target="tpu_custom_call" | custom-call | flops 536870912 | bytes 2097152 | tf_op jit(solution)/shard_map/pallas_call | solution.py:43
  13.4 0.0 collective-permute-done.h0
  13.4 0.0 collective-permute-done.1.h1
  13.4 0.0 collective-permute-done.2.h2
  13.4 1.3 %collective-permute-done.3.h3 = bf16[64,512]{1,0:T(8,128)(2,1)S(1)} collective-permute-done((bf16[64,512]{1,0:T(8,128)(2,1)S(1)}, bf16[64,512]{1,0:T(8,128)(2,1)S(1)}, u32[]{:S(2)}, u32[]{:S(2)}) %collective-permute-start.3) | collective-permute-done | bytes 65568 | tf_op jit(solution)/shard_map/ppermute | solution.py:522
  14.8 0.0 collective-permute-done.4._.w_node_ref
  14.8 1.5 %shard_map.156 = (bf16[64,512]{1,0:T(8,128)(2,1)S(1)}, bf16[64,512]{1,0:T(8,128)(2,1)S(1)}, bf16[64,512]{1,0:T(8,128)(2,1)S(1)}, bf16[64,512]{1,0:T(8,128)(2,1)S...) custom-call(bf16[64,512]{1,0:T(8,128)(2,1)S(1)} %collective-permute-, ...), custom_call_target="tpu_custom_call" | custom-call | flops 1073741824 | bytes 5242880 | tf_op jit(solution)/shard_map/pallas_call | solution.py:43
  16.3 0.5 collective-permute-start.9
  16.8 1.6 %collective-permute-start.5 = (bf16[64,512]{1,0:T(8,128)(2,1)S(1)}, bf16[64,512]{1,0:T(8,128)(2,1)S(1)}, u32[]{:S(2)}, u32[]{:S(2)}) collective-permute-start(bf16[64,512]{1,0:T(8,128)(2,1)S(1)} %get-tuple-element.74), channel_id=1, source_target_pairs={{0,3},{1,2},{2,1},{3,0},{4,7},{5,6},{6,5},{7,4},{8,11},{9,10},{10,... | collective-permute-start | bytes 196616 | tf_op jit(solution)/shard_map/ppermute | solution.py:522
  18.4 2.6 %collective-permute-start.6 = (bf16[64,512]{1,0:T(8,128)(2,1)S(1)}, bf16[64,512]{1,0:T(8,128)(2,1)S(1)}, u32[]{:S(2)}, u32[]{:S(2)}) collective-permute-start(bf16[64,512]{1,0:T(8,128)(2,1)S(1)} %get-tuple-element.75), channel_id=1, source_target_pairs={{0,15},{1,14},{2,5},{3,4},{4,3},{5,2},{6,9},{7,8},{8,7},{9,6},{10,... | collective-permute-start | bytes 196616 | tf_op jit(solution)/shard_map/ppermute | solution.py:522
  21.0 0.0 collective-permute-start.7
  21.0 0.3 collective-permute-start.8
  21.3 0.6 shard_map.159
  21.9 0.0 collective-permute-done.9.both_ref
  21.9 0.8 %shard_map.157.refs_5_ = f32[512,512]{1,0:T(8,128)S(1)} custom-call(bf16[2,256,512]{2,1,0:T(8,128)(2,1)S(1)} %get-tuple-element.70.g_ref, bf16[512,1024]{1,0:T(8,128)(2,1)S(1)} %collective-permute-done.9.both_ref, bf16[2,256,256]{2,1,0:T(8,128)(2,1)S(1)} %get-tuple-element.79.back_ref, bf16[512,512]{1,0:T(8,128)(2,1)S(1)} %collective-permute-done.4._.w_node_ref), custom_call_target="tpu_custom_call" | custom-call | flops 268435456 | bytes 2621440 | tf_op jit(solution)/shard_map/pallas_call | solution.py:43
  22.7 0.0 collective-permute-done.5.refs_1_
  22.7 2.2 %collective-permute-done.6.refs_2_ = bf16[64,512]{1,0:T(8,128)(2,1)S(1)} collective-permute-done((bf16[64,512]{1,0:T(8,128)(2,1)S(1)}, bf16[64,512]{1,0:T(8,128)(2,1)S(1)}, u32[]{:S(2)}, u32[]{:S(2)}) %collective-permute-start.6) | collective-permute-done | bytes 65568 | tf_op jit(solution)/shard_map/ppermute | solution.py:522
  24.9 0.2 collective-permute-done.7.refs_3_
  25.2 1.9 %collective-permute-done.8.refs_4_ = bf16[64,512]{1,0:T(8,128)(2,1)S(1)} collective-permute-done((bf16[64,512]{1,0:T(8,128)(2,1)S(1)}, bf16[64,512]{1,0:T(8,128)(2,1)S(1)}, u32[]{:S(2)}, u32[]{:S(2)}) %collective-permute-start.8) | collective-permute-done | bytes 65568 | tf_op jit(solution)/shard_map/ppermute | solution.py:522
  27.1 1.2 %shard_map.158 = (bf16[512,512]{1,0:T(8,128)(2,1)S(1)}, bf16[512,512]{1,0:T(8,128)(2,1)S(1)}, bf16[512,512]{1,0:T(8,128)(2,1)S(1)}, f32[8,512]{1,0:T(8,128)S(1)}) custom-call(bf16[256,128]{1,0:T(8,128)(2,1)S(1)} %get-tuple-element.60.refs_0_.onehot_ref, bf16[64,512]{1,0:T(8,128)(2,1)S(1)} %collective-permute-done.5.refs_1_, ...), custom_call_target="tpu_custom_call" | custom-call | flops 536870912 | bytes 4194304 | tf_op jit(solution)/shard_map/pallas_call | solution.py:43
  28.3 1.8 %shard_map.160 = (f32[4,200,512]{2,1,0:T(8,128)S(1)}, bf16[928,512]{1,0:T(8,128)(2,1)S(1)}, bf16[64,512]{1,0:T(8,128)(2,1)S(1)}, bf16[128,512]{1,0:T(8,128)(2,1)S(1)}, bf16[256,1024]{1,0:T(8,128)(2,1)S(1)}) custom-call(bf16[512,512]{1,0:T(8,128)(2,1)S(1)} %get-tuple-element.83.gpre_ref, bf16[512,512]{1,0:T(8,128)(2,1)S(1)} %get-tuple-element.84.gpn_ref, ...), custom_call_target="tpu_custom_call" | custom-call | flops 1073741824 | bytes 4194304 | tf_op jit(solution)/shard_map/pallas_call | solution.py:43
  30.1 0.9 %collective-permute-start.10 = (bf16[928,512]{1,0:T(8,128)(2,1)S(1)}, bf16[928,512]{1,0:T(8,128)(2,1)S(1)}, u32[]{:S(2)}, u32[]{:S(2)}) collective-permute-start(bf16[928,512]{1,0:T(8,128)(2,1)S(1)} %get-tuple-element.96), channel_id=1, source_target_pairs={{0,4},{1,3},{2,6},{3,1},{4,0},{5,7},{6,2},{7,5},{8,12},{9,11},{10,... | collective-permute-start | bytes 2850824 | tf_op jit(solution)/shard_map/ppermute | solution.py:532
  31.0 0.8 %shard_map.161 = (f32[512,512]{1,0:T(8,128)S(1)}, bf16[512,512]{1,0:T(8,128)(2,1)S(1)}) custom-call(bf16[512,512]{1,0:T(8,128)(2,1)S(1)} %get-tuple-element.98.g_ref, bf16[512,512]{1,0:T(8,128)(2,1)S(1)} %get-tuple-element.83.gpre_ref, bf16[256,1024]{1,0:T(8,128)(2,1)S(1)} %get-tuple-element.99.gm_ref, bf16[2,256,256]{2,1,0:T(8,128)(2,1)S(1)} %get-tuple-element.79.back_ref, ...), custom_call_target="tpu_custom_call" | custom-call | flops 268435456 | bytes 2621440 | tf_op jit(solution)/shard_map/pallas_call | solution.py:43
  31.8 12.8 %collective-permute-done.10.recv.rest_2_ = bf16[928,512]{1,0:T(8,128)(2,1)S(1)} collective-permute-done((bf16[928,512]{1,0:T(8,128)(2,1)S(1)}, bf16[928,512]{1,0:T(8,128)(2,1)S(1)}, u32[]{:S(2)}, u32[]{:S(2)}) %collective-permute-start.10) | collective-permute-done | bytes 950304 | tf_op jit(solution)/shard_map/ppermute | solution.py:532
  44.6 0.2 shard_map.162
  44.8 0.9 %collective-permute-start.11 = (bf16[528,512]{1,0:T(8,128)(2,1)S(1)}, bf16[528,512]{1,0:T(8,128)(2,1)S(1)}, u32[]{:S(2)}, u32[]{:S(2)}) collective-permute-start(bf16[528,512]{1,0:T(8,128)(2,1)S(1)} %get-tuple-element.102), channel_id=1, source_target_pairs={{0,2},{1,5},{2,0},{3,7},{4,6},{5,1},{6,4},{7,3},{8,10},{9,13},{10,... | collective-permute-start | bytes 1622024 | tf_op jit(solution)/shard_map/ppermute | solution.py:532
  45.7 0.0 collective-permute-start.14
  45.7 3.5 %collective-permute-start.12 = (bf16[128,512]{1,0:T(8,128)(2,1)S(1)}, bf16[128,512]{1,0:T(8,128)(2,1)S(1)}, u32[]{:S(2)}, u32[]{:S(2)}) collective-permute-start(bf16[128,512]{1,0:T(8,128)(2,1)S(1)} %get-tuple-element.103), channel_id=1, source_target_pairs={{0,12},{2,14},{4,8},{6,10},{8,4},{10,6},{12,0},{14,2},{16,28},{18,... | collective-permute-start | bytes 393224 | tf_op jit(solution)/shard_map/ppermute | solution.py:522
  49.2 5.9 %collective-permute-done.12._.rest_3_ = bf16[128,512]{1,0:T(8,128)(2,1)S(1)} collective-permute-done((bf16[128,512]{1,0:T(8,128)(2,1)S(1)}, bf16[128,512]{1,0:T(8,128)(2,1)S(1)}, u32[]{:S(2)}, u32[]{:S(2)}) %collective-permute-start.12) | collective-permute-done | bytes 131104 | tf_op jit(solution)/shard_map/ppermute | solution.py:522
  55.2 0.0 collective-permute-done.11.recv.rest_0_.rest_1_
  55.2 0.1 shard_map.163
  55.2 0.1 collective-permute-start.15
  55.3 3.6 %collective-permute-start.13 = (bf16[128,512]{1,0:T(8,128)(2,1)S(1)}, bf16[128,512]{1,0:T(8,128)(2,1)S(1)}, u32[]{:S(2)}, u32[]{:S(2)}) collective-permute-start(bf16[128,512]{1,0:T(8,128)(2,1)S(1)} %collective-permute-done.12._.rest_3_), channel_id=1, source_target_pairs={{0,2},{2,0},{4,6},{6,4},{8,10},{10,8},{12,14},{14,12},{16,18},{18,... | collective-permute-start | bytes 393224 | tf_op jit(solution)/shard_map/ppermute | solution.py:522
  58.9 3.3 %collective-permute-done.13.rest_4_ = bf16[128,512]{1,0:T(8,128)(2,1)S(1)} collective-permute-done((bf16[128,512]{1,0:T(8,128)(2,1)S(1)}, bf16[128,512]{1,0:T(8,128)(2,1)S(1)}, u32[]{:S(2)}, u32[]{:S(2)}) %collective-permute-start.13) | collective-permute-done | bytes 131104 | tf_op jit(solution)/shard_map/ppermute | solution.py:522
  62.2 0.0 collective-permute-done.14.rest_6_
  62.2 1.0 %collective-permute-done.15.rest_8_ = bf16[200,512]{1,0:T(8,128)(2,1)S(1)} collective-permute-done((bf16[200,512]{1,0:T(8,128)(2,1)S(1)}, bf16[200,512]{1,0:T(8,128)(2,1)S(1)}, u32[]{:S(2)}, u32[]{:S(2)}) %collective-permute-start.15) | collective-permute-done | bytes 204832 | tf_op jit(solution)/shard_map/ppermute | solution.py:532
  63.2 1.3 %shard_map.164 = (bf16[2,256,512]{2,1,0:T(8,128)(2,1)}, f32[64,512]{1,0:T(8,128)}, f32[64,512]{1,0:T(8,128)}, f32[64,512]{1,0:T(8,128)}, f32[1,512]{1,0:T(1,128)}, /*index=5*/f32[1,512]{1,0:T(1,128)}) custom-call(bf16[256,128]{1,0:T(8,128)(2,1)S(1)} %get-tuple-element.60.refs_0_.onehot_ref, ...), custom_call_target="tpu_custom_call" | custom-call | flops 67108864 | bytes 1572864 | tf_op jit(solution)/shard_map/pallas_call | solution.py:43
Async XLA Ops:
  0.6 14.1 %collective-permute-start.4 = (bf16[512,512]{1,0:T(8,128)(2,1)}, bf16[512,512]{1,0:T(8,128)(2,1)S(1)}, u32[]{:S(2)}, u32[]{:S(2)}) collective-permute-start(bf16[512,512]{1,0:T(8,128)(2,1)} %bitcast.12), channel_id=1, source_target_pairs={{0,1},{1,0},{2,3},{3,2},{4,5},{5,4},{6,7},{7,6},{8,9},{9,8},{10,11... | collective-permute-start | bytes 1572872 | tf_op jit(solution)/shard_map/ppermute | solution.py:529
  2.5 10.9 %collective-permute-start = (bf16[64,512]{1,0:T(8,128)(2,1)S(1)}, bf16[64,512]{1,0:T(8,128)(2,1)S(1)}, u32[]{:S(2)}, u32[]{:S(2)}) collective-permute-start(bf16[64,512]{1,0:T(8,128)(2,1)S(1)} %get-tuple-element.61), channel_id=1, source_target_pairs={{0,2},{1,3},{2,0},{3,1},{4,6},{5,7},{6,4},{7,5},{8,10},{9,11},{10,... | collective-permute-start | bytes 196616 | tf_op jit(solution)/shard_map/ppermute | solution.py:522
  5.1 8.3 %collective-permute-start.1 = (bf16[64,512]{1,0:T(8,128)(2,1)S(1)}, bf16[64,512]{1,0:T(8,128)(2,1)S(1)}, u32[]{:S(2)}, u32[]{:S(2)}) collective-permute-start(bf16[64,512]{1,0:T(8,128)(2,1)S(1)} %get-tuple-element.62), channel_id=1, source_target_pairs={{0,14},{1,15},{2,4},{3,5},{4,2},{5,3},{6,8},{7,9},{8,6},{9,7},{10,... | collective-permute-start | bytes 196616 | tf_op jit(solution)/shard_map/ppermute | solution.py:522
  8.6 4.8 %collective-permute-start.2 = (bf16[64,512]{1,0:T(8,128)(2,1)S(1)}, bf16[64,512]{1,0:T(8,128)(2,1)S(1)}, u32[]{:S(2)}, u32[]{:S(2)}) collective-permute-start(bf16[64,512]{1,0:T(8,128)(2,1)S(1)} %get-tuple-element.63), channel_id=1, source_target_pairs={{0,4},{1,5},{2,6},{3,7},{4,0},{5,1},{6,2},{7,3},{8,12},{9,13},{10,... | collective-permute-start | bytes 196616 | tf_op jit(solution)/shard_map/ppermute | solution.py:522
  8.6 6.1 %collective-permute-start.3 = (bf16[64,512]{1,0:T(8,128)(2,1)S(1)}, bf16[64,512]{1,0:T(8,128)(2,1)S(1)}, u32[]{:S(2)}, u32[]{:S(2)}) collective-permute-start(bf16[64,512]{1,0:T(8,128)(2,1)S(1)} %get-tuple-element.64), channel_id=1, source_target_pairs={{0,12},{1,13},{2,14},{3,15},{4,8},{5,9},{6,10},{7,11},{8,4},{9,5},... | collective-permute-start | bytes 196616 | tf_op jit(solution)/shard_map/ppermute | solution.py:522
  10.2 0.7 %copy-start = (s32[1,2,7]{2,1,0:T(2,128)S(1)}, s32[1,2,7]{2,1,0:T(2,128)}, u32[]{:S(2)}) copy-start(s32[1,2,7]{2,1,0:T(2,128)} %pairs_ref.1) | copy-start | bytes 172
  16.3 5.6 %collective-permute-start.9 = (bf16[512,1024]{1,0:T(8,128)(2,1)S(1)}, bf16[512,1024]{1,0:T(8,128)(2,1)S(1)}, u32[]{:S(2)}, u32[]{:S(2)}) collective-permute-start(bf16[512,1024]{1,0:T(8,128)(2,1)S(1)} %get-tuple-element.78), channel_id=1, source_target_pairs={{0,1},{1,0},{2,3},{3,2},{4,5},{5,4},{6,7},{7,6},{8,9},{9,8},{10,11... | collective-permute-start | bytes 3145736 | tf_op jit(solution)/shard_map/ppermute | solution.py:529
  16.8 5.9 %collective-permute-start.5 = (bf16[64,512]{1,0:T(8,128)(2,1)S(1)}, bf16[64,512]{1,0:T(8,128)(2,1)S(1)}, u32[]{:S(2)}, u32[]{:S(2)}) collective-permute-start(bf16[64,512]{1,0:T(8,128)(2,1)S(1)} %get-tuple-element.74), channel_id=1, source_target_pairs={{0,3},{1,2},{2,1},{3,0},{4,7},{5,6},{6,5},{7,4},{8,11},{9,10},{10,... | collective-permute-start | bytes 196616 | tf_op jit(solution)/shard_map/ppermute | solution.py:522
  18.4 6.5 %collective-permute-start.6 = (bf16[64,512]{1,0:T(8,128)(2,1)S(1)}, bf16[64,512]{1,0:T(8,128)(2,1)S(1)}, u32[]{:S(2)}, u32[]{:S(2)}) collective-permute-start(bf16[64,512]{1,0:T(8,128)(2,1)S(1)} %get-tuple-element.75), channel_id=1, source_target_pairs={{0,15},{1,14},{2,5},{3,4},{4,3},{5,2},{6,9},{7,8},{8,7},{9,6},{10,... | collective-permute-start | bytes 196616 | tf_op jit(solution)/shard_map/ppermute | solution.py:522
  21.0 4.1 %collective-permute-start.7 = (bf16[64,512]{1,0:T(8,128)(2,1)S(1)}, bf16[64,512]{1,0:T(8,128)(2,1)S(1)}, u32[]{:S(2)}, u32[]{:S(2)}) collective-permute-start(bf16[64,512]{1,0:T(8,128)(2,1)S(1)} %get-tuple-element.76), channel_id=1, source_target_pairs={{0,5},{1,4},{2,7},{3,6},{4,1},{5,0},{6,3},{7,2},{8,13},{9,12},{10,... | collective-permute-start | bytes 196616 | tf_op jit(solution)/shard_map/ppermute | solution.py:522
  21.0 6.0 %collective-permute-start.8 = (bf16[64,512]{1,0:T(8,128)(2,1)S(1)}, bf16[64,512]{1,0:T(8,128)(2,1)S(1)}, u32[]{:S(2)}, u32[]{:S(2)}) collective-permute-start(bf16[64,512]{1,0:T(8,128)(2,1)S(1)} %get-tuple-element.77), channel_id=1, source_target_pairs={{0,13},{1,12},{2,15},{3,14},{4,9},{5,8},{6,11},{7,10},{8,5},{9,4},... | collective-permute-start | bytes 196616 | tf_op jit(solution)/shard_map/ppermute | solution.py:522
  30.1 14.5 %collective-permute-start.10 = (bf16[928,512]{1,0:T(8,128)(2,1)S(1)}, bf16[928,512]{1,0:T(8,128)(2,1)S(1)}, u32[]{:S(2)}, u32[]{:S(2)}) collective-permute-start(bf16[928,512]{1,0:T(8,128)(2,1)S(1)} %get-tuple-element.96), channel_id=1, source_target_pairs={{0,4},{1,3},{2,6},{3,1},{4,0},{5,7},{6,2},{7,5},{8,12},{9,11},{10,... | collective-permute-start | bytes 2850824 | tf_op jit(solution)/shard_map/ppermute | solution.py:532
  44.8 10.4 %collective-permute-start.11 = (bf16[528,512]{1,0:T(8,128)(2,1)S(1)}, bf16[528,512]{1,0:T(8,128)(2,1)S(1)}, u32[]{:S(2)}, u32[]{:S(2)}) collective-permute-start(bf16[528,512]{1,0:T(8,128)(2,1)S(1)} %get-tuple-element.102), channel_id=1, source_target_pairs={{0,2},{1,5},{2,0},{3,7},{4,6},{5,1},{6,4},{7,3},{8,10},{9,13},{10,... | collective-permute-start | bytes 1622024 | tf_op jit(solution)/shard_map/ppermute | solution.py:532
  45.7 16.5 %collective-permute-start.14 = (bf16[512,512]{1,0:T(8,128)(2,1)S(1)}, bf16[512,512]{1,0:T(8,128)(2,1)S(1)}, u32[]{:S(2)}, u32[]{:S(2)}) collective-permute-start(bf16[512,512]{1,0:T(8,128)(2,1)S(1)} %get-tuple-element.104), channel_id=1, source_target_pairs={{0,1},{1,0},{2,3},{3,2},{4,5},{5,4},{6,7},{7,6},{8,9},{9,8},{10,11... | collective-permute-start | bytes 1572872 | tf_op jit(solution)/shard_map/ppermute | solution.py:529
  45.7 9.4 %collective-permute-start.12 = (bf16[128,512]{1,0:T(8,128)(2,1)S(1)}, bf16[128,512]{1,0:T(8,128)(2,1)S(1)}, u32[]{:S(2)}, u32[]{:S(2)}) collective-permute-start(bf16[128,512]{1,0:T(8,128)(2,1)S(1)} %get-tuple-element.103), channel_id=1, source_target_pairs={{0,12},{2,14},{4,8},{6,10},{8,4},{10,6},{12,0},{14,2},{16,28},{18,... | collective-permute-start | bytes 393224 | tf_op jit(solution)/shard_map/ppermute | solution.py:522
  55.2 8.0 %collective-permute-start.15 = (bf16[200,512]{1,0:T(8,128)(2,1)S(1)}, bf16[200,512]{1,0:T(8,128)(2,1)S(1)}, u32[]{:S(2)}, u32[]{:S(2)}) collective-permute-start(bf16[200,512]{1,0:T(8,128)(2,1)S(1)} %get-tuple-element.107), channel_id=1, source_target_pairs={{0,8},{1,9},{2,10},{3,11},{4,12},{5,13},{6,14},{7,15},{8,0},{9,1},... | collective-permute-start | bytes 614408 | tf_op jit(solution)/shard_map/ppermute | solution.py:532
  55.3 6.9 %collective-permute-start.13 = (bf16[128,512]{1,0:T(8,128)(2,1)S(1)}, bf16[128,512]{1,0:T(8,128)(2,1)S(1)}, u32[]{:S(2)}, u32[]{:S(2)}) collective-permute-start(bf16[128,512]{1,0:T(8,128)(2,1)S(1)} %collective-permute-done.12._.rest_3_), channel_id=1, source_target_pairs={{0,2},{2,0},{4,6},{6,4},{8,10},{10,8},{12,14},{14,12},{16,18},{18,... | collective-permute-start | bytes 393224 | tf_op jit(solution)/shard_map/ppermute | solution.py:522

commit v7 on v6

--- a/solution.py
+++ b/solution.py
@@ -206,27 +206,28 @@
             dact_ref[at, :] = sig * (1.0 + preact * (1.0 - sig))
     for part in parts:
         s0_ref[part, :] = nn_dot(hidden_ref[part, :], w_out_ref[...])
-    def normalize(at):
+    def normalize(at, keep):
         output = s0_ref[at, :]
         centred = output - row_mean(output)
         inv_std = lax.rsqrt(row_mean(centred * centred) + EPSILON)
         normed = centred * inv_std
-        normed_ref[at, :] = normed
-        inv_ref[at, :] = jnp.broadcast_to(inv_std, (PIECE, 128))
+        if keep:
+            normed_ref[at, :] = normed
+            inv_ref[at, :] = jnp.broadcast_to(inv_std, (PIECE, 128))
         return normed, inv_std
 
     @on_core(0)
     def _():
         for part in parts:
             for at in pieces(part):
-                normalize(at)
+                normalize(at, True)
 
     @on_core(1)
     def _():
         gain_sum = jnp.zeros((1, feat), F32)
         for m, part in enumerate(parts):
             for at in pieces(part):
-                normed, inv_std = normalize(at)
+                normed, inv_std = normalize(at, False)
                 g = g_ref[m, at.start - part.start : at.stop - part.start, :].astype(F32)
                 gpn_ref[at, :] = norm_back(g, normed, inv_std, gain)
                 gain_sum += jnp.sum(g * normed, axis=0, keepdims=True)

time: 64.7 us -> 64.7 us (level)
  no operation moved by 1% of the time
where the time goes in v7:
time: 64.7 us; the launch traced here: 64.4 us
  waiting for transfers between devices  28.7 us (44%)
  starting transfers between devices  21.6 us (33%)
  Pallas kernels  12 us (19%)
  between operations  1.44 us (2%)
  local copies, waits for them, and re-layouts  0.67 us (1%)
    ppermute x10, starting transfers between devices, swapped(): lax.ppermute(v, ('dom', 'segment'), [(2 * p + s, 2 * swap_partner(p, k) +...  18.6 us
    ppermute x10, waiting for transfers between devices, swapped(): lax.ppermute(v, ('dom', 'segment'), [(2 * p + s, 2 * swap_partner(p, k) +...  14.9 us
    ppermute x3, waiting for transfers between devices, flipped(): lax.ppermute(v, ('dom', 'segment'), [(2 * p + s, 2 * (p ^ 1 << bits[s]) +...  13.8 us
    pallas_call x11, Pallas kernels, call(): pl.pallas_call(kernel, out_shape=outs, in_specs=[SMEM] * scalars + [HBM]...  12 us
    ppermute x3, starting transfers between devices, flipped(): lax.ppermute(v, ('dom', 'segment'), [(2 * p + s, 2 * (p ^ 1 << bits[s]) +...  1.94 us
  transfers between devices with their start and end apart: 16, of which 8 were waited for; matrix products, arithmetic and copies ran while one was open for 0% of the time, Pallas kernels for 9%

profile of v7, /device:TPU:0, one launch (start us, length us, event | category | flops | bytes accessed | tf_op | source)
XLA Modules:
  0.0 64.4 jit_solution(3355398351933281338)
XLA Ops:
  0.6 0.5 collective-permute-start.4
  1.1 1.3 %shard_map.154 = (bf16[64,512]{1,0:T(8,128)(2,1)S(1)}, bf16[64,512]{1,0:T(8,128)(2,1)S(1)}, bf16[64,512]{1,0:T(8,128)(2,1)S(1)}, bf16[64,512]{1,0:T(8,128)(2,1)S...) custom-call(s32[1,4,32]{2,1,0:T(4,128)} %targets_hbm.1, bf16[2,256,512]{2,1,0:T(8,128)(2,1)} %bitcast.9), custom_call_target="tpu_custom_call" | custom-call | flops 33554432 | bytes 524288 | tf_op jit(solution)/shard_map/pallas_call | solution.py:43
  2.5 2.6 %collective-permute-start = (bf16[64,512]{1,0:T(8,128)(2,1)S(1)}, bf16[64,512]{1,0:T(8,128)(2,1)S(1)}, u32[]{:S(2)}, u32[]{:S(2)}) collective-permute-start(bf16[64,512]{1,0:T(8,128)(2,1)S(1)} %get-tuple-element.61), channel_id=1, source_target_pairs={{0,2},{1,3},{2,0},{3,1},{4,6},{5,7},{6,4},{7,5},{8,10},{9,11},{10,... | collective-permute-start | bytes 196616 | tf_op jit(solution)/shard_map/ppermute | solution.py:523
  5.1 3.6 %collective-permute-start.1 = (bf16[64,512]{1,0:T(8,128)(2,1)S(1)}, bf16[64,512]{1,0:T(8,128)(2,1)S(1)}, u32[]{:S(2)}, u32[]{:S(2)}) collective-permute-start(bf16[64,512]{1,0:T(8,128)(2,1)S(1)} %get-tuple-element.62), channel_id=1, source_target_pairs={{0,14},{1,15},{2,4},{3,5},{4,2},{5,3},{6,8},{7,9},{8,6},{9,7},{10,... | collective-permute-start | bytes 196616 | tf_op jit(solution)/shard_map/ppermute | solution.py:523
  8.6 0.0 collective-permute-start.2
  8.6 0.9 %collective-permute-start.3 = (bf16[64,512]{1,0:T(8,128)(2,1)S(1)}, bf16[64,512]{1,0:T(8,128)(2,1)S(1)}, u32[]{:S(2)}, u32[]{:S(2)}) collective-permute-start(bf16[64,512]{1,0:T(8,128)(2,1)S(1)} %get-tuple-element.64), channel_id=1, source_target_pairs={{0,12},{1,13},{2,14},{3,15},{4,8},{5,9},{6,10},{7,11},{8,4},{9,5},... | collective-permute-start | bytes 196616 | tf_op jit(solution)/shard_map/ppermute | solution.py:523
  10.2 0.0 copy-start
  10.2 0.7 %copy-done = s32[1,2,7]{2,1,0:T(2,128)S(1)} copy-done((s32[1,2,7]{2,1,0:T(2,128)S(1)}, s32[1,2,7]{2,1,0:T(2,128)}, u32[]{:S(2)}) %copy-start) | copy-done | bytes 80
  10.9 2.5 %shard_map.155 = (f32[512,512]{1,0:T(8,128)S(1)}, f32[256,1024]{1,0:T(8,128)S(1)}, bf16[2,256,128]{2,1,0:T(8,128)(2,1)S(1)}, bf16[2,256,256]{2,1,0:T(8,128)(2,1)...) custom-call(s32[1,2,7]{2,1,0:T(2,128)S(1)} %copy-done, ...), custom_call_target="tpu_custom_call" | custom-call | flops 536870912 | bytes 2097152 | tf_op jit(solution)/shard_map/pallas_call | solution.py:43
  13.4 0.0 collective-permute-done.h0
  13.4 0.0 collective-permute-done.1.h1
  13.4 0.0 collective-permute-done.2.h2
  13.4 1.3 %collective-permute-done.3.h3 = bf16[64,512]{1,0:T(8,128)(2,1)S(1)} collective-permute-done((bf16[64,512]{1,0:T(8,128)(2,1)S(1)}, bf16[64,512]{1,0:T(8,128)(2,1)S(1)}, u32[]{:S(2)}, u32[]{:S(2)}) %collective-permute-start.3) | collective-permute-done | bytes 65568 | tf_op jit(solution)/shard_map/ppermute | solution.py:523
  14.8 0.0 collective-permute-done.4._.w_node_ref
  14.8 1.5 %shard_map.156 = (bf16[64,512]{1,0:T(8,128)(2,1)S(1)}, bf16[64,512]{1,0:T(8,128)(2,1)S(1)}, bf16[64,512]{1,0:T(8,128)(2,1)S(1)}, bf16[64,512]{1,0:T(8,128)(2,1)S...) custom-call(bf16[64,512]{1,0:T(8,128)(2,1)S(1)} %collective-permute-, ...), custom_call_target="tpu_custom_call" | custom-call | flops 1073741824 | bytes 5242880 | tf_op jit(solution)/shard_map/pallas_call | solution.py:43
  16.3 0.5 collective-permute-start.9
  16.8 1.6 %collective-permute-start.5 = (bf16[64,512]{1,0:T(8,128)(2,1)S(1)}, bf16[64,512]{1,0:T(8,128)(2,1)S(1)}, u32[]{:S(2)}, u32[]{:S(2)}) collective-permute-start(bf16[64,512]{1,0:T(8,128)(2,1)S(1)} %get-tuple-element.74), channel_id=1, source_target_pairs={{0,3},{1,2},{2,1},{3,0},{4,7},{5,6},{6,5},{7,4},{8,11},{9,10},{10,... | collective-permute-start | bytes 196616 | tf_op jit(solution)/shard_map/ppermute | solution.py:523
  18.4 2.6 %collective-permute-start.6 = (bf16[64,512]{1,0:T(8,128)(2,1)S(1)}, bf16[64,512]{1,0:T(8,128)(2,1)S(1)}, u32[]{:S(2)}, u32[]{:S(2)}) collective-permute-start(bf16[64,512]{1,0:T(8,128)(2,1)S(1)} %get-tuple-element.75), channel_id=1, source_target_pairs={{0,15},{1,14},{2,5},{3,4},{4,3},{5,2},{6,9},{7,8},{8,7},{9,6},{10,... | collective-permute-start | bytes 196616 | tf_op jit(solution)/shard_map/ppermute | solution.py:523
  21.0 0.0 collective-permute-start.7
  21.0 0.3 collective-permute-start.8
  21.3 0.6 shard_map.159
  21.9 0.0 collective-permute-done.9.both_ref
  21.9 0.8 %shard_map.157.refs_5_ = f32[512,512]{1,0:T(8,128)S(1)} custom-call(bf16[2,256,512]{2,1,0:T(8,128)(2,1)S(1)} %get-tuple-element.70.g_ref, bf16[512,1024]{1,0:T(8,128)(2,1)S(1)} %collective-permute-done.9.both_ref, bf16[2,256,256]{2,1,0:T(8,128)(2,1)S(1)} %get-tuple-element.79.back_ref, bf16[512,512]{1,0:T(8,128)(2,1)S(1)} %collective-permute-done.4._.w_node_ref), custom_call_target="tpu_custom_call" | custom-call | flops 268435456 | bytes 2621440 | tf_op jit(solution)/shard_map/pallas_call | solution.py:43
  22.7 0.0 collective-permute-done.5.refs_1_
  22.7 2.2 %collective-permute-done.6.refs_2_ = bf16[64,512]{1,0:T(8,128)(2,1)S(1)} collective-permute-done((bf16[64,512]{1,0:T(8,128)(2,1)S(1)}, bf16[64,512]{1,0:T(8,128)(2,1)S(1)}, u32[]{:S(2)}, u32[]{:S(2)}) %collective-permute-start.6) | collective-permute-done | bytes 65568 | tf_op jit(solution)/shard_map/ppermute | solution.py:523
  24.9 0.2 collective-permute-done.7.refs_3_
  25.1 1.9 %collective-permute-done.8.refs_4_ = bf16[64,512]{1,0:T(8,128)(2,1)S(1)} collective-permute-done((bf16[64,512]{1,0:T(8,128)(2,1)S(1)}, bf16[64,512]{1,0:T(8,128)(2,1)S(1)}, u32[]{:S(2)}, u32[]{:S(2)}) %collective-permute-start.8) | collective-permute-done | bytes 65568 | tf_op jit(solution)/shard_map/ppermute | solution.py:523
  27.0 1.2 %shard_map.158 = (bf16[512,512]{1,0:T(8,128)(2,1)S(1)}, bf16[512,512]{1,0:T(8,128)(2,1)S(1)}, bf16[512,512]{1,0:T(8,128)(2,1)S(1)}, f32[8,512]{1,0:T(8,128)S(1)}) custom-call(bf16[256,128]{1,0:T(8,128)(2,1)S(1)} %get-tuple-element.60.refs_0_.onehot_ref, bf16[64,512]{1,0:T(8,128)(2,1)S(1)} %collective-permute-done.5.refs_1_, ...), custom_call_target="tpu_custom_call" | custom-call | flops 536870912 | bytes 4194304 | tf_op jit(solution)/shard_map/pallas_call | solution.py:43
  28.2 1.8 %shard_map.160 = (f32[4,200,512]{2,1,0:T(8,128)S(1)}, bf16[928,512]{1,0:T(8,128)(2,1)S(1)}, bf16[64,512]{1,0:T(8,128)(2,1)S(1)}, bf16[128,512]{1,0:T(8,128)(2,1)S(1)}, bf16[256,1024]{1,0:T(8,128)(2,1)S(1)}) custom-call(bf16[512,512]{1,0:T(8,128)(2,1)S(1)} %get-tuple-element.83.gpre_ref, bf16[512,512]{1,0:T(8,128)(2,1)S(1)} %get-tuple-element.84.gpn_ref, ...), custom_call_target="tpu_custom_call" | custom-call | flops 1073741824 | bytes 4194304 | tf_op jit(solution)/shard_map/pallas_call | solution.py:43
  30.0 0.9 %collective-permute-start.10 = (bf16[928,512]{1,0:T(8,128)(2,1)S(1)}, bf16[928,512]{1,0:T(8,128)(2,1)S(1)}, u32[]{:S(2)}, u32[]{:S(2)}) collective-permute-start(bf16[928,512]{1,0:T(8,128)(2,1)S(1)} %get-tuple-element.96), channel_id=1, source_target_pairs={{0,4},{1,3},{2,6},{3,1},{4,0},{5,7},{6,2},{7,5},{8,12},{9,11},{10,... | collective-permute-start | bytes 2850824 | tf_op jit(solution)/shard_map/ppermute | solution.py:533
  31.0 0.8 %shard_map.161 = (f32[512,512]{1,0:T(8,128)S(1)}, bf16[512,512]{1,0:T(8,128)(2,1)S(1)}) custom-call(bf16[512,512]{1,0:T(8,128)(2,1)S(1)} %get-tuple-element.98.g_ref, bf16[512,512]{1,0:T(8,128)(2,1)S(1)} %get-tuple-element.83.gpre_ref, bf16[256,1024]{1,0:T(8,128)(2,1)S(1)} %get-tuple-element.99.gm_ref, bf16[2,256,256]{2,1,0:T(8,128)(2,1)S(1)} %get-tuple-element.79.back_ref, ...), custom_call_target="tpu_custom_call" | custom-call | flops 268435456 | bytes 2621440 | tf_op jit(solution)/shard_map/pallas_call | solution.py:43
  31.8 12.8 %collective-permute-done.10.recv.rest_2_ = bf16[928,512]{1,0:T(8,128)(2,1)S(1)} collective-permute-done((bf16[928,512]{1,0:T(8,128)(2,1)S(1)}, bf16[928,512]{1,0:T(8,128)(2,1)S(1)}, u32[]{:S(2)}, u32[]{:S(2)}) %collective-permute-start.10) | collective-permute-done | bytes 950304 | tf_op jit(solution)/shard_map/ppermute | solution.py:533
  44.6 0.2 shard_map.162
  44.8 0.9 %collective-permute-start.11 = (bf16[528,512]{1,0:T(8,128)(2,1)S(1)}, bf16[528,512]{1,0:T(8,128)(2,1)S(1)}, u32[]{:S(2)}, u32[]{:S(2)}) collective-permute-start(bf16[528,512]{1,0:T(8,128)(2,1)S(1)} %get-tuple-element.102), channel_id=1, source_target_pairs={{0,2},{1,5},{2,0},{3,7},{4,6},{5,1},{6,4},{7,3},{8,10},{9,13},{10,... | collective-permute-start | bytes 1622024 | tf_op jit(solution)/shard_map/ppermute | solution.py:533
  45.7 0.0 collective-permute-start.14
  45.7 3.5 %collective-permute-start.12 = (bf16[128,512]{1,0:T(8,128)(2,1)S(1)}, bf16[128,512]{1,0:T(8,128)(2,1)S(1)}, u32[]{:S(2)}, u32[]{:S(2)}) collective-permute-start(bf16[128,512]{1,0:T(8,128)(2,1)S(1)} %get-tuple-element.103), channel_id=1, source_target_pairs={{0,12},{2,14},{4,8},{6,10},{8,4},{10,6},{12,0},{14,2},{16,28},{18,... | collective-permute-start | bytes 393224 | tf_op jit(solution)/shard_map/ppermute | solution.py:523
  49.2 5.9 %collective-permute-done.12._.rest_3_ = bf16[128,512]{1,0:T(8,128)(2,1)S(1)} collective-permute-done((bf16[128,512]{1,0:T(8,128)(2,1)S(1)}, bf16[128,512]{1,0:T(8,128)(2,1)S(1)}, u32[]{:S(2)}, u32[]{:S(2)}) %collective-permute-start.12) | collective-permute-done | bytes 131104 | tf_op jit(solution)/shard_map/ppermute | solution.py:523
  55.1 0.0 collective-permute-done.11.recv.rest_0_.rest_1_
  55.1 0.1 shard_map.163
  55.2 0.1 collective-permute-start.15
  55.3 3.6 %collective-permute-start.13 = (bf16[128,512]{1,0:T(8,128)(2,1)S(1)}, bf16[128,512]{1,0:T(8,128)(2,1)S(1)}, u32[]{:S(2)}, u32[]{:S(2)}) collective-permute-start(bf16[128,512]{1,0:T(8,128)(2,1)S(1)} %collective-permute-done.12._.rest_3_), channel_id=1, source_target_pairs={{0,2},{2,0},{4,6},{6,4},{8,10},{10,8},{12,14},{14,12},{16,18},{18,... | collective-permute-start | bytes 393224 | tf_op jit(solution)/shard_map/ppermute | solution.py:523
  58.9 3.3 %collective-permute-done.13.rest_4_ = bf16[128,512]{1,0:T(8,128)(2,1)S(1)} collective-permute-done((bf16[128,512]{1,0:T(8,128)(2,1)S(1)}, bf16[128,512]{1,0:T(8,128)(2,1)S(1)}, u32[]{:S(2)}, u32[]{:S(2)}) %collective-permute-start.13) | collective-permute-done | bytes 131104 | tf_op jit(solution)/shard_map/ppermute | solution.py:523
  62.2 0.0 collective-permute-done.14.rest_6_
  62.2 1.0 %collective-permute-done.15.rest_8_ = bf16[200,512]{1,0:T(8,128)(2,1)S(1)} collective-permute-done((bf16[200,512]{1,0:T(8,128)(2,1)S(1)}, bf16[200,512]{1,0:T(8,128)(2,1)S(1)}, u32[]{:S(2)}, u32[]{:S(2)}) %collective-permute-start.15) | collective-permute-done | bytes 204832 | tf_op jit(solution)/shard_map/ppermute | solution.py:533
  63.2 1.3 %shard_map.164 = (bf16[2,256,512]{2,1,0:T(8,128)(2,1)}, f32[64,512]{1,0:T(8,128)}, f32[64,512]{1,0:T(8,128)}, f32[64,512]{1,0:T(8,128)}, f32[1,512]{1,0:T(1,128)}, /*index=5*/f32[1,512]{1,0:T(1,128)}) custom-call(bf16[256,128]{1,0:T(8,128)(2,1)S(1)} %get-tuple-element.60.refs_0_.onehot_ref, ...), custom_call_target="tpu_custom_call" | custom-call | flops 67108864 | bytes 1572864 | tf_op jit(solution)/shard_map/pallas_call | solution.py:43
Async XLA Ops:
  0.6 14.1 %collective-permute-start.4 = (bf16[512,512]{1,0:T(8,128)(2,1)}, bf16[512,512]{1,0:T(8,128)(2,1)S(1)}, u32[]{:S(2)}, u32[]{:S(2)}) collective-permute-start(bf16[512,512]{1,0:T(8,128)(2,1)} %bitcast.12), channel_id=1, source_target_pairs={{0,1},{1,0},{2,3},{3,2},{4,5},{5,4},{6,7},{7,6},{8,9},{9,8},{10,11... | collective-permute-start | bytes 1572872 | tf_op jit(solution)/shard_map/ppermute | solution.py:530
  2.5 10.9 %collective-permute-start = (bf16[64,512]{1,0:T(8,128)(2,1)S(1)}, bf16[64,512]{1,0:T(8,128)(2,1)S(1)}, u32[]{:S(2)}, u32[]{:S(2)}) collective-permute-start(bf16[64,512]{1,0:T(8,128)(2,1)S(1)} %get-tuple-element.61), channel_id=1, source_target_pairs={{0,2},{1,3},{2,0},{3,1},{4,6},{5,7},{6,4},{7,5},{8,10},{9,11},{10,... | collective-permute-start | bytes 196616 | tf_op jit(solution)/shard_map/ppermute | solution.py:523
  5.1 8.3 %collective-permute-start.1 = (bf16[64,512]{1,0:T(8,128)(2,1)S(1)}, bf16[64,512]{1,0:T(8,128)(2,1)S(1)}, u32[]{:S(2)}, u32[]{:S(2)}) collective-permute-start(bf16[64,512]{1,0:T(8,128)(2,1)S(1)} %get-tuple-element.62), channel_id=1, source_target_pairs={{0,14},{1,15},{2,4},{3,5},{4,2},{5,3},{6,8},{7,9},{8,6},{9,7},{10,... | collective-permute-start | bytes 196616 | tf_op jit(solution)/shard_map/ppermute | solution.py:523
  8.6 4.8 %collective-permute-start.2 = (bf16[64,512]{1,0:T(8,128)(2,1)S(1)}, bf16[64,512]{1,0:T(8,128)(2,1)S(1)}, u32[]{:S(2)}, u32[]{:S(2)}) collective-permute-start(bf16[64,512]{1,0:T(8,128)(2,1)S(1)} %get-tuple-element.63), channel_id=1, source_target_pairs={{0,4},{1,5},{2,6},{3,7},{4,0},{5,1},{6,2},{7,3},{8,12},{9,13},{10,... | collective-permute-start | bytes 196616 | tf_op jit(solution)/shard_map/ppermute | solution.py:523
  8.6 6.1 %collective-permute-start.3 = (bf16[64,512]{1,0:T(8,128)(2,1)S(1)}, bf16[64,512]{1,0:T(8,128)(2,1)S(1)}, u32[]{:S(2)}, u32[]{:S(2)}) collective-permute-start(bf16[64,512]{1,0:T(8,128)(2,1)S(1)} %get-tuple-element.64), channel_id=1, source_target_pairs={{0,12},{1,13},{2,14},{3,15},{4,8},{5,9},{6,10},{7,11},{8,4},{9,5},... | collective-permute-start | bytes 196616 | tf_op jit(solution)/shard_map/ppermute | solution.py:523
  10.2 0.7 %copy-start = (s32[1,2,7]{2,1,0:T(2,128)S(1)}, s32[1,2,7]{2,1,0:T(2,128)}, u32[]{:S(2)}) copy-start(s32[1,2,7]{2,1,0:T(2,128)} %pairs_ref.1) | copy-start | bytes 172
  16.3 5.6 %collective-permute-start.9 = (bf16[512,1024]{1,0:T(8,128)(2,1)S(1)}, bf16[512,1024]{1,0:T(8,128)(2,1)S(1)}, u32[]{:S(2)}, u32[]{:S(2)}) collective-permute-start(bf16[512,1024]{1,0:T(8,128)(2,1)S(1)} %get-tuple-element.78), channel_id=1, source_target_pairs={{0,1},{1,0},{2,3},{3,2},{4,5},{5,4},{6,7},{7,6},{8,9},{9,8},{10,11... | collective-permute-start | bytes 3145736 | tf_op jit(solution)/shard_map/ppermute | solution.py:530
  16.8 5.9 %collective-permute-start.5 = (bf16[64,512]{1,0:T(8,128)(2,1)S(1)}, bf16[64,512]{1,0:T(8,128)(2,1)S(1)}, u32[]{:S(2)}, u32[]{:S(2)}) collective-permute-start(bf16[64,512]{1,0:T(8,128)(2,1)S(1)} %get-tuple-element.74), channel_id=1, source_target_pairs={{0,3},{1,2},{2,1},{3,0},{4,7},{5,6},{6,5},{7,4},{8,11},{9,10},{10,... | collective-permute-start | bytes 196616 | tf_op jit(solution)/shard_map/ppermute | solution.py:523
  18.4 6.5 %collective-permute-start.6 = (bf16[64,512]{1,0:T(8,128)(2,1)S(1)}, bf16[64,512]{1,0:T(8,128)(2,1)S(1)}, u32[]{:S(2)}, u32[]{:S(2)}) collective-permute-start(bf16[64,512]{1,0:T(8,128)(2,1)S(1)} %get-tuple-element.75), channel_id=1, source_target_pairs={{0,15},{1,14},{2,5},{3,4},{4,3},{5,2},{6,9},{7,8},{8,7},{9,6},{10,... | collective-permute-start | bytes 196616 | tf_op jit(solution)/shard_map/ppermute | solution.py:523
  21.0 4.1 %collective-permute-start.7 = (bf16[64,512]{1,0:T(8,128)(2,1)S(1)}, bf16[64,512]{1,0:T(8,128)(2,1)S(1)}, u32[]{:S(2)}, u32[]{:S(2)}) collective-permute-start(bf16[64,512]{1,0:T(8,128)(2,1)S(1)} %get-tuple-element.76), channel_id=1, source_target_pairs={{0,5},{1,4},{2,7},{3,6},{4,1},{5,0},{6,3},{7,2},{8,13},{9,12},{10,... | collective-permute-start | bytes 196616 | tf_op jit(solution)/shard_map/ppermute | solution.py:523
  21.0 6.0 %collective-permute-start.8 = (bf16[64,512]{1,0:T(8,128)(2,1)S(1)}, bf16[64,512]{1,0:T(8,128)(2,1)S(1)}, u32[]{:S(2)}, u32[]{:S(2)}) collective-permute-start(bf16[64,512]{1,0:T(8,128)(2,1)S(1)} %get-tuple-element.77), channel_id=1, source_target_pairs={{0,13},{1,12},{2,15},{3,14},{4,9},{5,8},{6,11},{7,10},{8,5},{9,4},... | collective-permute-start | bytes 196616 | tf_op jit(solution)/shard_map/ppermute | solution.py:523
  30.0 14.5 %collective-permute-start.10 = (bf16[928,512]{1,0:T(8,128)(2,1)S(1)}, bf16[928,512]{1,0:T(8,128)(2,1)S(1)}, u32[]{:S(2)}, u32[]{:S(2)}) collective-permute-start(bf16[928,512]{1,0:T(8,128)(2,1)S(1)} %get-tuple-element.96), channel_id=1, source_target_pairs={{0,4},{1,3},{2,6},{3,1},{4,0},{5,7},{6,2},{7,5},{8,12},{9,11},{10,... | collective-permute-start | bytes 2850824 | tf_op jit(solution)/shard_map/ppermute | solution.py:533
  44.8 10.4 %collective-permute-start.11 = (bf16[528,512]{1,0:T(8,128)(2,1)S(1)}, bf16[528,512]{1,0:T(8,128)(2,1)S(1)}, u32[]{:S(2)}, u32[]{:S(2)}) collective-permute-start(bf16[528,512]{1,0:T(8,128)(2,1)S(1)} %get-tuple-element.102), channel_id=1, source_target_pairs={{0,2},{1,5},{2,0},{3,7},{4,6},{5,1},{6,4},{7,3},{8,10},{9,13},{10,... | collective-permute-start | bytes 1622024 | tf_op jit(solution)/shard_map/ppermute | solution.py:533
  45.7 16.5 %collective-permute-start.14 = (bf16[512,512]{1,0:T(8,128)(2,1)S(1)}, bf16[512,512]{1,0:T(8,128)(2,1)S(1)}, u32[]{:S(2)}, u32[]{:S(2)}) collective-permute-start(bf16[512,512]{1,0:T(8,128)(2,1)S(1)} %get-tuple-element.104), channel_id=1, source_target_pairs={{0,1},{1,0},{2,3},{3,2},{4,5},{5,4},{6,7},{7,6},{8,9},{9,8},{10,11... | collective-permute-start | bytes 1572872 | tf_op jit(solution)/shard_map/ppermute | solution.py:530
  45.7 9.4 %collective-permute-start.12 = (bf16[128,512]{1,0:T(8,128)(2,1)S(1)}, bf16[128,512]{1,0:T(8,128)(2,1)S(1)}, u32[]{:S(2)}, u32[]{:S(2)}) collective-permute-start(bf16[128,512]{1,0:T(8,128)(2,1)S(1)} %get-tuple-element.103), channel_id=1, source_target_pairs={{0,12},{2,14},{4,8},{6,10},{8,4},{10,6},{12,0},{14,2},{16,28},{18,... | collective-permute-start | bytes 393224 | tf_op jit(solution)/shard_map/ppermute | solution.py:523
  55.2 8.0 %collective-permute-start.15 = (bf16[200,512]{1,0:T(8,128)(2,1)S(1)}, bf16[200,512]{1,0:T(8,128)(2,1)S(1)}, u32[]{:S(2)}, u32[]{:S(2)}) collective-permute-start(bf16[200,512]{1,0:T(8,128)(2,1)S(1)} %get-tuple-element.107), channel_id=1, source_target_pairs={{0,8},{1,9},{2,10},{3,11},{4,12},{5,13},{6,14},{7,15},{8,0},{9,1},... | collective-permute-start | bytes 614408 | tf_op jit(solution)/shard_map/ppermute | solution.py:533
  55.3 6.9 %collective-permute-start.13 = (bf16[128,512]{1,0:T(8,128)(2,1)S(1)}, bf16[128,512]{1,0:T(8,128)(2,1)S(1)}, u32[]{:S(2)}, u32[]{:S(2)}) collective-permute-start(bf16[128,512]{1,0:T(8,128)(2,1)S(1)} %collective-permute-done.12._.rest_3_), channel_id=1, source_target_pairs={{0,2},{2,0},{4,6},{6,4},{8,10},{10,8},{12,14},{14,12},{16,18},{18,... | collective-permute-start | bytes 393224 | tf_op jit(solution)/shard_map/ppermute | solution.py:523
